TPU v7x, 32 devices: a whole 2x2x4 slice. The times are simulated.
32 devices in a mesh: seq: 16 (over z, y, x), chan: 2 (over core).
Axes of the slice: x: 2, y: 2, z: 4, core: 2. Of those that a mesh axis runs over, the one named last changes fastest.
Arguments:
- streams: bfloat16 [3, 4096, 8192], P(None, 'seq', 'chan'), may hold values from -6 to 6
- grad_out: bfloat16 [4096, 8192], P('seq', 'chan'), may hold values from -9 to 9
- long_filter: float32 [8192, 8192], P('seq', 'chan'), may hold values from -0.0625 to 0.0625
- short_filter: float32 [3, 7, 8192], P(None, None, 'chan'), may hold values from -3 to 3
- skip_gain: float32 [8192], P('chan'), may hold values from -4 to 4
Outputs:
- output: bfloat16 [4096, 8192], P('seq', 'chan')
- grad_streams: bfloat16 [3, 4096, 8192], P(None, 'seq', 'chan')
- filter_grad: float32 [8192, 8192], P('seq', 'chan')
- short_grad: float32 [3, 7, 8192], P(None, None, 'chan')
- bias_grad: float32 [8192], P('chan')
All inputs are finite; a program needn't handle non-finite values.
Results may differ from a plain program's by a relative error of at most 0.0075.
Values may be sent and summed in bfloat16 or wider, within the bound.
No kernel may reach another device: no remote copies, remote signals or barrier semaphores. Data moves between devices by JAX's collectives and lax.ppermute only.
A program may use at most 320 MiB of HBM per device.

v0:
```python
import math

import jax
import jax.numpy as jnp
from jax import lax
from jax.sharding import PartitionSpec as P

D = 8192
LF = 8192
TAPS = 7


precise = lax.Precision.HIGHEST


def from_behind(block, axis, distance):
    devices = range(lax.axis_size(axis))
    route = [(i - distance, i) for i in devices if i - distance in devices]
    return lax.ppermute(block, axis, route)


def dft_tables(point_count):
    outer_len = point_count // 128
    outer_k = jnp.arange(outer_len, dtype=jnp.int32)[:, None]
    outer_n = jnp.arange(outer_len // 2, dtype=jnp.int32)[None, :]
    outer_angle = 2.0 * math.pi / outer_len * (outer_k * outer_n % outer_len).astype(jnp.float32)
    outer_both = jnp.concatenate([jnp.cos(outer_angle), -jnp.sin(outer_angle)], axis=0)
    inner_n = jnp.arange(128, dtype=jnp.int32)[None, :]
    twist_angle = (
        2.0 * math.pi / point_count * (outer_k * inner_n % point_count).astype(jnp.float32)
    )
    inner_k = jnp.arange(128, dtype=jnp.int32)[:, None]
    inner_angle = 2.0 * math.pi / 128 * (inner_k * inner_n % 128).astype(jnp.float32)
    inner_cos = jnp.cos(inner_angle)
    inner_sin = jnp.sin(inner_angle)
    inner_fwd = jnp.concatenate(
        [
            jnp.concatenate([inner_cos, -inner_sin], axis=1),
            jnp.concatenate([inner_sin, inner_cos], axis=1),
        ],
        axis=0,
    )
    inner_inv = jnp.concatenate(
        [
            jnp.concatenate([inner_cos, inner_sin], axis=1),
            jnp.concatenate([-inner_sin, inner_cos], axis=1),
        ],
        axis=0,
    )
    return (outer_both, jnp.cos(twist_angle), jnp.sin(twist_angle), inner_fwd, inner_inv)


def spectrum(signal, tables):
    outer_both, twist_cos, twist_sin, inner_fwd, inner_inv = tables
    outer_len = twist_cos.shape[0]
    first = jnp.einsum("kn,cnm->ckm", outer_both, signal, precision=precise)
    first_real = first[:, :outer_len]
    first_imag = first[:, outer_len:]
    middle = jnp.concatenate(
        [
            first_real * twist_cos + first_imag * twist_sin,
            first_imag * twist_cos - first_real * twist_sin,
        ],
        axis=2,
    )
    return jnp.einsum("ckm,mj->ckj", middle, inner_fwd, precision=precise)


def signal_of(spec, tables, point_count):
    outer_both, twist_cos, twist_sin, inner_fwd, inner_inv = tables
    first = jnp.einsum("ckm,mj->ckj", spec, inner_inv, precision=precise)
    first_real = first[:, :, :128]
    first_imag = first[:, :, 128:]
    middle = jnp.concatenate(
        [
            first_real * twist_cos - first_imag * twist_sin,
            first_real * twist_sin + first_imag * twist_cos,
        ],
        axis=1,
    )
    timed = jnp.einsum("kn,ckm->cnm", outer_both, middle, precision=precise)
    return (timed / point_count).reshape(spec.shape[0], point_count // 2)


def times_spec(left, right):
    left_real, left_imag = (left[:, :, :128], left[:, :, 128:])
    right_real, right_imag = (right[:, :, :128], right[:, :, 128:])
    return jnp.concatenate(
        [
            left_real * right_real - left_imag * right_imag,
            left_real * right_imag + left_imag * right_real,
        ],
        axis=2,
    )


def conj_times(left, right):
    left_real, left_imag = (left[:, :, :128], left[:, :, 128:])
    right_real, right_imag = (right[:, :, :128], right[:, :, 128:])
    return jnp.concatenate(
        [
            left_real * right_real + left_imag * right_imag,
            left_real * right_imag - left_imag * right_real,
        ],
        axis=2,
    )


def real_spectrum(signal2d, tables):
    channels = signal2d.shape[0]
    widened = signal2d.astype(jnp.float32).reshape(channels, signal2d.shape[1] // 128, 128)
    return spectrum(widened, tables)


def filter_spectrum(taps_t, length, tables):
    live_taps = min(taps_t.shape[1], length)
    padded = taps_t[:, :live_taps]
    return real_spectrum(padded, tables)


def value_path(gated_t, spec_filter, skip_slice, tables, point_count):
    gated_f = gated_t.astype(jnp.float32)
    spec_gated = real_spectrum(gated_t, tables)
    long_out = signal_of(times_spec(spec_gated, spec_filter), tables, point_count)
    mixed_t = (long_out + skip_slice[:, None] * gated_f).astype(jnp.bfloat16)
    return (mixed_t, spec_gated)


def grad_path(mix_t, spec_filter, spec_gated, skip_slice, tables, point_count, filter_len):
    mix_f = mix_t.astype(jnp.float32)
    spec_mix = real_spectrum(mix_t, tables)
    back = signal_of(conj_times(spec_filter, spec_mix), tables, point_count)
    grad_gated_t = (back + skip_slice[:, None] * mix_f).astype(jnp.bfloat16)
    corr = signal_of(conj_times(spec_gated, spec_mix), tables, point_count)
    live_taps = min(filter_len, point_count // 2)
    raw_filter_t = jnp.pad(corr, ((0, 0), (0, filter_len - live_taps)))
    return (grad_gated_t, raw_filter_t)


def body(streams, grad_out, long_filter, short_filter, skip_gain):
    shards = lax.axis_size("seq")
    tok_rows = streams.shape[1]
    feat_width = streams.shape[2]
    local_chans = feat_width // shards
    length = tok_rows * shards
    point_count = 2 * length
    filter_len = long_filter.shape[0] * shards
    tables = dft_tables(point_count)
    last_rows = streams[:, tok_rows - (TAPS - 1) :, :]
    before = from_behind(last_rows, "seq", 1)
    extended = jnp.concatenate([before, streams], axis=1).astype(jnp.float32)
    filtered = short_filter[:, 0, None, :] * extended[:, TAPS - 1 :, :]
    for offset in range(1, TAPS):
        filtered = (
            filtered
            + short_filter[:, offset, None, :]
            * extended[:, TAPS - 1 - offset : TAPS - 1 - offset + tok_rows, :]
        )
    gated = (filtered[0] * filtered[2]).astype(jnp.bfloat16)
    gout = grad_out.astype(jnp.float32)
    grad_mix = (gout * filtered[1]).astype(jnp.bfloat16)
    skip_slice = lax.dynamic_slice_in_dim(
        skip_gain, lax.axis_index("seq") * local_chans, local_chans
    )
    taps_t = lax.all_to_all(long_filter.T, "seq", split_axis=0, concat_axis=1, tiled=True)
    spec_filter = filter_spectrum(taps_t, length, tables)
    gated_t = lax.all_to_all(gated.T, "seq", split_axis=0, concat_axis=1, tiled=True)
    mixed_t, spec_gated = value_path(gated_t, spec_filter, skip_slice, tables, point_count)
    mixed_back = lax.all_to_all(mixed_t, "seq", split_axis=1, concat_axis=0, tiled=True)
    mix_t = lax.all_to_all(grad_mix.T, "seq", split_axis=0, concat_axis=1, tiled=True)
    grad_gated_t, raw_filter_t = grad_path(
        mix_t, spec_filter, spec_gated, skip_slice, tables, point_count, filter_len
    )
    grad_gated_back = lax.all_to_all(grad_gated_t, "seq", split_axis=1, concat_axis=0, tiled=True)
    raw_filter = lax.all_to_all(raw_filter_t, "seq", split_axis=1, concat_axis=0, tiled=True).T
    mixed_f = mixed_back.T.astype(jnp.float32)
    gg_f = grad_gated_back.T.astype(jnp.float32)
    output = (filtered[1] * mixed_f).astype(jnp.bfloat16)
    grad_pre = jnp.stack([gg_f * filtered[2], gout * mixed_f, gg_f * filtered[0]])
    first_rows = grad_pre[:, : TAPS - 1, :]
    next_first = from_behind(first_rows, "seq", -1)
    grad_ext = jnp.concatenate([grad_pre, next_first], axis=1)
    grad_in = short_filter[:, 0, None, :] * grad_pre
    short_terms = [jnp.sum(grad_pre * extended[:, TAPS - 1 :, :], axis=1)]
    for offset in range(1, TAPS):
        grad_in = (
            grad_in + short_filter[:, offset, None, :] * grad_ext[:, offset : offset + tok_rows, :]
        )
        short_terms.append(
            jnp.sum(
                grad_pre * extended[:, TAPS - 1 - offset : TAPS - 1 - offset + tok_rows, :], axis=1
            )
        )
    grad_streams = grad_in.astype(jnp.bfloat16)
    short_part = jnp.stack(short_terms, axis=1)
    bias_part = jnp.sum(grad_mix.astype(jnp.float32) * gated.astype(jnp.float32), axis=0)
    raw_short, raw_bias = lax.psum((short_part, bias_part), "seq")
    local_sq = (
        jnp.sum(raw_filter * raw_filter)
        + (jnp.sum(raw_short * raw_short) + jnp.sum(raw_bias * raw_bias)) / shards
    )
    sq_total = lax.psum(local_sq, ("seq", "chan"))
    param_count = LF * D + (3 * TAPS + 1) * D
    clip_factor = 1.0 / jnp.sqrt(sq_total / param_count + 1e-06)
    return (
        output,
        grad_streams,
        raw_filter * clip_factor,
        raw_short * clip_factor,
        raw_bias * clip_factor,
    )


def solution(mesh):
    placed = (
        P(None, "seq", "chan"),
        P("seq", "chan"),
        P("seq", "chan"),
        P(None, None, "chan"),
        P("chan"),
    )
    return jax.shard_map(
        body,
        mesh=mesh,
        in_specs=placed,
        out_specs=(
            P("seq", "chan"),
            P(None, "seq", "chan"),
            P("seq", "chan"),
            P(None, None, "chan"),
            P("chan"),
        ),
        check_vma=False,
    )
```

profile of v0, /device:TPU:0, one launch (start us, length us, event | category | flops | bytes accessed | tf_op | source)
XLA Modules:
  0.0 1487.5 jit_solution(6204775299134442421)
XLA Ops:
  26.7 35.5 %multiply_add_fusion = f32[3,256,4096]{2,1,0:T(8,128)} fusion(f32[3,262,4096]{2,1,0:T(8,128)} %maximum_convert_fusion, f32[3,4096]{1,0:T(4,128)S(1)} %get-tuple-element.77, f32[3,4096]{1,0:T(4,128)S(1)} %get-tuple-element.78, f32[3,4096]{1,0:T(4,128)S(1)} %get-tuple-element.79, f32[3,4096]{1,0:T(4,128)S(1)} %get-tuple-element.80, ...), kind=kLoop, calls=%fused_computation.46 | loop fusion | flops 40894464 | bytes 101007360 | tf_op jit(solution)/shard_map/add | solution.py:155
  85.7 38.4 %all-to-all-done.3 = bf16[16,256,256]{2,1,0:T(8,128)(2,1)S(1)} async-done(((bf16[16,256,256]{2,1,0:T(8,128)(2,1)}), bf16[16,256,256]{2,1,0:T(8,128)(2,1)S(1)}, u32[]{:S(2)}, u32[]{:S(2)}) %all-to-all-start.3) | async-done | bytes 2097184 | tf_op jit(solution)/shard_map/all_to_all | solution.py:170
  152.1 24.4 %all-to-all-done = bf16[16,256,256]{2,1,0:T(8,128)(2,1)} async-done(((bf16[16,256,256]{2,1,0:T(8,128)(2,1)}), bf16[16,256,256]{2,1,0:T(8,128)(2,1)}, u32[]{:S(2)}, u32[]{:S(2)}) %all-to-all-start) | async-done | bytes 2097184 | tf_op jit(solution)/shard_map/all_to_all | solution.py:167
  221.5 120.0 %all-to-all-done.1 = f32[16,256,512]{1,2,0:T(8,128)} async-done(((f32[16,256,512]{1,2,0:T(8,128)}), f32[16,256,512]{1,2,0:T(8,128)}, u32[]{:S(2)}, u32[]{:S(2)}) %all-to-all-start.1) | async-done | bytes 8388640 | tf_op jit(solution)/shard_map/all_to_all | solution.py:165
  351.4 17.9 %convolution_bitcast_fusion.1 = f32[256,128,128]{2,1,0:T(8,128)} fusion(f32[128,32,1]{0,1,2:T(8,128)S(1)} %maximum_bitcast_fusion, f32[256,32,128]{2,1,0:T(8,128)} %copy.133), kind=kOutput, calls=%fused_computation.48 | convolution fusion | flops 1610612736 | bytes 20987904 | tf_op jit(solution)/shard_map/kn,cnm->ckm/dot_general | solution.py:56
  369.3 33.5 %multiply_add_fusion.5 = (f32[256,64,128]{2,1,0:T(8,128)}, f32[256,64,128]{2,1,0:T(8,128)}, f32[256,64,128]{2,1,0:T(8,128)}, f32[256,64,128]{2,1,0:T(8,128)}, f3...) fusion(f32[256,128,128]{2,1,0:T(8,128)} %convolution_bitcast_fusion, f32[64,128]{1,0:T(8,128)S(1)} %get-tuple-element.83, ...), kind=kLoop, calls=%fused_computation.60 | loop fusion | flops 37748736 | bytes 100728832 | tf_op jit(solution)/shard_map/add | solution.py:61
  402.8 13.4 pad_maximum_fusion.3
  425.3 32.9 %fusion.12 = f32[256,64,256]{0,2,1:T(8,128)} fusion(f32[256,64,256]{2,1,0:T(8,128)} %pad_maximum_fusion.3, f32[128,128]{0,1:T(8,128)S(1)} %get-tuple-element.86, f32[128,128]{0,1:T(8,128)S(1)} %get-tuple-element.85, f32[128,128]{0,1:T(8,128)S(1)} %fusion.65), kind=kOutput, calls=%fused_computation.18 | convolution fusion | flops 12885098496 | bytes 33751040 | tf_op jit(solution)/shard_map/ckm,mj->ckj/dot_general | solution.py:66
  458.2 33.1 %fusion.16 = f32[256,64,256]{0,2,1:T(8,128)} fusion(f32[256,64,256]{2,1,0:T(8,128)} %pad_maximum_fusion, f32[128,128]{0,1:T(8,128)S(1)} %get-tuple-element.86, f32[128,128]{0,1:T(8,128)S(1)} %get-tuple-element.85, f32[128,128]{0,1:T(8,128)S(1)} %fusion.65), kind=kOutput, calls=%fused_computation.22 | convolution fusion | flops 12885098496 | bytes 33751040 | tf_op jit(solution)/shard_map/ckm,mj->ckj/dot_general | solution.py:66
  500.9 32.9 %fusion.14 = f32[256,64,256]{0,2,1:T(8,128)} fusion(f32[256,64,256]{2,1,0:T(8,128)} %pad_maximum_fusion.1, f32[128,128]{0,1:T(8,128)S(1)} %get-tuple-element.86, f32[128,128]{0,1:T(8,128)S(1)} %get-tuple-element.85, f32[128,128]{0,1:T(8,128)S(1)} %fusion.65), kind=kOutput, calls=%fused_computation.20 | convolution fusion | flops 12885098496 | bytes 33751040 | tf_op jit(solution)/shard_map/ckm,mj->ckj/dot_general | solution.py:66
  533.8 19.3 %multiply_add_fusion.4 = (f32[256,64,128]{0,2,1:T(8,128)}, f32[256,64,128]{0,2,1:T(8,128)}) fusion(f32[256,64,256]{0,2,1:T(8,128)} %fusion.12, f32[256,64,256]{0,2,1:T(8,128)} %fusion.14), kind=kLoop, calls=%fused_computation.58 | loop fusion | flops 12582912 | bytes 50331648 | tf_op jit(solution)/shard_map/add | solution.py:102
  553.1 26.5 %multiply_add_fusion.2 = (f32[256,64,128]{0,2,1:T(8,128)S(1)}, f32[256,64,128]{0,2,1:T(8,128)}, f32[256,64,128]{0,2,1:T(8,128)}, f32[256,64,128]{0,2,1:T(8,128)}) fusion(f32[256,64,256]{0,2,1:T(8,128)} %fusion.12, f32[256,64,256]{0,2,1:T(8,128)} %fusion.16, f32[256,64,256]{0,2,1:T(8,128)} %fusion.14), kind=kLoop, calls=%fused_computation.54 | loop fusion | flops 25165824 | bytes 83886080 | tf_op jit(solution)/shard_map/add | solution.py:102
  589.4 17.7 %copy.115 = f32[256,64,256]{2,1,0:T(8,128)} copy(f32[256,64,256]{0,2,1:T(8,128)} %pad_maximum_fusion.5) | data formatting | bytes 33554432 | tf_op jit(solution)/shard_map/concatenate | solution.py:100
  607.1 18.4 %fusion.42 = f32[256,64,256]{2,1,0:T(8,128)} fusion(f32[256,64,256]{2,1,0:T(8,128)} %copy.115, f32[128,128]{0,1:T(8,128)S(1)} %get-tuple-element.86, f32[128,128]{0,1:T(8,128)S(1)} %fusion.65, f32[128,128]{0,1:T(8,128)S(1)} %get-tuple-element.85), kind=kOutput, calls=%fused_computation.103 | convolution fusion | flops 12885098496 | bytes 33751040 | tf_op jit(solution)/shard_map/ckm,mj->ckj/dot_general | solution.py:71
  625.6 11.5 pad_maximum_fusion.2
  637.1 17.7 %copy.109 = f32[256,64,256]{2,1,0:T(8,128)} copy(f32[256,64,256]{0,2,1:T(8,128)} %pad_maximum_fusion.2) | data formatting | bytes 33554432 | tf_op jit(solution)/shard_map/concatenate | solution.py:88
  654.8 18.8 %fusion.46 = f32[256,64,256]{2,1,0:T(8,128)} fusion(f32[256,64,256]{2,1,0:T(8,128)} %copy.109, f32[128,128]{0,1:T(8,128)S(1)} %get-tuple-element.86, f32[128,128]{0,1:T(8,128)S(1)} %fusion.65, f32[128,128]{0,1:T(8,128)S(1)} %get-tuple-element.85), kind=kOutput, calls=%fused_computation.105 | convolution fusion | flops 12885098496 | bytes 33751040 | tf_op jit(solution)/shard_map/ckm,mj->ckj/dot_general | solution.py:71
  673.6 11.5 pad_maximum_fusion.4
  685.1 17.7 %copy.112 = f32[256,64,256]{2,1,0:T(8,128)} copy(f32[256,64,256]{0,2,1:T(8,128)} %pad_maximum_fusion.4) | data formatting | bytes 33554432 | tf_op jit(solution)/shard_map/concatenate | solution.py:100
  702.8 18.5 %fusion.44 = f32[256,64,256]{2,1,0:T(8,128)} fusion(f32[256,64,256]{2,1,0:T(8,128)} %copy.112, f32[128,128]{0,1:T(8,128)S(1)} %get-tuple-element.86, f32[128,128]{0,1:T(8,128)S(1)} %fusion.65, f32[128,128]{0,1:T(8,128)S(1)} %get-tuple-element.85), kind=kOutput, calls=%fused_computation.104 | convolution fusion | flops 12885098496 | bytes 33751040 | tf_op jit(solution)/shard_map/ckm,mj->ckj/dot_general | solution.py:71
  721.3 33.4 %multiply_subtract_fusion = (f32[256,64,128]{2,1,0:T(8,128)}, f32[256,64,128]{2,1,0:T(8,128)}, f32[256,64,128]{2,1,0:T(8,128)}, f32[256,64,128]{2,1,0:T(8,128)},...) fusion(f32[256,64,256]{2,1,0:T(8,128)} %fusion.42, f32[64,128]{1,0:T(8,128)S(1)} %copy-done.26, ...), kind=kLoop, calls=%fused_computation.52 | loop fusion | flops 37748736 | bytes 100728832 | tf_op jit(solution)/shard_map/sub | solution.py:76
  754.7 13.6 multiply_bitcast_fusion.1
  773.5 13.4 multiply_bitcast_fusion.2
  802.8 86.6 %all_to_all.84 = bf16[256,16,256]{2,0,1:T(8,128)(2,1)} all-to-all(bf16[256,16,256]{2,0,1:T(8,128)(2,1)S(1)} %get-tuple-element.73), channel_id=1, replica_groups=mesh['seq'=16,'chan'=2] {'seq'}, dimensions={1} | all-to-all | bytes 4194304 | tf_op jit(solution)/shard_map/all_to_all | solution.py:174
  893.3 13.4 multiply_bitcast_fusion
  918.1 17.0 %all-to-all-done.2 = bf16[256,16,256]{2,0,1:T(8,128)(2,1)S(1)} async-done(((bf16[256,16,256]{2,0,1:T(8,128)(2,1)}), bf16[256,16,256]{2,0,1:T(8,128)(2,1)S(1)}, u32[]{:S(2)}, u32[]{:S(2)}) %all-to-all-start.2) | async-done | bytes 2097184 | tf_op jit(solution)/shard_map/all_to_all | solution.py:169
  945.1 240.4 %psum.22 = f32[4096]{0:T(1024)S(1)} all-reduce(f32[4096]{0:T(1024)S(1)} %copy-done.29), channel_id=1, replica_groups=mesh['seq'=16,'chan'=2] {'seq'}, use_global_device_ids=true, to_apply=%region_11.12 | all-reduce | flops 4096 | bytes 32768 | tf_op jit(solution)/shard_map/psum | solution.py:197
  1204.0 13.3 fusion.27
  1217.2 39.8 %multiply_reduce_fusion = (f32[3,4096]{1,0:T(4,128)S(1)}, f32[3,4096]{1,0:T(4,128)S(1)}, f32[3,4096]{1,0:T(4,128)S(1)}, f32[3,4096]{1,0:T(4,128)S(1)}, f32[3,409...) fusion(f32[3,262,4096]{2,1,0:T(8,128)} %maximum_convert_fusion, ...), kind=kLoop, calls=%fused_computation.39 | loop fusion | flops 50245632 | bytes 113590272 | tf_op jit(solution)/shard_map/reduce_sum | solution.py:190
  1279.3 90.4 %all-reduce.3.cloned.1.call-done = f32[3,7,4096]{2,0,1:T(4,128)} async-done(((f32[3,7,4096]{2,0,1:T(4,128)}), f32[3,7,4096]{2,0,1:T(4,128)}) %all-reduce.3.cloned.1.call-update) | async-done | bytes 344080 | tf_op jit(solution)/shard_map/psum | solution.py:197
  1379.6 32.9 %fusion.19 = bf16[3,256,4096]{2,1,0:T(8,128)(2,1)} fusion(f32[3,262,4096]{2,1,0:T(8,128)} %pad_maximum_fusion.6, f32[3,4096]{1,0:T(4,128)S(1)} %copy-done.12, f32[3,4096]{1,0:T(4,128)S(1)} %copy-done.14, f32[3,4096]{1,0:T(4,128)S(1)} %copy-done.16, f32[3,4096]{1,0:T(4,128)S(1)} %copy-done.18, f32[3,4096]{1,0:T(4,128)S(1)} %copy-done.20, ...), kind=kLoop, calls=%fused_computation.27 | loop fusion | flops 50331648 | bytes 94715904 | tf_op jit(solution)/shard_map/convert_element_type | solution.py:194
  1412.5 39.3 %psum.23 = f32[]{:T(128)} all-reduce(f32[]{:T(128)S(6)} %add.206), channel_id=1, replica_groups=mesh['seq'=16,'chan'=2] {'seq','chan'}, use_global_device_ids=true, to_apply=%region_13.14 | all-reduce | flops 1 | bytes 8 | tf_op jit(solution)/shard_map/psum | solution.py:202
  (135 shorter events, 276.8 us)
Async XLA Ops:
  8.1 9.0 collective-permute-start
  16.2 10.5 copy-start.11
  16.2 10.4 copy-start.13
  16.3 10.4 copy-start.15
  16.3 10.4 copy-start.17
  26.7 35.6 %copy-start.4 = (bf16[256,4096]{1,0:T(8,128)(2,1)S(1)}, bf16[256,4096]{1,0:T(8,128)(2,1)}, u32[]{:S(2)}) copy-start(bf16[256,4096]{1,0:T(8,128)(2,1)} %param.6) | copy-start | bytes 6291460
  73.7 50.3 %all-to-all-start.3 = ((bf16[16,256,256]{2,1,0:T(8,128)(2,1)}), bf16[16,256,256]{2,1,0:T(8,128)(2,1)S(1)}, u32[]{:S(2)}, u32[]{:S(2)}) async-start(bf16[16,256,256]{2,1,0:T(8,128)(2,1)} %bitcast.149), calls=%async_computation.3 | async-start | bytes 4194304 | tf_op jit(solution)/shard_map/all_to_all | solution.py:170
  124.0 64.8 %copy-start.2 = (bf16[16,256,256]{2,1,0:T(8,128)(2,1)}, bf16[16,256,256]{2,1,0:T(8,128)(2,1)S(1)}, u32[]{:S(2)}) copy-start(bf16[16,256,256]{2,1,0:T(8,128)(2,1)S(1)} %all-to-all-done.3) | copy-start | bytes 6291460
  124.0 52.5 %all-to-all-start = ((bf16[16,256,256]{2,1,0:T(8,128)(2,1)}), bf16[16,256,256]{2,1,0:T(8,128)(2,1)}, u32[]{:S(2)}, u32[]{:S(2)}) async-start(bf16[16,256,256]{2,1,0:T(8,128)(2,1)} %bitcast.148), calls=%async_computation | async-start | bytes 4194304 | tf_op jit(solution)/shard_map/all_to_all | solution.py:167
  176.5 165.0 %all-to-all-start.1 = ((f32[16,256,512]{1,2,0:T(8,128)}), f32[16,256,512]{1,2,0:T(8,128)}, u32[]{:S(2)}, u32[]{:S(2)}) async-start(f32[16,256,512]{1,2,0:T(8,128)} %copy.83), calls=%async_computation.1 | async-start | bytes 16777216 | tf_op jit(solution)/shard_map/all_to_all | solution.py:165
  188.1 163.3 %copy-start.8 = (f32[128,32,1]{0,1,2:T(8,128)}, f32[128,32,1]{0,1,2:T(8,128)S(1)}, u32[]{:S(2)}) copy-start(f32[128,32,1]{0,1,2:T(8,128)S(1)} %maximum_bitcast_fusion) | copy-start | bytes 49156
  188.3 181.0 %copy-start.25 = (f32[64,128]{1,0:T(8,128)}, f32[64,128]{1,0:T(8,128)S(1)}, u32[]{:S(2)}) copy-start(f32[64,128]{1,0:T(8,128)S(1)} %get-tuple-element.83) | copy-start | bytes 98308
  188.3 181.0 %copy-start.27 = (f32[64,128]{1,0:T(8,128)}, f32[64,128]{1,0:T(8,128)S(1)}, u32[]{:S(2)}) copy-start(f32[64,128]{1,0:T(8,128)S(1)} %get-tuple-element.84) | copy-start | bytes 98308
  200.3 11.5 copy-start.6
  402.8 13.4 copy-start
  402.8 16.4 %copy-start.1 = (f32[256,64,128]{2,1,0:T(8,128)S(1)}, f32[256,64,128]{2,1,0:T(8,128)}, u32[]{:S(2)}) copy-start(f32[256,64,128]{2,1,0:T(8,128)} %get-tuple-element.72) | copy-start | bytes 25165828
  425.3 66.0 %slice-start = ((s8[8388608]{0:T(1024)(128)(4,1)}), s8[4194304]{0:T(1024)(128)(4,1)S(1)}, s32[]{:S(2)}) async-start(s8[8388608]{0:T(1024)(128)(4,1)} %bitcast.141), calls=%async_computation.7 | async-start | bytes 8388608
  458.2 33.2 %slice-start.1 = ((s8[8388608]{0:T(1024)(128)(4,1)}), s8[4194304]{0:T(1024)(128)(4,1)S(1)}, s32[]{:S(2)}) async-start(s8[8388608]{0:T(1024)(128)(4,1)} %bitcast.141), calls=%async_computation.8 | async-start | bytes 8388608
  702.8 18.5 %copy-start.26 = (f32[64,128]{1,0:T(8,128)S(1)}, f32[64,128]{1,0:T(8,128)}, u32[]{:S(2)}) copy-start(f32[64,128]{1,0:T(8,128)} %copy-done.25) | copy-start | bytes 98308
  702.8 18.5 %copy-start.28 = (f32[64,128]{1,0:T(8,128)S(1)}, f32[64,128]{1,0:T(8,128)}, u32[]{:S(2)}) copy-start(f32[64,128]{1,0:T(8,128)} %copy-done.27) | copy-start | bytes 98308
  721.3 33.4 %copy-start.9 = (f32[128,32,1]{0,1,2:T(8,128)S(1)}, f32[128,32,1]{0,1,2:T(8,128)}, u32[]{:S(2)}) copy-start(f32[128,32,1]{0,1,2:T(8,128)} %copy-done.8) | copy-start | bytes 49156
  889.4 45.6 %all-to-all-start.2 = ((bf16[256,16,256]{2,0,1:T(8,128)(2,1)}), bf16[256,16,256]{2,0,1:T(8,128)(2,1)S(1)}, u32[]{:S(2)}, u32[]{:S(2)}) async-start(bf16[256,16,256]{2,0,1:T(8,128)(2,1)} %get-tuple-element.74), calls=%async_computation.2 | async-start | bytes 4194304 | tf_op jit(solution)/shard_map/all_to_all | solution.py:169
  935.0 437.7 %all-to-all-start.5 = ((f32[256,16,512]{0,2,1:T(8,128)}), f32[256,16,512]{0,2,1:T(8,128)}, u32[]{:S(2)}, u32[]{:S(2)}) async-start(f32[256,16,512]{0,2,1:T(8,128)} %bitcast.139), calls=%async_computation.5 | async-start | bytes 16777216 | tf_op jit(solution)/shard_map/all_to_all | solution.py:175
  945.0 424.6 %all-reduce.3.cloned.1.call-start = ((), (), s32[]{:S(2)}) async-start(), calls=%async_computation.6 | async-start | bytes 917504 | tf_op jit(solution)/shard_map/psum | solution.py:197
  1258.1 9.9 collective-permute-start.1
  1279.2 100.3 %copy-start.12 = (f32[3,4096]{1,0:T(4,128)S(1)}, f32[3,4096]{1,0:T(4,128)}, u32[]{:S(2)}) copy-start(f32[3,4096]{1,0:T(4,128)} %copy-done.11) | copy-start | bytes 147460
  1279.2 100.3 %copy-start.14 = (f32[3,4096]{1,0:T(4,128)S(1)}, f32[3,4096]{1,0:T(4,128)}, u32[]{:S(2)}) copy-start(f32[3,4096]{1,0:T(4,128)} %copy-done.13) | copy-start | bytes 147460
  1279.2 100.3 %copy-start.16 = (f32[3,4096]{1,0:T(4,128)S(1)}, f32[3,4096]{1,0:T(4,128)}, u32[]{:S(2)}) copy-start(f32[3,4096]{1,0:T(4,128)} %copy-done.15) | copy-start | bytes 147460
  1279.2 100.3 %copy-start.18 = (f32[3,4096]{1,0:T(4,128)S(1)}, f32[3,4096]{1,0:T(4,128)}, u32[]{:S(2)}) copy-start(f32[3,4096]{1,0:T(4,128)} %copy-done.17) | copy-start | bytes 147460
  1279.3 100.3 %copy-start.20 = (f32[3,4096]{1,0:T(4,128)S(1)}, f32[3,4096]{1,0:T(4,128)}, u32[]{:S(2)}) copy-start(f32[3,4096]{1,0:T(4,128)} %copy-done.19) | copy-start | bytes 147460
  1279.3 100.3 %copy-start.22 = (f32[3,4096]{1,0:T(4,128)S(1)}, f32[3,4096]{1,0:T(4,128)}, u32[]{:S(2)}) copy-start(f32[3,4096]{1,0:T(4,128)} %copy-done.21) | copy-start | bytes 147460
  1279.3 100.3 %copy-start.24 = (f32[3,1,4096]{2,0,1:T(4,128)S(1)}, f32[3,1,4096]{2,0,1:T(4,128)}, u32[]{:S(2)}) copy-start(f32[3,1,4096]{2,0,1:T(4,128)} %copy-done.23) | copy-start | bytes 147460
  (9 other events, 67.4 us)
Sparse Core Ops, SparseCore 0:
  1260.5 109.1 all-reduce.2
where the time goes:
time: 1500 us; the launch traced here: 1490 us
  blocking collectives  366 us (24%)
  other arithmetic  359 us (24%)
  waiting for transfers between devices  298 us (20%)
  matrix products  234 us (16%)
  local copies, waits for them, and re-layouts  164 us (11%)
  starting transfers between devices  47.9 us (3%)
  between operations  17.6 us (1%)
    psum x1, blocking collectives, body(): raw_short, raw_bias = lax.psum((short_part, bias_part), 'seq')  240 us
    all_to_all x1, waiting for transfers between devices, body(): lax.all_to_all(long_filter.T, 'seq', split_axis=0, concat_axis=1, tiled=T...  120 us
    dot_general x3, matrix products, spectrum(): return jnp.einsum('ckm,mj->ckj', middle, inner_fwd, precision=precise)  98.9 us
    psum x1, waiting for transfers between devices, body(): raw_short, raw_bias = lax.psum((short_part, bias_part), 'seq')  90.4 us
    all_to_all x1, blocking collectives, body(): lax.all_to_all(grad_gated_t, 'seq', split_axis=1, concat_axis=0, tiled=True)  86.6 us
    dot_general x3, matrix products, signal_of(): first = jnp.einsum('ckm,mj->ckj', spec, inner_inv, precision=precise)  55.7 us
    add x2, other arithmetic, conj_times(): left_real * right_real + left_imag * right_imag  45.9 us
    dot_general x3, matrix products, signal_of(): timed = jnp.einsum('kn,ckm->cnm', outer_both, middle, precision=precise)  40.4 us
  transfers between devices with their start and end apart: 8, of which 7 were waited for; matrix products, arithmetic and copies ran while one was open for 11% of the time, Pallas kernels for 0%

commit v1 on v0

v1 whole, which is shorter than its diff:
```python
import math

import jax
import jax.numpy as jnp
from jax import lax
from jax.experimental import pallas as pl
from jax.experimental.pallas import tpu as pltpu
from jax.sharding import PartitionSpec as P

D = 8192
LF = 8192
TAPS = 7
HALO = 8
LANES = 128
F32 = jnp.float32
BF16 = jnp.bfloat16


def add(a, b):
    if a is None:
        return b
    if b is None:
        return a
    return a + b


def neg(a):
    return None if a is None else -a


def sub(a, b):
    if b is None:
        return a
    if a is None:
        return -b
    return a - b


def scaled(a, c):
    if a is None or abs(c) < 1e-12:
        return None
    if abs(c - 1.0) < 1e-12:
        return a
    if abs(c + 1.0) < 1e-12:
        return -a
    return a * c


def cadd(a, b):
    return (add(a[0], b[0]), add(a[1], b[1]))


def csub(a, b):
    return (sub(a[0], b[0]), sub(a[1], b[1]))


def times_i(a, sign):
    return (neg(a[1]), a[0]) if sign > 0 else (a[1], neg(a[0]))


def cmul(a, angle, gain=1.0):
    c = math.cos(angle)
    s = math.sin(angle)
    re, im = a
    if abs(abs(c) - abs(s)) < 1e-12 and re is not None and im is not None:
        root = abs(c) * gain
        sc = 1.0 if c > 0 else -1.0
        ss = 1.0 if s > 0 else -1.0
        if sc * ss > 0:
            return ((re - im) * (root * sc), (re + im) * (root * sc))
        return ((re + im) * (root * sc), (im - re) * (root * sc))
    c = c * gain
    s = s * gain
    return (sub(scaled(re, c), scaled(im, s)), add(scaled(im, c), scaled(re, s)))


def complex_dft(xs, sign):
    n = len(xs)
    if n == 1:
        return list(xs)
    half = n // 2
    sums = [cadd(xs[i], xs[i + half]) for i in range(half)]
    difs = [csub(xs[i], xs[i + half]) for i in range(half)]
    if n == 2:
        return [sums[0], difs[0]]
    quarter = n // 4
    out = [None] * n
    out[0::2] = complex_dft(sums, sign)
    turn = sign * 2.0 * math.pi / n
    first = []
    third = []
    for i in range(quarter):
        rot = times_i(difs[i + quarter], sign)
        first.append(cmul(cadd(difs[i], rot), turn * i))
        third.append(cmul(csub(difs[i], rot), turn * 3 * i))
    out[1::4] = complex_dft(first, sign)
    out[3::4] = complex_dft(third, sign)
    return out


def real_dft(xs):
    n = len(xs)
    if n == 1:
        return [(xs[0], None)]
    half = n // 2
    sums = [add(xs[i], xs[i + half]) for i in range(half)]
    difs = [sub(xs[i], xs[i + half]) for i in range(half)]
    if n == 2:
        return [(sums[0], None), (difs[0], None)]
    quarter = n // 4
    out = [None] * (half + 1)
    out[0::2] = real_dft(sums)
    turn = -2.0 * math.pi / n
    odd = [cmul((difs[i], neg(difs[i + quarter])), turn * i) for i in range(quarter)]
    for j, value in enumerate(complex_dft(odd, -1)):
        k = 4 * j + 1
        if k <= half:
            out[k] = value
        else:
            out[n - k] = (value[0], neg(value[1]))
    return out


def real_idft(spec, keep):
    n = 2 * (len(spec) - 1)
    if n == 2:
        both = [add(spec[0][0], spec[1][0]), sub(spec[0][0], spec[1][0])]
        return both[:keep]
    half = n // 2
    quarter = n // 4
    even = real_idft(spec[0::2], half)
    odd = []
    for j in range(quarter):
        k = 4 * j + 1
        odd.append(spec[k] if k <= half else (spec[n - k][0], neg(spec[n - k][1])))
    turn = 2.0 * math.pi / n
    rest = [cmul(v, turn * i, 2.0) for i, v in enumerate(complex_dft(odd, 1))]
    wave = [rest[i][0] for i in range(quarter)] + [neg(rest[i][1]) for i in range(quarter)]
    out = [add(even[i], wave[i]) for i in range(half)]
    if keep > half:
        out = out + [sub(even[i], wave[i]) for i in range(half)]
    return out[:keep]


def turn_tables(shards, rows):
    radix = 2 * shards
    count = radix * rows
    k1 = jnp.arange(shards + 1, dtype=jnp.int32)[:, None]
    r = jnp.arange(rows, dtype=jnp.int32)
    fine = 2.0 * math.pi / count * (k1 * r[None, :] % count).astype(F32)
    coarse = 2.0 * math.pi / rows * (r[:, None] * r[None, :] % rows).astype(F32)
    fine_c = jnp.cos(fine)
    fine_s = jnp.sin(fine)
    coarse_c = jnp.cos(coarse)[None]
    coarse_s = jnp.sin(coarse)[None]

    def pair(fc, fs, gain):
        cos = fc * coarse_c - fs * coarse_s
        sin = fs * coarse_c + fc * coarse_s
        return (jnp.concatenate([cos, sin], axis=1) * gain).astype(BF16)

    fwd = pair(fine_c[:, None, :], fine_s[:, None, :], 1.0)
    inv = pair(fine_c[:, :, None], fine_s[:, :, None], 1.0 / count)
    return fwd, inv


def lane_step(chans):
    return 128 if chans % 128 == 0 else chans


def over_tiles(rows, chans, work):
    lanes = lane_step(chans)
    sub_rows = 16
    across = chans // lanes

    def step(i, carry):
        r = pl.multiple_of((i // across) * sub_rows, sub_rows)
        if across == 1:
            c = 0
        else:
            c = pl.multiple_of((i % across) * lanes, lanes)
        work(pl.ds(r, sub_rows), pl.ds(c, lanes))
        return carry

    lax.fori_loop(0, (rows // sub_rows) * across, step, 0)


def split_in(src, dst, at, shards, rows, chans):
    blocks = src.shape[0]

    def work(rs, cs):
        xs = [src[s, rs, cs].astype(F32) for s in range(blocks)]
        xs = xs + [None] * (2 * shards - blocks)
        for k, (re, im) in enumerate(real_dft(xs)):
            dst[k, at, rs, cs] = re.astype(BF16)
            if im is None:
                dst[k, at + 1, rs, cs] = jnp.zeros(re.shape, BF16)
            else:
                dst[k, at + 1, rs, cs] = im.astype(BF16)

    over_tiles(rows, chans, work)


def load_spec(src, at, shards, rs, cs):
    spec = []
    for k in range(shards + 1):
        edge = k == 0 or k == shards
        spec.append((src[k, at, rs, cs], None if edge else src[k, at + 1, rs, cs]))
    return spec


def dot(a, b):
    return jnp.dot(a, b, preferred_element_type=F32)


def forward(table, a_re, a_im, rows):
    p = dot(table, a_re)
    q = dot(table, a_im)
    return p[:rows] + q[rows:], q[:rows] - p[rows:]


def backward(table, z_re, z_im, rows):
    p = dot(table, z_re.astype(BF16))
    q = dot(table, z_im.astype(BF16))
    return p[:rows] - q[rows:], p[rows:] + q[:rows]


def whole(shape):
    zeros = (0,) * len(shape)
    return pl.BlockSpec(shape, lambda *_: zeros, pipeline_mode=pl.Buffered(1))


def per_step(shape):
    zeros = (0,) * (len(shape) - 1)
    return pl.BlockSpec(shape, lambda i: (i,) + zeros)


def value_path(gated, taps, skip, fwd, inv):
    shards, rows, chans = gated.shape
    live = min(taps.shape[0], shards)
    steps = shards + 1

    def kernel(g_ref, h_ref, skip_ref, fwd_ref, inv_ref, mixed_ref, gs_ref, hs_ref, a_ref, y_ref):
        k = pl.program_id(0)

        @pl.when(k == 0)
        def _():
            split_in(g_ref, a_ref, 0, shards, rows, chans)
            split_in(h_ref, a_ref, 2, shards, rows, chans)

        g_re, g_im = forward(fwd_ref[0], a_ref[k, 0], a_ref[k, 1], rows)
        h_re, h_im = forward(fwd_ref[0], a_ref[k, 2], a_ref[k, 3], rows)
        gs_ref[0, 0] = g_re
        gs_ref[0, 1] = g_im
        hs_ref[0, 0] = h_re
        hs_ref[0, 1] = h_im
        y_re, y_im = backward(inv_ref[0], g_re * h_re - g_im * h_im, g_re * h_im + g_im * h_re, rows)
        y_ref[k, 0] = y_re
        y_ref[k, 1] = y_im

        @pl.when(k == steps - 1)
        def _():
            def work(rs, cs):
                out = real_idft(load_spec(y_ref, 0, shards, rs, cs), shards)
                gain = skip_ref[:, cs]
                for s in range(shards):
                    mixed = out[s] + gain * g_ref[s, rs, cs].astype(F32)
                    mixed_ref[s, rs, cs] = mixed.astype(BF16)

            over_tiles(rows, chans, work)

    spec_shape = jax.ShapeDtypeStruct((steps, 2, rows, chans), F32)
    return pl.pallas_call(
        kernel,
        grid=(steps,),
        in_specs=[
            whole((shards, rows, chans)),
            whole((live, rows, chans)),
            whole((1, chans)),
            per_step((1, 2 * rows, rows)),
            per_step((1, 2 * rows, rows)),
        ],
        out_specs=[
            whole((shards, rows, chans)),
            per_step((1, 2, rows, chans)),
            per_step((1, 2, rows, chans)),
        ],
        out_shape=[jax.ShapeDtypeStruct((shards, rows, chans), BF16), spec_shape, spec_shape],
        scratch_shapes=[
            pltpu.VMEM((steps, 4, rows, chans), BF16),
            pltpu.VMEM((steps, 2, rows, chans), F32),
        ],
        cost_estimate=pl.CostEstimate(flops=30 * 10**9, transcendentals=0, bytes_accessed=40 * 10**6),
        name="value_path",
    )(gated, taps, skip, fwd, inv)


def grad_path(mix, spec_g, spec_h, skip, fwd, inv, filter_blocks):
    shards, rows, chans = mix.shape
    live = min(filter_blocks, shards)
    steps = shards + 1

    def kernel(m_ref, gs_ref, hs_ref, skip_ref, fwd_ref, inv_ref, gg_ref, raw_ref, sq_ref, a_ref, y_ref):
        k = pl.program_id(0)

        @pl.when(k == 0)
        def _():
            split_in(m_ref, a_ref, 0, shards, rows, chans)

        m_re, m_im = forward(fwd_ref[0], a_ref[k, 0], a_ref[k, 1], rows)
        for at, ref in ((0, hs_ref), (2, gs_ref)):
            c_re = ref[0, 0]
            c_im = ref[0, 1]
            y_re, y_im = backward(inv_ref[0], c_re * m_re + c_im * m_im, c_re * m_im - c_im * m_re, rows)
            y_ref[k, at] = y_re
            y_ref[k, at + 1] = y_im

        @pl.when(k == steps - 1)
        def _():
            sq_ref[...] = jnp.zeros(sq_ref.shape, F32)

            def back_work(rs, cs):
                out = real_idft(load_spec(y_ref, 0, shards, rs, cs), shards)
                gain = skip_ref[:, cs]
                for s in range(shards):
                    total = out[s] + gain * m_ref[s, rs, cs].astype(F32)
                    gg_ref[s, rs, cs] = total.astype(BF16)

            over_tiles(rows, chans, back_work)

            def raw_work(rs, cs):
                out = real_idft(load_spec(y_ref, 2, shards, rs, cs), shards)
                square = None
                for s in range(live):
                    raw_ref[s, rs, cs] = out[s].astype(BF16)
                    square = add(square, out[s] * out[s])
                for s in range(live, filter_blocks):
                    raw_ref[s, rs, cs] = jnp.zeros(out[0].shape, BF16)
                sq_ref[:, cs] += square[:8] + square[8:]

            over_tiles(rows, chans, raw_work)

    return pl.pallas_call(
        kernel,
        grid=(steps,),
        in_specs=[
            whole((shards, rows, chans)),
            per_step((1, 2, rows, chans)),
            per_step((1, 2, rows, chans)),
            whole((1, chans)),
            per_step((1, 2 * rows, rows)),
            per_step((1, 2 * rows, rows)),
        ],
        out_specs=[
            whole((shards, rows, chans)),
            whole((filter_blocks, rows, chans)),
            whole((8, chans)),
        ],
        out_shape=[
            jax.ShapeDtypeStruct((shards, rows, chans), BF16),
            jax.ShapeDtypeStruct((filter_blocks, rows, chans), BF16),
            jax.ShapeDtypeStruct((8, chans), F32),
        ],
        scratch_shapes=[
            pltpu.VMEM((steps, 2, rows, chans), BF16),
            pltpu.VMEM((steps, 4, rows, chans), F32),
        ],
        cost_estimate=pl.CostEstimate(flops=30 * 10**9, transcendentals=0, bytes_accessed=40 * 10**6),
        name="grad_path",
    )(mix, spec_g, spec_h, skip, fwd, inv)


def groups_of(chans):
    return 1 if chans % LANES == 0 else LANES // chans


def put(ref, rs, c, value):
    groups, _, chans = ref.shape
    if groups == 1:
        ref[0, rs, pl.ds(c, value.shape[1])] = value
        return
    for i in range(groups):
        ref[i, rs, :] = value[:, i * chans : (i + 1) * chans]


def take(ref, rs, c, lanes):
    groups = ref.shape[0]
    if groups == 1:
        return ref[0, rs, pl.ds(c, lanes)].astype(F32)
    return jnp.concatenate([ref[i, rs, :].astype(F32) for i in range(groups)], axis=1)


def pack_taps(long_filter, shards):
    rows, width = long_filter.shape
    chans = width // shards
    groups = groups_of(chans)

    def kernel(x_ref, o_ref):
        for c in range(0, chans * groups, LANES):
            put(o_ref, pl.ds(0, rows), c, x_ref[:, pl.ds(c, LANES)].astype(BF16))

    return pl.pallas_call(
        kernel,
        grid=(shards // groups,),
        in_specs=[pl.BlockSpec((rows, chans * groups), lambda i: (0, i))],
        out_specs=pl.BlockSpec((groups, rows, chans), lambda i: (i, 0, 0)),
        out_shape=jax.ShapeDtypeStruct((shards, rows, chans), BF16),
        name="pack_taps",
    )(long_filter)


def scale_taps(raw, clip):
    shards, rows, chans = raw.shape
    groups = groups_of(chans)

    def kernel(c_ref, x_ref, o_ref):
        for c in range(0, chans * groups, LANES):
            o_ref[:, pl.ds(c, LANES)] = take(x_ref, pl.ds(0, rows), c, LANES) * c_ref[0, 0]

    return pl.pallas_call(
        kernel,
        grid=(shards // groups,),
        in_specs=[
            pl.BlockSpec(memory_space=pltpu.SMEM),
            pl.BlockSpec((groups, rows, chans), lambda i: (i, 0, 0)),
        ],
        out_specs=pl.BlockSpec((rows, chans * groups), lambda i: (0, i)),
        out_shape=jax.ShapeDtypeStruct((rows, shards * chans), F32),
        name="scale_taps",
    )(clip, raw)


def short_rows(ext_ref, w_ref, i, cs, r, rows):
    total = w_ref[i, 0:1, cs] * ext_ref[i, pl.ds(HALO + r, rows), :]
    for j in range(1, TAPS):
        total = total + w_ref[i, j : j + 1, cs] * ext_ref[i, pl.ds(HALO + r - j, rows), :]
    return total


def gates(streams, before, grad_out, short_filter, shards):
    _, rows, width = streams.shape
    chans = width // shards
    groups = groups_of(chans)
    block = chans * groups
    chunk = math.gcd(rows, 64)

    def kernel(x_ref, b_ref, go_ref, w_ref, g_ref, m_ref, bias_ref, ext_ref):
        for c in range(0, block, LANES):
            cs = pl.ds(c, LANES)
            for i in range(3):
                ext_ref[i, pl.ds(0, HALO), :] = b_ref[i, :, cs].astype(F32)
                ext_ref[i, pl.ds(HALO, rows), :] = x_ref[i, :, cs].astype(F32)
            total = jnp.zeros((1, LANES), F32)
            for r in range(0, rows, chunk):
                rs = pl.ds(r, chunk)
                gated = short_rows(ext_ref, w_ref, 0, cs, r, chunk) * short_rows(ext_ref, w_ref, 2, cs, r, chunk)
                gated = gated.astype(BF16)
                mix = go_ref[rs, cs].astype(F32) * short_rows(ext_ref, w_ref, 1, cs, r, chunk)
                mix = mix.astype(BF16)
                put(g_ref, rs, c, gated)
                put(m_ref, rs, c, mix)
                total = total + jnp.sum(gated.astype(F32) * mix.astype(F32), axis=0, keepdims=True)
            bias_ref[:, cs] = total

    blocks = jax.ShapeDtypeStruct((shards, rows, chans), BF16)
    return pl.pallas_call(
        kernel,
        grid=(shards // groups,),
        in_specs=[
            pl.BlockSpec((3, rows, block), lambda i: (0, 0, i)),
            pl.BlockSpec((3, HALO, block), lambda i: (0, 0, i)),
            pl.BlockSpec((rows, block), lambda i: (0, i)),
            pl.BlockSpec((3, TAPS, block), lambda i: (0, 0, i)),
        ],
        out_specs=[
            pl.BlockSpec((groups, rows, chans), lambda i: (i, 0, 0)),
            pl.BlockSpec((groups, rows, chans), lambda i: (i, 0, 0)),
            pl.BlockSpec((1, block), lambda i: (0, i)),
        ],
        out_shape=[blocks, blocks, jax.ShapeDtypeStruct((1, width), F32)],
        scratch_shapes=[pltpu.VMEM((3, rows + HALO, LANES), F32)],
        cost_estimate=pl.CostEstimate(flops=60 * 10**6, transcendentals=0, bytes_accessed=14 * 10**6),
        name="gates",
    )(streams, before, grad_out, short_filter)


def finish(streams, before, grad_out, short_filter, mixed, gg, after, shards):
    _, rows, width = streams.shape
    chans = width // shards
    groups = groups_of(chans)
    block = chans * groups
    chunk = math.gcd(rows, 64)

    def kernel(x_ref, b_ref, go_ref, w_ref, mi_ref, gg_ref, n_ref, o_ref, gs_ref, st_ref, ext_ref, pre_ref):
        for c in range(0, block, LANES):
            cs = pl.ds(c, LANES)
            for i in range(3):
                ext_ref[i, pl.ds(0, HALO), :] = b_ref[i, :, cs].astype(F32)
                ext_ref[i, pl.ds(HALO, rows), :] = x_ref[i, :, cs].astype(F32)
                pre_ref[i, pl.ds(rows, HALO), :] = n_ref[i, :, cs]
            for r in range(0, rows, chunk):
                rs = pl.ds(r, chunk)
                mixed_rows = take(mi_ref, rs, c, LANES)
                back = take(gg_ref, rs, c, LANES)
                pre_ref[0, rs, :] = back * short_rows(ext_ref, w_ref, 2, cs, r, chunk)
                pre_ref[2, rs, :] = back * short_rows(ext_ref, w_ref, 0, cs, r, chunk)
                pre_ref[1, rs, :] = go_ref[rs, cs].astype(F32) * mixed_rows
                o_ref[rs, cs] = (short_rows(ext_ref, w_ref, 1, cs, r, chunk) * mixed_rows).astype(BF16)
            for i in range(3):
                sums = [jnp.zeros((8, LANES), F32) for _ in range(TAPS)]
                for r in range(0, rows, chunk):
                    rs = pl.ds(r, chunk)
                    own = pre_ref[i, rs, :]
                    total = w_ref[i, 0:1, cs] * own
                    for j in range(TAPS):
                        if j:
                            total = total + w_ref[i, j : j + 1, cs] * pre_ref[i, pl.ds(r + j, chunk), :]
                        term = own * ext_ref[i, pl.ds(HALO + r - j, chunk), :]
                        sums[j] = sums[j] + jnp.sum(term.reshape(chunk // 8, 8, LANES), axis=0)
                    gs_ref[i, rs, cs] = total.astype(BF16)
                for j in range(TAPS):
                    st_ref[i, j : j + 1, cs] = jnp.sum(sums[j], axis=0, keepdims=True)

    return pl.pallas_call(
        kernel,
        grid=(shards // groups,),
        in_specs=[
            pl.BlockSpec((3, rows, block), lambda i: (0, 0, i)),
            pl.BlockSpec((3, HALO, block), lambda i: (0, 0, i)),
            pl.BlockSpec((rows, block), lambda i: (0, i)),
            pl.BlockSpec((3, TAPS, block), lambda i: (0, 0, i)),
            pl.BlockSpec((groups, rows, chans), lambda i: (i, 0, 0)),
            pl.BlockSpec((groups, rows, chans), lambda i: (i, 0, 0)),
            pl.BlockSpec((3, HALO, block), lambda i: (0, 0, i)),
        ],
        out_specs=[
            pl.BlockSpec((rows, block), lambda i: (0, i)),
            pl.BlockSpec((3, rows, block), lambda i: (0, 0, i)),
            pl.BlockSpec((3, TAPS, block), lambda i: (0, 0, i)),
        ],
        out_shape=[
            jax.ShapeDtypeStruct((rows, width), BF16),
            jax.ShapeDtypeStruct((3, rows, width), BF16),
            jax.ShapeDtypeStruct((3, TAPS, width), F32),
        ],
        scratch_shapes=[
            pltpu.VMEM((3, rows + HALO, LANES), F32),
            pltpu.VMEM((3, rows + HALO, LANES), F32),
        ],
        cost_estimate=pl.CostEstimate(flops=150 * 10**6, transcendentals=0, bytes_accessed=24 * 10**6),
        name="finish",
    )(streams, before, grad_out, short_filter, mixed, gg, after)


def from_behind(block, axis, distance):
    devices = range(lax.axis_size(axis))
    route = [(i - distance, i) for i in devices if i - distance in devices]
    return lax.ppermute(block, axis, route)


def exchange(blocks):
    return lax.all_to_all(blocks, "seq", split_axis=0, concat_axis=0, tiled=True)


def first_rows_of(streams, before, grad_out, short_filter, mixed, gg, shards):
    width = streams.shape[2]
    top = jnp.concatenate([before, streams[:, :HALO]], axis=1).astype(F32)

    def short(i):
        total = short_filter[i, 0] * top[i, HALO:]
        for j in range(1, TAPS):
            total = total + short_filter[i, j] * top[i, HALO - j : 2 * HALO - j]
        return total

    def rows_of(blocks):
        return blocks[:, :HALO].transpose(1, 0, 2).reshape(HALO, width).astype(F32)

    mixed_top = rows_of(mixed)
    gg_top = rows_of(gg)
    gout_top = grad_out[:HALO].astype(F32)
    return jnp.stack([gg_top * short(2), gout_top * mixed_top, gg_top * short(0)])


def body(streams, grad_out, long_filter, short_filter, skip_gain):
    shards = lax.axis_size("seq")
    rows = streams.shape[1]
    chans = streams.shape[2] // shards
    filter_len = long_filter.shape[0] * shards
    filter_blocks = filter_len // rows
    fwd, inv = turn_tables(shards, rows)
    taps = exchange(pack_taps(long_filter, shards)).reshape(filter_blocks, rows, chans)
    before = from_behind(streams[:, rows - HALO :], "seq", 1)
    gated, mix, bias_part = gates(streams, before, grad_out, short_filter, shards)
    skip = lax.dynamic_slice_in_dim(skip_gain, lax.axis_index("seq") * chans, chans)[None]
    gated_all = exchange(gated)
    mix_all = exchange(mix)
    mixed_all, spec_g, spec_h = value_path(gated_all, taps, skip, fwd, inv)
    mixed = exchange(mixed_all)
    gg_all, raw_all, sq_part = grad_path(mix_all, spec_g, spec_h, skip, fwd, inv, filter_blocks)
    gg = exchange(gg_all)
    raw = exchange(raw_all.reshape(shards, filter_len // shards, chans))
    after = from_behind(first_rows_of(streams, before, grad_out, short_filter, mixed, gg, shards), "seq", -1)
    output, grad_streams, short_part = finish(
        streams, before, grad_out, short_filter, mixed, gg, after, shards
    )
    short_bias = jnp.concatenate([short_part.reshape(3 * TAPS, -1), bias_part], axis=0)
    short_bias = lax.psum(short_bias, "seq")
    local_sq = jnp.sum(sq_part) + jnp.sum(short_bias * short_bias) / shards
    sq_total = lax.psum(local_sq, ("seq", "chan"))
    param_count = LF * D + (3 * TAPS + 1) * D
    clip = 1.0 / jnp.sqrt(sq_total / param_count + 1e-06)
    filter_grad = scale_taps(raw, clip.reshape(1, 1))
    small = short_bias * clip
    return (
        output,
        grad_streams,
        filter_grad,
        small[: 3 * TAPS].reshape(3, TAPS, -1),
        small[3 * TAPS],
    )


def solution(mesh):
    placed = (
        P(None, "seq", "chan"),
        P("seq", "chan"),
        P("seq", "chan"),
        P(None, None, "chan"),
        P("chan"),
    )
    return jax.shard_map(
        body,
        mesh=mesh,
        in_specs=placed,
        out_specs=(
            P("seq", "chan"),
            P(None, "seq", "chan"),
            P("seq", "chan"),
            P(None, None, "chan"),
            P("chan"),
        ),
        check_vma=False,
    )
```

time: 1500 us -> 649 us (0.43)
  other arithmetic: 359 us -> 17.4 us
  blocking collectives: 366 us -> 97.5 us
  matrix products: 234 us -> 0 us
  local copies, waits for them, and re-layouts: 164 us -> 7.81 us
  Pallas kernels: 0 us -> 125 us
  waiting for transfers between devices: 298 us -> 324 us
    psum x1 -> x0, blocking collectives: 240 us -> none  [body(): raw_short, raw_bias = lax.psum((short_part, bias_part), 'seq')]
    dot_general x12 -> x0, matrix products: 234 us -> none  [the longest x3 98.9 us: spectrum(): return jnp.einsum('ckm,mj->ckj', middle, inner_fwd, precision=precise)]
    pallas_call x0 -> x6, Pallas kernels: none -> 125 us  [the longest x1 32.8 us: value_path(): pl.pallas_call(kernel, grid=(steps,), in_specs=[whole((shards, rows, chan...]
    add x4 -> x0, other arithmetic: 115 us -> none  [the longest x2 45.9 us: conj_times(): left_real * right_real + left_imag * right_imag]
    psum x1, waiting for transfers between devices: 90.4 us -> 186 us  [body(): short_bias = lax.psum(short_bias, 'seq')]
    all_to_all x5, waiting for transfers between devices: 200 us -> 117 us  [exchange(): lax.all_to_all(blocks, 'seq', split_axis=0, concat_axis=0, tiled=True)]
    concatenate x8 -> x2, other arithmetic: 73.2 us -> 3.19 us  [the longest x1 2.4 us: pair(): return (jnp.concatenate([cos, sin], axis=1) * gain).astype(BF16)]
    convert_element_type x5 -> x4, other arithmetic: 59.3 us -> 4.18 us  [the longest x1 3.26 us: pair(): return (jnp.concatenate([cos, sin], axis=1) * gain).astype(BF16)]
  transfers between devices with their start and end apart: 8 -> 8, of which waited for: 7 -> 7; matrix products, arithmetic and copies ran while one was open for 11% -> 3% of each run, Pallas kernels for 0% -> 15%
where the time goes in v1:
time: 649 us; the launch traced here: 646 us
  waiting for transfers between devices  324 us (50%)
  Pallas kernels  125 us (19%)
  blocking collectives  97.5 us (15%)
  starting transfers between devices  57.9 us (9%)
  other arithmetic  17.4 us (3%)
  between operations  16.2 us (2%)
  local copies, waits for them, and re-layouts  7.81 us (1%)
    psum x1, waiting for transfers between devices, body(): short_bias = lax.psum(short_bias, 'seq')  186 us
    all_to_all x5, waiting for transfers between devices, exchange(): lax.all_to_all(blocks, 'seq', split_axis=0, concat_axis=0, tiled=True)  117 us
    all_to_all x1, blocking collectives, exchange(): lax.all_to_all(blocks, 'seq', split_axis=0, concat_axis=0, tiled=True)  58.1 us
    all_to_all x5, starting transfers between devices, exchange(): lax.all_to_all(blocks, 'seq', split_axis=0, concat_axis=0, tiled=True)  51.5 us
    psum x1, blocking collectives, body(): sq_total = lax.psum(local_sq, ('seq', 'chan'))  39.4 us
    pallas_call x1, Pallas kernels, value_path(): pl.pallas_call(kernel, grid=(steps,), in_specs=[whole((shards, rows, chan...  32.8 us
    pallas_call x1, Pallas kernels, grad_path(): pl.pallas_call(kernel, grid=(steps,), in_specs=[whole((shards, rows, chan...  32.2 us
    pallas_call x1, Pallas kernels, finish(): pl.pallas_call(kernel, grid=(shards // groups,), in_specs=[pl.BlockSpec((...  24.1 us
  transfers between devices with their start and end apart: 8, of which 7 were waited for; matrix products, arithmetic and copies ran while one was open for 3% of the time, Pallas kernels for 15%

profile of v1, /device:TPU:0, one launch (start us, length us, event | category | flops | bytes accessed | tf_op | source)
XLA Modules:
  0.0 646.1 jit_solution(10020067753472321239)
XLA Ops:
  7.2 1.1 fusion.31
  8.2 4.9 collective-permute-start
  13.1 4.1 collective-permute-done.b_ref
  17.9 14.2 %gates.1 = (bf16[16,256,256]{2,1,0:T(8,128)(2,1)}, bf16[16,256,256]{2,1,0:T(8,128)(2,1)}, f32[1,4096]{1,0:T(1,128)}) custom-call(bf16[3,256,4096]{2,1,0:T(8,128)(2,1)} %x_ref.5, bf16[3,8,4096]{2,1,0:T(8,128)(2,1)} %copy-done.4, bf16[256,4096]{1,0:T(8,128)(2,1)} %go_ref.3, f32[3,7,4096]{2,1,0:T(8,128)} %w_ref.3), custom_call_target="tpu_custom_call" | custom-call | flops 60000000 | bytes 14000000 | tf_op jit(solution)/shard_map/gates/pallas_call | solution.py:466
  32.1 7.9 %all-to-all-start = ((bf16[16,256,256]{2,1,0:T(8,128)(2,1)}), bf16[16,256,256]{2,1,0:T(8,128)(2,1)S(1)}, u32[]{:S(2)}, u32[]{:S(2)}) async-start(bf16[16,256,256]{2,1,0:T(8,128)(2,1)} %get-tuple-element.17), calls=%async_computation | async-start | bytes 4194304 | tf_op jit(solution)/shard_map/all_to_all | solution.py:562
  40.0 11.0 %pack_taps.1 = bf16[16,512,256]{2,1,0:T(8,128)(2,1)} custom-call(f32[512,4096]{1,0:T(8,128)} %x_ref.4), custom_call_target="tpu_custom_call" | custom-call | tf_op jit(solution)/shard_map/pack_taps/pallas_call | solution.py:402
  51.0 31.4 %all-to-all-done.g_ref = bf16[16,256,256]{2,1,0:T(8,128)(2,1)S(1)} async-done(((bf16[16,256,256]{2,1,0:T(8,128)(2,1)}), bf16[16,256,256]{2,1,0:T(8,128)(2,1)S(1)}, u32[]{:S(2)}, u32[]{:S(2)}) %all-to-all-start) | async-done | bytes 2097184 | tf_op jit(solution)/shard_map/all_to_all | solution.py:562
  82.4 9.9 %all-to-all-start.1 = ((bf16[16,512,256]{2,1,0:T(8,128)(2,1)}), bf16[16,512,256]{2,1,0:T(8,128)(2,1)}, u32[]{:S(2)}, u32[]{:S(2)}) async-start(bf16[16,512,256]{2,1,0:T(8,128)(2,1)} %pack_taps.1), calls=%async_computation.1 | async-start | bytes 8388608 | tf_op jit(solution)/shard_map/all_to_all | solution.py:562
  92.3 1.4 dynamic_slice.3
  93.7 1.7 fusion.21
  95.4 75.4 %all-to-all-done.1 = bf16[16,512,256]{2,1,0:T(8,128)(2,1)} async-done(((bf16[16,512,256]{2,1,0:T(8,128)(2,1)}), bf16[16,512,256]{2,1,0:T(8,128)(2,1)}, u32[]{:S(2)}, u32[]{:S(2)}) %all-to-all-start.1) | async-done | bytes 4194336 | tf_op jit(solution)/shard_map/all_to_all | solution.py:562
  170.7 19.3 %all-to-all-start.3 = ((bf16[16,256,256]{2,1,0:T(8,128)(2,1)}), bf16[16,256,256]{2,1,0:T(8,128)(2,1)S(1)}, u32[]{:S(2)}, u32[]{:S(2)}) async-start(bf16[16,256,256]{2,1,0:T(8,128)(2,1)} %get-tuple-element.19), calls=%async_computation.3 | async-start | bytes 4194304 | tf_op jit(solution)/shard_map/all_to_all | solution.py:562
  190.2 3.7 multiply_subtract_fusion
  194.0 2.4 pad_maximum_fusion.fwd_ref
  196.4 3.3 fusion.inv_ref
  199.6 32.8 %value_path.1 = (bf16[16,256,256]{2,1,0:T(8,128)(2,1)}, f32[17,2,256,256]{3,2,1,0:T(8,128)}, f32[17,2,256,256]{3,2,1,0:T(8,128)}) custom-call(bf16[16,256,256]{2,1,0:T(8,128)(2,1)} %copy-done.2, bf16[32,256,256]{2,1,0:T(8,128)(2,1)} %bitcast.h_ref, f32[1,256]{1,0:T(1,128)} %bitcast.48, bf16[17,512,256]{2,1,0:T(8,128)(2,1)} %pad_maximum_fusion.fwd_ref, ...), custom_call_target="tpu_custom_call" | custom-call | flops 30000001024 | bytes 40000000 | tf_op jit(solution)/shard_map/value_path/pallas_call | solution.py:273
  232.7 1.3 copy-done.3
  234.0 9.8 %all-to-all-start.2 = ((bf16[16,256,256]{2,1,0:T(8,128)(2,1)}), bf16[16,256,256]{2,1,0:T(8,128)(2,1)S(1)}, u32[]{:S(2)}, u32[]{:S(2)}) async-start(bf16[16,256,256]{2,1,0:T(8,128)(2,1)} %get-tuple-element.18), calls=%async_computation.2 | async-start | bytes 4194304 | tf_op jit(solution)/shard_map/all_to_all | solution.py:562
  243.8 32.2 %grad_path.1 = (bf16[16,256,256]{2,1,0:T(8,128)(2,1)}, bf16[32,256,256]{2,1,0:T(8,128)(2,1)}, f32[8,256]{1,0:T(8,128)}) custom-call(bf16[16,256,256]{2,1,0:T(8,128)(2,1)} %copy-done.3, f32[17,2,256,256]{3,2,1,0:T(8,128)} %get-tuple-element.20.gs_ref, f32[17,2,256,256]{3,2,1,0:T(8,128)} %get-tuple-element.21.hs_ref, f32[1,256]{1,0:T(1,128)} %bitcast.49, ...), custom_call_target="tpu_custom_call" | custom-call | flops 30000001024 | bytes 40000000 | tf_op jit(solution)/shard_map/grad_path/pallas_call | solution.py:343
  275.9 10.4 %all-to-all-done.2.mi_ref = bf16[16,256,256]{2,1,0:T(8,128)(2,1)S(1)} async-done(((bf16[16,256,256]{2,1,0:T(8,128)(2,1)}), bf16[16,256,256]{2,1,0:T(8,128)(2,1)S(1)}, u32[]{:S(2)}, u32[]{:S(2)}) %all-to-all-start.2) | async-done | bytes 2097184 | tf_op jit(solution)/shard_map/all_to_all | solution.py:562
  286.3 58.1 %all_to_all.30.gg_ref = bf16[16,256,256]{2,1,0:T(8,128)(2,1)} all-to-all(bf16[16,256,256]{2,1,0:T(8,128)(2,1)} %get-tuple-element.22), channel_id=1, replica_groups=mesh['seq'=16,'chan'=2] {'seq'}, dimensions={0} | all-to-all | bytes 4194304 | tf_op jit(solution)/shard_map/all_to_all | solution.py:562
  344.5 4.7 all-to-all-start.5
  350.4 0.9 multiply_bitcast_fusion
  351.5 1.4 collective-permute-start.1
  353.0 16.8 %collective-permute-done.1.n_ref = f32[3,8,4096]{2,1,0:T(8,128)S(1)} collective-permute-done((f32[3,8,4096]{2,1,0:T(8,128)S(1)}, f32[3,8,4096]{2,1,0:T(8,128)S(1)}, u32[]{:S(2)}, u32[]{:S(2)}) %collective-permute-start.1) | collective-permute-done | bytes 393248 | tf_op jit(solution)/shard_map/ppermute | solution.py:558
  370.5 24.1 %finish.1 = (bf16[256,4096]{1,0:T(8,128)(2,1)}, bf16[3,256,4096]{2,1,0:T(8,128)(2,1)}, f32[3,7,4096]{2,1,0:T(8,128)}) custom-call(bf16[3,256,4096]{2,1,0:T(8,128)(2,1)} %x_ref.5, bf16[3,8,4096]{2,1,0:T(8,128)(2,1)} %copy-done.4, bf16[256,4096]{1,0:T(8,128)(2,1)} %go_ref.3, f32[3,7,4096]{2,1,0:T(8,128)} %w_ref.3, bf16[16,256,256]{2,1,0:T(8,128)(2,1)} %copy-done, ...), custom_call_target="tpu_custom_call" | custom-call | flops 150000000 | bytes 24000000 | tf_op jit(solution)/shard_map/finish/pallas_call | solution.py:524
  394.5 1.0 reshape.247
  397.0 186.0 %all-reduce.2.cloned.1.call-done = f32[22,4096]{1,0:T(8,128)} async-done(((f32[22,4096]{1,0:T(8,128)}), f32[22,4096]{1,0:T(8,128)}) %all-reduce.2.cloned.1.call-update) | async-done | bytes 360464 | tf_op jit(solution)/shard_map/psum | solution.py:607
  583.0 1.7 multiply_reduce_fusion
  586.0 39.4 %psum.15 = f32[]{:T(128)} all-reduce(f32[]{:T(128)S(6)} %add.129), channel_id=1, replica_groups=mesh['seq'=16,'chan'=2] {'seq','chan'}, use_global_device_ids=true, to_apply=%region_3.4 | all-reduce | flops 1 | bytes 8 | tf_op jit(solution)/shard_map/psum | solution.py:609
  626.0 1.0 broadcast_multiply_fusion
  628.5 10.8 %scale_taps.1 = f32[512,4096]{1,0:T(8,128)} custom-call(f32[1,1]{1,0:T(1,128)} %bitcast.22.c_ref, bf16[16,512,256]{2,1,0:T(8,128)(2,1)} %all-to-all-done.5.x_ref), custom_call_target="tpu_custom_call" | custom-call | tf_op jit(solution)/shard_map/scale_taps/pallas_call | solution.py:420
  (33 shorter events, 6.0 us)
Async XLA Ops:
  8.2 9.0 %collective-permute-start = (bf16[3,8,4096]{2,1,0:T(8,128)(2,1)S(1)}, bf16[3,8,4096]{2,1,0:T(8,128)(2,1)S(1)}, u32[]{:S(2)}, u32[]{:S(2)}) collective-permute-start(bf16[3,8,4096]{2,1,0:T(8,128)(2,1)S(1)} %get-tuple-element.30), channel_id=1, source_target_pairs={{0,2},{2,4},{4,6},{6,8},{8,10},{10,12},{12,14},{14,16},{16,18},{18... | collective-permute-start | bytes 589832 | tf_op jit(solution)/shard_map/ppermute | solution.py:558
  17.2 0.7 copy-start.4
  32.1 50.3 %all-to-all-start = ((bf16[16,256,256]{2,1,0:T(8,128)(2,1)}), bf16[16,256,256]{2,1,0:T(8,128)(2,1)S(1)}, u32[]{:S(2)}, u32[]{:S(2)}) async-start(bf16[16,256,256]{2,1,0:T(8,128)(2,1)} %get-tuple-element.17), calls=%async_computation | async-start | bytes 4194304 | tf_op jit(solution)/shard_map/all_to_all | solution.py:562
  82.4 13.0 %copy-start.2 = (bf16[16,256,256]{2,1,0:T(8,128)(2,1)}, bf16[16,256,256]{2,1,0:T(8,128)(2,1)S(1)}, u32[]{:S(2)}) copy-start(bf16[16,256,256]{2,1,0:T(8,128)(2,1)S(1)} %all-to-all-done.g_ref) | copy-start | bytes 6291460
  82.4 88.3 %all-to-all-start.1 = ((bf16[16,512,256]{2,1,0:T(8,128)(2,1)}), bf16[16,512,256]{2,1,0:T(8,128)(2,1)}, u32[]{:S(2)}, u32[]{:S(2)}) async-start(bf16[16,512,256]{2,1,0:T(8,128)(2,1)} %pack_taps.1), calls=%async_computation.1 | async-start | bytes 8388608 | tf_op jit(solution)/shard_map/all_to_all | solution.py:562
  170.7 61.9 %all-to-all-start.3 = ((bf16[16,256,256]{2,1,0:T(8,128)(2,1)}), bf16[16,256,256]{2,1,0:T(8,128)(2,1)S(1)}, u32[]{:S(2)}, u32[]{:S(2)}) async-start(bf16[16,256,256]{2,1,0:T(8,128)(2,1)} %get-tuple-element.19), calls=%async_computation.3 | async-start | bytes 4194304 | tf_op jit(solution)/shard_map/all_to_all | solution.py:562
  232.6 1.3 copy-start.3
  234.0 52.4 %all-to-all-start.2 = ((bf16[16,256,256]{2,1,0:T(8,128)(2,1)}), bf16[16,256,256]{2,1,0:T(8,128)(2,1)S(1)}, u32[]{:S(2)}, u32[]{:S(2)}) async-start(bf16[16,256,256]{2,1,0:T(8,128)(2,1)} %get-tuple-element.18), calls=%async_computation.2 | async-start | bytes 4194304 | tf_op jit(solution)/shard_map/all_to_all | solution.py:562
  286.3 64.0 %copy-start = (bf16[16,256,256]{2,1,0:T(8,128)(2,1)}, bf16[16,256,256]{2,1,0:T(8,128)(2,1)S(1)}, u32[]{:S(2)}) copy-start(bf16[16,256,256]{2,1,0:T(8,128)(2,1)S(1)} %all-to-all-done.2.mi_ref) | copy-start | bytes 6291460
  344.5 4.7 copy-start.1
  344.5 4.9 copy-start.5
  344.5 284.0 %all-to-all-start.5 = ((bf16[16,512,256]{2,1,0:T(8,128)(2,1)}), bf16[16,512,256]{2,1,0:T(8,128)(2,1)}, u32[]{:S(2)}, u32[]{:S(2)}) async-start(bf16[16,512,256]{2,1,0:T(8,128)(2,1)} %bitcast.28), calls=%async_computation.5 | async-start | bytes 8388608 | tf_op jit(solution)/shard_map/all_to_all | solution.py:562
  349.2 233.8 %all-reduce.2.cloned.1.call-start = ((), (), s32[]{:S(2)}) async-start(), calls=%async_computation.6 | async-start | bytes 786432 | tf_op jit(solution)/shard_map/psum | solution.py:607
  351.5 44.1 %copy-start.7 = (f32[1,4096]{1,0:T(1,128)S(1)}, f32[1,4096]{1,0:T(1,128)}, u32[]{:S(2)}) copy-start(f32[1,4096]{1,0:T(1,128)} %get-tuple-element.27) | copy-start | bytes 49156
  351.5 44.9 %copy-start.8 = (f32[8,256]{1,0:T(8,128)S(1)}, f32[8,256]{1,0:T(8,128)}, u32[]{:S(2)}) copy-start(f32[8,256]{1,0:T(8,128)} %get-tuple-element.25) | copy-start | bytes 24580
  351.5 18.2 %collective-permute-start.1 = (f32[3,8,4096]{2,1,0:T(8,128)S(1)}, f32[3,8,4096]{2,1,0:T(8,128)S(1)}, u32[]{:S(2)}, u32[]{:S(2)}) collective-permute-start(f32[3,8,4096]{2,1,0:T(8,128)S(1)} %pad_maximum_fusion.1), channel_id=1, source_target_pairs={{2,0},{4,2},{6,4},{8,6},{10,8},{12,10},{14,12},{16,14},{18,16},{20... | collective-permute-start | bytes 1179656 | tf_op jit(solution)/shard_map/ppermute | solution.py:558
  369.7 0.7 copy-start.6
Sparse Core Ops, SparseCore 0:
  396.5 186.4 all-reduce.1

commit v2 on v1

v2 whole, which is shorter than its diff:
```python
import math

import jax
import jax.numpy as jnp
from jax import lax
from jax.experimental import pallas as pl
from jax.experimental.pallas import tpu as pltpu
from jax.sharding import PartitionSpec as P

D = 8192
LF = 8192
TAPS = 7
HALO = 8
EDGE = 16
LANES = 128
SUMS = 24
F32 = jnp.float32
BF16 = jnp.bfloat16


def add(a, b):
    if a is None:
        return b
    if b is None:
        return a
    return a + b


def neg(a):
    return None if a is None else -a


def sub(a, b):
    if b is None:
        return a
    if a is None:
        return -b
    return a - b


def scaled(a, c):
    if a is None or abs(c) < 1e-12:
        return None
    if abs(c - 1.0) < 1e-12:
        return a
    if abs(c + 1.0) < 1e-12:
        return -a
    return a * c


def cadd(a, b):
    return (add(a[0], b[0]), add(a[1], b[1]))


def csub(a, b):
    return (sub(a[0], b[0]), sub(a[1], b[1]))


def times_i(a, sign):
    return (neg(a[1]), a[0]) if sign > 0 else (a[1], neg(a[0]))


def cmul(a, angle, gain=1.0):
    c = math.cos(angle)
    s = math.sin(angle)
    re, im = a
    if abs(abs(c) - abs(s)) < 1e-12 and re is not None and im is not None:
        root = abs(c) * gain
        sc = 1.0 if c > 0 else -1.0
        ss = 1.0 if s > 0 else -1.0
        if sc * ss > 0:
            return ((re - im) * (root * sc), (re + im) * (root * sc))
        return ((re + im) * (root * sc), (im - re) * (root * sc))
    c = c * gain
    s = s * gain
    return (sub(scaled(re, c), scaled(im, s)), add(scaled(im, c), scaled(re, s)))


def complex_dft(xs, sign):
    n = len(xs)
    if n == 1:
        return list(xs)
    half = n // 2
    sums = [cadd(xs[i], xs[i + half]) for i in range(half)]
    difs = [csub(xs[i], xs[i + half]) for i in range(half)]
    if n == 2:
        return [sums[0], difs[0]]
    quarter = n // 4
    out = [None] * n
    out[0::2] = complex_dft(sums, sign)
    turn = sign * 2.0 * math.pi / n
    first = []
    third = []
    for i in range(quarter):
        rot = times_i(difs[i + quarter], sign)
        first.append(cmul(cadd(difs[i], rot), turn * i))
        third.append(cmul(csub(difs[i], rot), turn * 3 * i))
    out[1::4] = complex_dft(first, sign)
    out[3::4] = complex_dft(third, sign)
    return out


def real_dft(xs):
    n = len(xs)
    if n == 1:
        return [(xs[0], None)]
    half = n // 2
    sums = [add(xs[i], xs[i + half]) for i in range(half)]
    difs = [sub(xs[i], xs[i + half]) for i in range(half)]
    if n == 2:
        return [(sums[0], None), (difs[0], None)]
    quarter = n // 4
    out = [None] * (half + 1)
    out[0::2] = real_dft(sums)
    turn = -2.0 * math.pi / n
    odd = [cmul((difs[i], neg(difs[i + quarter])), turn * i) for i in range(quarter)]
    for j, value in enumerate(complex_dft(odd, -1)):
        k = 4 * j + 1
        if k <= half:
            out[k] = value
        else:
            out[n - k] = (value[0], neg(value[1]))
    return out


def real_idft(spec, keep):
    n = 2 * (len(spec) - 1)
    if n == 2:
        both = [add(spec[0][0], spec[1][0]), sub(spec[0][0], spec[1][0])]
        return both[:keep]
    half = n // 2
    quarter = n // 4
    even = real_idft(spec[0::2], half)
    odd = []
    for j in range(quarter):
        k = 4 * j + 1
        odd.append(spec[k] if k <= half else (spec[n - k][0], neg(spec[n - k][1])))
    turn = 2.0 * math.pi / n
    rest = [cmul(v, turn * i, 2.0) for i, v in enumerate(complex_dft(odd, 1))]
    wave = [rest[i][0] for i in range(quarter)] + [neg(rest[i][1]) for i in range(quarter)]
    out = [add(even[i], wave[i]) for i in range(half)]
    if keep > half:
        out = out + [sub(even[i], wave[i]) for i in range(half)]
    return out[:keep]


def turn_tables(shards, rows):
    radix = 2 * shards
    count = radix * rows
    k1 = jnp.arange(shards + 1, dtype=jnp.int32)[:, None]
    r = jnp.arange(rows, dtype=jnp.int32)
    fine = 2.0 * math.pi / count * (k1 * r[None, :] % count).astype(F32)
    coarse = 2.0 * math.pi / rows * (r[:, None] * r[None, :] % rows).astype(F32)
    fine_c = jnp.cos(fine)
    fine_s = jnp.sin(fine)
    coarse_c = jnp.cos(coarse)[None]
    coarse_s = jnp.sin(coarse)[None]

    def pair(fc, fs, gain):
        cos = fc * coarse_c - fs * coarse_s
        sin = fs * coarse_c + fc * coarse_s
        return (jnp.concatenate([cos, sin], axis=1) * gain).astype(BF16)

    fwd = pair(fine_c[:, None, :], fine_s[:, None, :], 1.0)
    inv = pair(fine_c[:, :, None], fine_s[:, :, None], 1.0 / count)
    return fwd, inv


def over_tiles(rows, work):
    def step(i, carry):
        work(pl.multiple_of(i * 16, 16))
        return carry

    lax.fori_loop(0, rows // 16, step, 0)


def split_in(load, blocks, shards, rows, store):
    def work(r):
        rs = pl.ds(r, 16)
        xs = [load(s, rs).astype(F32) for s in range(blocks)]
        xs = xs + [None] * (2 * shards - blocks)
        for k, (re, im) in enumerate(real_dft(xs)):
            if im is None:
                im = jnp.zeros(re.shape, F32)
            store(k, rs, re.astype(BF16), im.astype(BF16))

    over_tiles(rows, work)


def load_spec(load, shards):
    spec = []
    for k in range(shards + 1):
        re, im = load(k)
        spec.append((re, None if k == 0 or k == shards else im))
    return spec


def dot(a, b):
    return jnp.dot(a, b, preferred_element_type=F32)


def backward(table, z_re, z_im, rows, step):
    chans = z_re.shape[1]
    z_re = z_re.astype(BF16)
    z_im = z_im.astype(BF16)
    if step == chans:
        p = dot(table, jnp.concatenate([z_re, z_im], axis=1))
        return p[:rows, :step] - p[rows:, step:], p[rows:, :step] + p[:rows, step:]
    p = dot(table, z_re)
    q = dot(table, z_im)
    return p[:rows] - q[rows:], p[rows:] + q[:rows]


def whole(shape):
    zeros = (0,) * len(shape)
    return pl.BlockSpec(shape, lambda *_: zeros, pipeline_mode=pl.Buffered(1))


def per_step(shape):
    zeros = (0,) * (len(shape) - 1)
    return pl.BlockSpec(shape, lambda i: (i,) + zeros)


def in_smem():
    return pl.BlockSpec(memory_space=pltpu.SMEM)


def untouched():
    return pl.BlockSpec(memory_space=pl.ANY)


def raw_path(both, fwd, inv, is_low, packed, low_before, part, parts, tap_rows, live, fold):
    shards, _, rows, chans = both.shape
    steps = shards + 1
    step = max(chans, LANES)
    per_shard = tap_rows // rows
    blocks = live * per_shard

    def kernel(*refs):
        refs = list(refs)
        x_ref, fwd_ref, inv_ref = refs[:3]
        del refs[:3]
        if fold:
            flag_ref, h_ref = refs[:2]
            del refs[:2]
        if part:
            del refs[:1]
        spec_ref, low_ref, sq_ref = refs[:3]
        del refs[:3]
        if fold:
            send_ref = refs.pop(0)
        a_ref, y_ref = refs
        k = pl.program_id(0)

        @pl.when(k == 0)
        def _():
            for i in range(2):

                def store(at, rs, re, im, i=i):
                    a_ref[at, 0, rs, pl.ds(i * step, chans)] = re
                    a_ref[at, 1, rs, pl.ds(i * step, chans)] = im

                split_in(lambda s, rs, i=i: x_ref[s, i, rs, :], shards, shards, rows, store)

        p = dot(fwd_ref[0], a_ref[k, 0])
        q = dot(fwd_ref[0], a_ref[k, 1])
        re = p[:rows] + q[rows:]
        im = q[:rows] - p[rows:]
        spec_ref[0, 0] = re
        spec_ref[0, 1] = im
        g_re = re[:, :chans]
        g_im = im[:, :chans]
        m_re = re[:, step : step + chans]
        m_im = im[:, step : step + chans]
        y_re, y_im = backward(inv_ref[0], g_re * m_re + g_im * m_im, g_re * m_im - g_im * m_re, rows, step)
        y_ref[k, 0] = y_re
        y_ref[k, 1] = y_im

        @pl.when(k == steps - 1)
        def _():
            sq_ref[...] = jnp.zeros(sq_ref.shape, F32)

            def work(r):
                rs = pl.ds(r, 16)
                out = real_idft(load_spec(lambda at: (y_ref[at, 0, rs, :], y_ref[at, 1, rs, :]), shards), shards)
                square = None
                for s in range(blocks):
                    low_ref[s // per_shard, 0, pl.ds((s % per_shard) * rows + r, 16), :] = out[s].astype(BF16)
                    square = add(square, out[s] * out[s])
                sq_ref[...] += square[:8] + square[8:]

            over_tiles(rows, work)
            if fold:

                @pl.when(flag_ref[0, 0] == 1)
                def _():
                    for s in range(shards):
                        send_ref[s] = h_ref[s]

                @pl.when(flag_ref[0, 0] == 0)
                def _():
                    for s in range(shards):
                        if s < live:
                            send_ref[s] = low_ref[s, 0]
                        else:
                            send_ref[s] = jnp.zeros((tap_rows, chans), BF16)

    ins = [both, fwd, inv]
    in_specs = [
        whole(both.shape),
        per_step((1, 2 * rows, rows)),
        per_step((1, 2 * rows, rows)),
    ]
    if fold:
        ins += [is_low, packed]
        in_specs += [in_smem(), whole(packed.shape)]
    aliases = {}
    if part:
        aliases = {len(ins): 1}
        ins.append(low_before)
        in_specs.append(untouched())
    out_specs = [
        per_step((1, 2, rows, 2 * step)),
        pl.BlockSpec((live, 1, tap_rows, chans), lambda i: (0, part, 0, 0), pipeline_mode=pl.Buffered(1)),
        whole((8, chans)),
    ]
    out_shape = [
        jax.ShapeDtypeStruct((steps, 2, rows, 2 * step), F32),
        jax.ShapeDtypeStruct((live, parts, tap_rows, chans), BF16),
        jax.ShapeDtypeStruct((8, chans), F32),
    ]
    if fold:
        out_specs.append(whole(packed.shape))
        out_shape.append(jax.ShapeDtypeStruct(packed.shape, BF16))
    return pl.pallas_call(
        kernel,
        grid=(steps,),
        in_specs=in_specs,
        out_specs=out_specs,
        out_shape=out_shape,
        scratch_shapes=[
            pltpu.VMEM((steps, 2, rows, 2 * step), BF16),
            pltpu.VMEM((steps, 2, rows, chans), F32),
        ],
        input_output_aliases=aliases,
        cost_estimate=pl.CostEstimate(flops=20 * 10**9, transcendentals=0, bytes_accessed=25 * 10**6),
        name="raw_path",
    )(*ins)


def conv_path(both, taps, spec, skip, fwd, inv):
    shards, _, rows, chans = both.shape
    steps = shards + 1
    step = max(chans, LANES)
    blocks = min(taps.shape[0], shards)

    def kernel(x_ref, h_ref, spec_ref, skip_ref, fwd_ref, inv_ref, out_ref, a_ref, y_ref):
        k = pl.program_id(0)

        @pl.when(k == 0)
        def _():
            def store(at, rs, re, im):
                a_ref[at, rs, pl.ds(0, chans)] = re
                a_ref[at, rs, pl.ds(step, chans)] = im

            split_in(lambda s, rs: h_ref[s, rs, :], blocks, shards, rows, store)

        p = dot(fwd_ref[0], a_ref[k])
        h_re = p[:rows, :chans] + p[rows:, step : step + chans]
        h_im = p[:rows, step : step + chans] - p[rows:, :chans]
        g_re = spec_ref[0, 0, :, pl.ds(0, chans)]
        g_im = spec_ref[0, 1, :, pl.ds(0, chans)]
        m_re = spec_ref[0, 0, :, pl.ds(step, chans)]
        m_im = spec_ref[0, 1, :, pl.ds(step, chans)]
        y_re, y_im = backward(inv_ref[0], g_re * h_re - g_im * h_im, g_re * h_im + g_im * h_re, rows, step)
        y_ref[k, 0] = y_re
        y_ref[k, 1] = y_im
        y_re, y_im = backward(inv_ref[0], h_re * m_re + h_im * m_im, h_re * m_im - h_im * m_re, rows, step)
        y_ref[k, 2] = y_re
        y_ref[k, 3] = y_im

        @pl.when(k == steps - 1)
        def _():
            gain = skip_ref[...]
            for i in range(2):

                def work(r, i=i):
                    rs = pl.ds(r, 16)
                    spectrum = load_spec(lambda at: (y_ref[at, 2 * i, rs, :], y_ref[at, 2 * i + 1, rs, :]), shards)
                    out = real_idft(spectrum, shards)
                    out = [(out[s] + gain * x_ref[s, i, rs, :].astype(F32)).astype(BF16) for s in range(shards)]
                    for s in range(shards):
                        out_ref[s, i, rs, :] = out[s]

                    @pl.when(r == 0)
                    def _():
                        for s in range(shards - 1):
                            out_ref[s, i, pl.ds(rows, EDGE), :] = out[s + 1]
                        out_ref[shards - 1, i, pl.ds(rows, EDGE), :] = jnp.zeros((EDGE, chans), BF16)

                over_tiles(rows, work)

    out_block = (shards, 2, rows + EDGE, chans)
    return pl.pallas_call(
        kernel,
        grid=(steps,),
        in_specs=[
            whole(both.shape),
            whole((blocks, rows, chans)),
            per_step((1, 2, rows, 2 * step)),
            whole((1, chans)),
            per_step((1, 2 * rows, rows)),
            per_step((1, 2 * rows, rows)),
        ],
        out_specs=whole(out_block),
        out_shape=jax.ShapeDtypeStruct(out_block, BF16),
        scratch_shapes=[
            pltpu.VMEM((steps, rows, 2 * step), BF16),
            pltpu.VMEM((steps, 4, rows, chans), F32),
        ],
        cost_estimate=pl.CostEstimate(flops=20 * 10**9, transcendentals=0, bytes_accessed=25 * 10**6),
        name="conv_path",
    )(both, taps, spec, skip, fwd, inv)


def plan_lanes(width, chans):
    block = max(chans, LANES)
    while block < 512 and width % (2 * block) == 0:
        block *= 2
    return block


def put(ref, lead, rs, c, value):
    chans = ref.shape[-1]
    width = value.shape[1]
    if chans >= width:
        ref[(c // chans,) + lead + (rs, pl.ds(c % chans, width))] = value
        return
    for i in range(width // chans):
        ref[(c // chans + i,) + lead + (rs, slice(None))] = value[:, i * chans : (i + 1) * chans]


def take(ref, lead, rs, c, width):
    chans = ref.shape[-1]
    if chans >= width:
        return ref[(c // chans,) + lead + (rs, pl.ds(c % chans, width))].astype(F32)
    first = c // chans
    return jnp.concatenate(
        [ref[(first + i,) + lead + (rs, slice(None))].astype(F32) for i in range(width // chans)], axis=1
    )


def pack_taps(long_filter, shards, part, parts):
    rows, width = long_filter.shape
    width = width // parts
    chans = width // shards
    block = plan_lanes(width, chans)
    count = width // block
    groups = block // chans

    def kernel(x_ref, o_ref):
        for c in range(0, block, LANES):
            put(o_ref, (), pl.ds(0, rows), c, x_ref[:, pl.ds(c, LANES)].astype(BF16))

    return pl.pallas_call(
        kernel,
        grid=(count,),
        in_specs=[pl.BlockSpec((rows, block), lambda i: (0, part * count + i))],
        out_specs=pl.BlockSpec((groups, rows, chans), lambda i: (i, 0, 0)),
        out_shape=jax.ShapeDtypeStruct((shards, rows, chans), BF16),
        cost_estimate=pl.CostEstimate(flops=10**6, transcendentals=0, bytes_accessed=6 * 10**6),
        name="pack_taps",
    )(long_filter)


def scale_taps(clip, low, shared, shards):
    live, parts, rows, chans = low.shape
    width = shards * chans
    block = plan_lanes(width, chans)
    while (live * chans) % block:
        block //= 2
    count = width // block
    groups = block // chans
    split = live // groups

    def kernel(*refs):
        c_ref, low_ref = refs[:2]
        o_ref = refs[-1]
        q = pl.program_id(0)
        i = pl.program_id(1)
        gain = c_ref[0, 0]

        @pl.when(i < split)
        def _():
            for c in range(0, block, LANES):
                o_ref[:, pl.ds(c, LANES)] = take(low_ref, (0,), pl.ds(0, rows), c, LANES) * gain

        for part, x_ref in enumerate(refs[2:-1]):

            @pl.when(jnp.logical_and(i >= split, q == part))
            def _():
                for c in range(0, block, LANES):
                    o_ref[:, pl.ds(c, LANES)] = take(x_ref, (), pl.ds(0, rows), c, LANES) * gain

    def shared_map(part):
        def index(q, i):
            upper = jnp.maximum(i, split)
            held = split if part else count - 1
            return (jnp.where(q == part, upper, held), 0, 0)

        return index

    return pl.pallas_call(
        kernel,
        grid=(parts, count),
        in_specs=[
            in_smem(),
            pl.BlockSpec((groups, 1, rows, chans), lambda q, i: (jnp.minimum(i, split - 1), q, 0, 0)),
        ]
        + [pl.BlockSpec((groups, rows, chans), shared_map(p)) for p in range(len(shared))],
        out_specs=pl.BlockSpec((rows, block), lambda q, i: (0, q * count + i)),
        out_shape=jax.ShapeDtypeStruct((rows, parts * width), F32),
        name="scale_taps",
    )(clip, low, *shared)


def short_rows(ext_ref, w_ref, i, cs, r, rows):
    total = w_ref[i, 0:1, cs] * ext_ref[i, pl.ds(HALO + r, rows), :]
    for j in range(1, TAPS):
        total = total + w_ref[i, j : j + 1, cs] * ext_ref[i, pl.ds(HALO + r - j, rows), :]
    return total


def gates(streams, before, grad_out, short_filter, shards, part, parts):
    _, rows, width = streams.shape
    width = width // parts
    chans = width // shards
    block = plan_lanes(width, chans)
    count = width // block
    groups = block // chans
    chunk = math.gcd(rows, 64)

    def kernel(x_ref, b_ref, go_ref, w_ref, o_ref, ext_ref):
        for c in range(0, block, LANES):
            cs = pl.ds(c, LANES)
            for i in range(3):
                ext_ref[i, pl.ds(0, HALO), :] = b_ref[i, :, cs].astype(F32)
                ext_ref[i, pl.ds(HALO, rows), :] = x_ref[i, :, cs].astype(F32)
            for r in range(0, rows, chunk):
                rs = pl.ds(r, chunk)
                gated = short_rows(ext_ref, w_ref, 0, cs, r, chunk) * short_rows(ext_ref, w_ref, 2, cs, r, chunk)
                mix = go_ref[rs, cs].astype(F32) * short_rows(ext_ref, w_ref, 1, cs, r, chunk)
                put(o_ref, (0,), rs, c, gated.astype(BF16))
                put(o_ref, (1,), rs, c, mix.astype(BF16))

    return pl.pallas_call(
        kernel,
        grid=(count,),
        in_specs=[
            pl.BlockSpec((3, rows, block), lambda i: (0, 0, part * count + i)),
            pl.BlockSpec((3, HALO, block), lambda i: (0, 0, part * count + i)),
            pl.BlockSpec((rows, block), lambda i: (0, part * count + i)),
            pl.BlockSpec((3, TAPS, block), lambda i: (0, 0, part * count + i)),
        ],
        out_specs=pl.BlockSpec((groups, 2, rows, chans), lambda i: (i, 0, 0, 0)),
        out_shape=jax.ShapeDtypeStruct((shards, 2, rows, chans), BF16),
        scratch_shapes=[pltpu.VMEM((3, rows + HALO, LANES), F32)],
        cost_estimate=pl.CostEstimate(flops=60 * 10**6, transcendentals=0, bytes_accessed=7 * 10**6),
        name="gates",
    )(streams, before, grad_out, short_filter)


def finish(streams, before, after, grad_out, short_filter, back, earlier, shards, part, parts):
    _, rows, full = streams.shape
    width = full // parts
    chans = width // shards
    block = plan_lanes(width, chans)
    count = width // block
    groups = block // chans
    chunk = math.gcd(rows, 64)

    def kernel(x_ref, b_ref, n_ref, go_ref, w_ref, y_ref, *refs):
        o_ref, gs_ref, st_ref, ext_ref, pre_ref = refs[-5:]
        for c in range(0, block, LANES):
            cs = pl.ds(c, LANES)
            for i in range(3):
                ext_ref[i, pl.ds(0, HALO), :] = b_ref[i, :, cs].astype(F32)
                ext_ref[i, pl.ds(HALO, rows), :] = x_ref[i, :, cs].astype(F32)
                ext_ref[i, pl.ds(HALO + rows, HALO), :] = n_ref[i, :, cs].astype(F32)
            bias = jnp.zeros((8, LANES), F32)
            for r in range(0, rows, chunk):
                rs = pl.ds(r, chunk)
                gout = go_ref[rs, cs].astype(F32)
                mixed = take(y_ref, (0,), rs, c, LANES)
                upper = take(y_ref, (1,), rs, c, LANES)
                x1s = short_rows(ext_ref, w_ref, 0, cs, r, chunk)
                vs = short_rows(ext_ref, w_ref, 2, cs, r, chunk)
                pre_ref[0, rs, :] = upper * vs
                pre_ref[2, rs, :] = upper * x1s
                pre_ref[1, rs, :] = gout * mixed
                gated = (x1s * vs).astype(BF16).astype(F32)
                x2s = short_rows(ext_ref, w_ref, 1, cs, r, chunk)
                o_ref[rs, cs] = (x2s * mixed).astype(BF16)
                term = gated * (gout * x2s).astype(BF16).astype(F32)
                bias = bias + jnp.sum(term.reshape(chunk // 8, 8, LANES), axis=0)
            mixed = take(y_ref, (0,), pl.ds(rows, EDGE), c, LANES)[:HALO]
            upper = take(y_ref, (1,), pl.ds(rows, EDGE), c, LANES)[:HALO]
            pre_ref[0, pl.ds(rows, HALO), :] = upper * short_rows(ext_ref, w_ref, 2, cs, rows, HALO)
            pre_ref[2, pl.ds(rows, HALO), :] = upper * short_rows(ext_ref, w_ref, 0, cs, rows, HALO)
            pre_ref[1, pl.ds(rows, HALO), :] = n_ref[3, :, cs].astype(F32) * mixed
            lines = []
            for i in range(3):
                sums = [jnp.zeros((8, LANES), F32) for _ in range(TAPS)]
                for r in range(0, rows, chunk):
                    rs = pl.ds(r, chunk)
                    own = pre_ref[i, rs, :]
                    total = w_ref[i, 0:1, cs] * own
                    for j in range(TAPS):
                        if j:
                            total = total + w_ref[i, j : j + 1, cs] * pre_ref[i, pl.ds(r + j, chunk), :]
                        term = own * ext_ref[i, pl.ds(HALO + r - j, chunk), :]
                        sums[j] = sums[j] + jnp.sum(term.reshape(chunk // 8, 8, LANES), axis=0)
                    gs_ref[i, rs, cs] = total.astype(BF16)
                lines += [jnp.sum(v, axis=0, keepdims=True) for v in sums]
            lines.append(jnp.sum(bias, axis=0, keepdims=True))
            lines.append(jnp.zeros((SUMS - len(lines), LANES), F32))
            put(st_ref, (0,), pl.ds(0, SUMS), c, jnp.concatenate(lines, axis=0))

    at = lambda i: part * count + i
    ins = [streams, before, after, grad_out, short_filter, back]
    return pl.pallas_call(
        kernel,
        grid=(count,),
        in_specs=[
            pl.BlockSpec((3, rows, block), lambda i: (0, 0, at(i))),
            pl.BlockSpec((3, HALO, block), lambda i: (0, 0, at(i))),
            pl.BlockSpec((4, HALO, block), lambda i: (0, 0, at(i))),
            pl.BlockSpec((rows, block), lambda i: (0, at(i))),
            pl.BlockSpec((3, TAPS, block), lambda i: (0, 0, at(i))),
            pl.BlockSpec((groups, 2, rows + EDGE, chans), lambda i: (i, 0, 0, 0)),
        ]
        + [untouched() for _ in earlier],
        out_specs=[
            pl.BlockSpec((rows, block), lambda i: (0, at(i))),
            pl.BlockSpec((3, rows, block), lambda i: (0, 0, at(i))),
            pl.BlockSpec((groups, 1, SUMS, chans), lambda i: (i, part, 0, 0)),
        ],
        out_shape=[
            jax.ShapeDtypeStruct((rows, full), BF16),
            jax.ShapeDtypeStruct((3, rows, full), BF16),
            jax.ShapeDtypeStruct((shards, parts, SUMS, chans), F32),
        ],
        scratch_shapes=[
            pltpu.VMEM((3, rows + 2 * HALO, LANES), F32),
            pltpu.VMEM((3, rows + HALO, LANES), F32),
        ],
        input_output_aliases={len(ins) + i: i for i in range(len(earlier))},
        cost_estimate=pl.CostEstimate(flops=150 * 10**6, transcendentals=0, bytes_accessed=12 * 10**6),
        name="finish",
    )(*ins, *earlier)


def shift(block, axis, distance):
    devices = range(lax.axis_size(axis))
    route = [(i - distance, i) for i in devices if i - distance in devices]
    return lax.ppermute(block, axis, route)


def exchange(blocks, groups=None):
    return lax.all_to_all(blocks, "seq", split_axis=0, concat_axis=0, axis_index_groups=groups, tiled=True)


def following(value, earlier):
    return lax.optimization_barrier((value, earlier))[0]


def operator(streams, grad_out, long_filter, short_filter, skip_gain):
    shards = lax.axis_size("seq")
    rows = streams.shape[1]
    width = streams.shape[2]
    parts = 2 if width % (2 * shards * LANES) == 0 else 1
    span = width // parts
    chans = span // shards
    tap_rows = long_filter.shape[0]
    live = min(shards, shards * rows // tap_rows)
    fold = 2 * live <= shards
    mine = lax.axis_index("seq")
    is_low = (mine < live).astype(jnp.int32).reshape(1, 1)
    fwd, inv = turn_tables(shards, rows)
    before = shift(streams[:, rows - HALO :], "seq", 1)
    after = shift(jnp.concatenate([streams[:, :HALO], grad_out[None, :HALO]], axis=0), "seq", -1)
    skips = [lax.dynamic_slice_in_dim(skip_gain, p * span + mine * chans, chans)[None] for p in range(parts)]

    both = []
    packed = []
    for p in range(parts):
        sent = gates(streams, before, grad_out, short_filter, shards, p, parts)
        both.append(exchange(sent))
    for p in range(parts):
        packed.append(pack_taps(long_filter, shards, p, parts))
    spec = []
    shared = []
    squares = 0.0
    low = None
    for p in range(parts):
        out = raw_path(both[p], fwd, inv, is_low, packed[p], low, p, parts, tap_rows, live, fold)
        spec.append(out[0])
        low = out[1]
        squares = squares + jnp.sum(out[2])
        shared.append(exchange(out[3] if fold else packed[p]))
    back = []
    for p in range(parts):
        taps = shared[p].reshape(shards * tap_rows // rows, rows, chans)
        sent = conv_path(both[p], taps, spec[p], skips[p], fwd, inv)
        back.append(exchange(sent))
    groups = None
    if fold:
        groups = [list(range(i, i + live)) for i in range(0, shards, live)]
    raw = exchange(following(low, back[-1]), groups)
    done = []
    for p in range(parts):
        done = finish(streams, before, after, grad_out, short_filter, back[p], done, shards, p, parts)
    output, grad_streams, sums = done
    mine_sums = jnp.sum(exchange(following(sums, raw)), axis=0)
    local_sq = squares + jnp.sum(mine_sums * mine_sums)
    line = lax.broadcasted_iota(jnp.int32, mine_sums.shape, 1)
    mine_sums = jnp.where(line == SUMS - 1, local_sq, mine_sums)
    small = exchange(jnp.broadcast_to(mine_sums[None], (shards,) + mine_sums.shape))
    sq_total = lax.psum(jnp.sum(small[:, 0, SUMS - 1, 0]), "chan")
    param_count = LF * D + (3 * TAPS + 1) * D
    clip = 1.0 / jnp.sqrt(sq_total / param_count + 1e-06)
    kept = jnp.where(is_low == 1, clip, 0.0)
    filter_grad = scale_taps(kept, raw, shared if fold else [], shards)
    small = small.transpose(2, 1, 0, 3).reshape(SUMS, width) * clip
    return (
        output,
        grad_streams,
        filter_grad,
        small[: 3 * TAPS].reshape(3, TAPS, width),
        small[3 * TAPS],
    )


def solution(mesh):
    placed = (
        P(None, "seq", "chan"),
        P("seq", "chan"),
        P("seq", "chan"),
        P(None, None, "chan"),
        P("chan"),
    )
    return jax.shard_map(
        operator,
        mesh=mesh,
        in_specs=placed,
        out_specs=(
            P("seq", "chan"),
            P(None, "seq", "chan"),
            P("seq", "chan"),
            P(None, None, "chan"),
            P("chan"),
        ),
        check_vma=False,
    )
```

time: 649 us -> 479 us (0.74)
  waiting for transfers between devices: 324 us -> 165 us
  Pallas kernels: 125 us -> 146 us
  blocking collectives: 97.5 us -> 76.7 us
  between operations: 16.2 us -> 3.46 us
  starting transfers between devices: 57.9 us -> 64.6 us
    psum x1 -> x0, waiting for transfers between devices: 186 us -> none  [body(): short_bias = lax.psum(short_bias, 'seq')]
    psum x1, blocking collectives: 39.4 us -> 3.08 us  [operator(): sq_total = lax.psum(jnp.sum(small[:, 0, SUMS - 1, 0]), 'chan')]
    pallas_call x6 -> x11, Pallas kernels: 125 us -> 146 us  [the longest x2 47.7 us: raw_path(): pl.pallas_call(kernel, grid=(steps,), in_specs=in_specs, out_specs=out_sp...]
    all_to_all x5 -> x7, waiting for transfers between devices: 117 us -> 133 us  [exchange(): lax.all_to_all(blocks, 'seq', split_axis=0, concat_axis=0, axis_index_gro...]
    all_to_all x1 -> x2, blocking collectives: 58.1 us -> 73.6 us  [exchange(): lax.all_to_all(blocks, 'seq', split_axis=0, concat_axis=0, axis_index_gro...]
    ppermute x2, waiting for transfers between devices: 20.9 us -> 32 us  [shift(): return lax.ppermute(block, axis, route)]
    all_to_all x5 -> x7, starting transfers between devices: 51.5 us -> 58.2 us  [exchange(): lax.all_to_all(blocks, 'seq', split_axis=0, concat_axis=0, axis_index_gro...]
  transfers between devices with their start and end apart: 8 -> 9, of which waited for: 7 -> 8; matrix products, arithmetic and copies ran while one was open for 3% -> 3% of each run, Pallas kernels for 15% -> 23%
where the time goes in v2:
time: 479 us; the launch traced here: 476 us
  waiting for transfers between devices  165 us (34%)
  Pallas kernels  146 us (30%)
  blocking collectives  76.7 us (16%)
  starting transfers between devices  64.6 us (13%)
  other arithmetic  12.3 us (3%)
  local copies, waits for them, and re-layouts  7.53 us (2%)
    all_to_all x7, waiting for transfers between devices, exchange(): lax.all_to_all(blocks, 'seq', split_axis=0, concat_axis=0, axis_index_gro...  133 us
    all_to_all x2, blocking collectives, exchange(): lax.all_to_all(blocks, 'seq', split_axis=0, concat_axis=0, axis_index_gro...  73.6 us
    all_to_all x7, starting transfers between devices, exchange(): lax.all_to_all(blocks, 'seq', split_axis=0, concat_axis=0, axis_index_gro...  58.2 us
    pallas_call x2, Pallas kernels, raw_path(): pl.pallas_call(kernel, grid=(steps,), in_specs=in_specs, out_specs=out_sp...  47.7 us
    pallas_call x2, Pallas kernels, conv_path(): pl.pallas_call(kernel, grid=(steps,), in_specs=[whole(both.shape), whole(...  44.5 us
    ppermute x2, waiting for transfers between devices, shift(): return lax.ppermute(block, axis, route)  32 us
    pallas_call x2, Pallas kernels, finish(): pl.pallas_call(kernel, grid=(count,), in_specs=[pl.BlockSpec((3, rows, bl...  25.7 us
    pallas_call x2, Pallas kernels, gates(): pl.pallas_call(kernel, grid=(count,), in_specs=[pl.BlockSpec((3, rows, bl...  12.1 us
  transfers between devices with their start and end apart: 9, of which 8 were waited for; matrix products, arithmetic and copies ran while one was open for 3% of the time, Pallas kernels for 23%

profile of v2, /device:TPU:0, one launch (start us, length us, event | category | flops | bytes accessed | tf_op | source)
XLA Modules:
  0.0 476.5 jit_solution(16847032875642455953)
XLA Ops:
  1.7 4.9 %collective-permute-start = (bf16[3,8,4096]{2,1,0:T(8,128)(2,1)S(1)}, bf16[3,8,4096]{2,1,0:T(8,128)(2,1)S(1)}, u32[]{:S(2)}, u32[]{:S(2)}) collective-permute-start(bf16[3,8,4096]{2,1,0:T(8,128)(2,1)S(1)} %get-tuple-element.38), channel_id=1, source_target_pairs={{0,2},{2,4},{4,6},{6,8},{8,10},{10,12},{12,14},{14,16},{16,18},{18... | collective-permute-start | bytes 589832 | tf_op jit(solution)/shard_map/ppermute | solution.py:666
  6.6 4.1 collective-permute-done.b_ref
  11.4 6.1 %gates.3 = bf16[16,2,256,128]{3,2,1,0:T(8,128)(2,1)} custom-call(bf16[3,256,4096]{2,1,0:T(8,128)(2,1)} %x_ref.11, bf16[3,8,4096]{2,1,0:T(8,128)(2,1)} %copy-done.2, bf16[256,4096]{1,0:T(8,128)(2,1)} %go_ref.7, f32[3,7,4096]{2,1,0:T(8,128)} %w_ref.7), custom_call_target="tpu_custom_call" | custom-call | flops 60000000 | bytes 7000000 | tf_op jit(solution)/shard_map/gates/pallas_call | solution.py:556
  17.4 7.9 %all-to-all-start.1 = ((bf16[16,2,256,128]{3,2,1,0:T(8,128)(2,1)}), bf16[16,2,256,128]{3,2,1,0:T(8,128)(2,1)S(1)}, u32[]{:S(2)}, u32[]{:S(2)}) async-start(bf16[16,2,256,128]{3,2,1,0:T(8,128)(2,1)} %gates.3), calls=%async_computation.1 | async-start | bytes 4194304 | tf_op jit(solution)/shard_map/all_to_all | solution.py:670
  25.3 6.1 %gates.2 = bf16[16,2,256,128]{3,2,1,0:T(8,128)(2,1)} custom-call(bf16[3,256,4096]{2,1,0:T(8,128)(2,1)} %x_ref.11, bf16[3,8,4096]{2,1,0:T(8,128)(2,1)} %copy-done.2, bf16[256,4096]{1,0:T(8,128)(2,1)} %go_ref.7, f32[3,7,4096]{2,1,0:T(8,128)} %w_ref.7), custom_call_target="tpu_custom_call" | custom-call | flops 60000000 | bytes 7000000 | tf_op jit(solution)/shard_map/gates/pallas_call | solution.py:556
  31.4 36.4 %all-to-all-done.1.refs_0_.x_ref = bf16[16,2,256,128]{3,2,1,0:T(8,128)(2,1)S(1)} async-done(((bf16[16,2,256,128]{3,2,1,0:T(8,128)(2,1)}), bf16[16,2,256,128]{3,2,1,0:T(8,128)(2,1)S(1)}, u32[]{:S(2)}, u32[]{:S(2)}) %all-to-all-start.1) | async-done | bytes 2097184 | tf_op jit(solution)/shard_map/all_to_all | solution.py:670
  67.7 9.9 %all-to-all-start = ((bf16[16,2,256,128]{3,2,1,0:T(8,128)(2,1)}), bf16[16,2,256,128]{3,2,1,0:T(8,128)(2,1)}, u32[]{:S(2)}, u32[]{:S(2)}) async-start(bf16[16,2,256,128]{3,2,1,0:T(8,128)(2,1)} %gates.2), calls=%async_computation | async-start | bytes 4194304 | tf_op jit(solution)/shard_map/all_to_all | solution.py:670
  77.6 4.3 pack_taps.3.refs_4_
  81.9 4.3 pack_taps.2.refs_4_
  87.4 2.8 multiply_subtract_fusion
  90.2 2.4 pad_maximum_fusion.refs_1_.fwd_ref
  92.6 3.3 fusion.refs_2_.inv_ref
  95.9 23.8 %raw_path.2 = (f32[17,2,256,256]{3,2,1,0:T(8,128)}, bf16[8,2,512,128]{3,2,1,0:T(8,128)(2,1)}, f32[8,128]{1,0:T(8,128)}, bf16[16,512,128]{2,1,0:T(8,128)(2,1)}) custom-call(bf16[16,2,256,128]{3,2,1,0:T(8,128)(2,1)} %copy-done.3, bf16[17,512,256]{2,1,0:T(8,128)(2,1)} %pad_maximum_fusion.refs_1_.fwd_ref, bf16[17,512,256]{2,1,0:T(8,128)(2,1)} %fusion.refs_2_.inv_ref, ...), custom_call_target="tpu_custom_call" | custom-call | flops 20000000000 | bytes 25000000 | tf_op jit(solution)/shard_map/raw_path/pallas_call | solution.py:335
  120.2 23.8 %raw_path.3 = (f32[17,2,256,256]{3,2,1,0:T(8,128)}, bf16[8,2,512,128]{3,2,1,0:T(8,128)(2,1)}, f32[8,128]{1,0:T(8,128)}, bf16[16,512,128]{2,1,0:T(8,128)(2,1)}) custom-call(bf16[16,2,256,128]{3,2,1,0:T(8,128)(2,1)} %all-to-all-done.refs_0_.x_ref, bf16[17,512,256]{2,1,0:T(8,128)(2,1)} %pad_maximum_fusion.refs_1_.fwd_ref, ...), custom_call_target="tpu_custom_call", output_to_operand_aliasing={{1}: (5, {})} | custom-call | flops 20000000000 | bytes 25000000 | tf_op jit(solution)/shard_map/raw_path/pallas_call | solution.py:335
  144.1 58.1 %all_to_all.45.refs_3_ = bf16[16,512,128]{2,1,0:T(8,128)(2,1)} all-to-all(bf16[16,512,128]{2,1,0:T(8,128)(2,1)} %get-tuple-element.22), channel_id=1, replica_groups=mesh['seq'=16,'chan'=2] {'seq'}, dimensions={0} | all-to-all | bytes 4194304 | tf_op jit(solution)/shard_map/all_to_all | solution.py:670
  202.2 4.0 all-to-all-start.4
  207.5 22.2 %conv_path.2 = bf16[16,2,272,128]{3,2,1,0:T(8,128)(2,1)} custom-call(bf16[16,2,256,128]{3,2,1,0:T(8,128)(2,1)} %all-to-all-done.refs_0_.x_ref, bf16[32,256,128]{2,1,0:T(8,128)(2,1)} %bitcast.15, f32[17,2,256,256]{3,2,1,0:T(8,128)} %get-tuple-element.23.spec_ref, f32[1,128]{1,0:T(1,128)} %get-tuple-element.44.skip_ref, ...), custom_call_target="tpu_custom_call" | custom-call | flops 20000000000 | bytes 25000000 | tf_op jit(solution)/shard_map/conv_path/pallas_call | solution.py:404
  229.7 18.9 %all-to-all-done.4.refs_2_ = bf16[16,512,128]{2,1,0:T(8,128)(2,1)S(1)} async-done(((bf16[16,512,128]{2,1,0:T(8,128)(2,1)}), bf16[16,512,128]{2,1,0:T(8,128)(2,1)S(1)}, u32[]{:S(2)}, u32[]{:S(2)}) %all-to-all-start.4) | async-done | bytes 2097184 | tf_op jit(solution)/shard_map/all_to_all | solution.py:670
  250.0 9.8 %all-to-all-start.3 = ((bf16[16,2,272,128]{3,2,1,0:T(8,128)(2,1)}), bf16[16,2,272,128]{3,2,1,0:T(8,128)(2,1)S(1)}, u32[]{:S(2)}, u32[]{:S(2)}) async-start(bf16[16,2,272,128]{3,2,1,0:T(8,128)(2,1)} %conv_path.2), calls=%async_computation.3 | async-start | bytes 4456448 | tf_op jit(solution)/shard_map/all_to_all | solution.py:670
  259.9 22.3 %conv_path.3 = bf16[16,2,272,128]{3,2,1,0:T(8,128)(2,1)} custom-call(bf16[16,2,256,128]{3,2,1,0:T(8,128)(2,1)} %copy-done.3, bf16[32,256,128]{2,1,0:T(8,128)(2,1)} %bitcast.16, f32[17,2,256,256]{3,2,1,0:T(8,128)} %get-tuple-element.25.spec_ref, f32[1,128]{1,0:T(1,128)} %get-tuple-element.43.skip_ref, bf16[17,512,256]{2,1,0:T(8,128)(2,1)} %pad_maximum_fusion.refs_1_.fwd_ref, ...), custom_call_target="tpu_custom_call" | custom-call | flops 20000000000 | bytes 25000000 | tf_op jit(solution)/shard_map/conv_path/pallas_call | solution.py:404
  282.1 22.5 %all-to-all-done.3.y_ref = bf16[16,2,272,128]{3,2,1,0:T(8,128)(2,1)S(1)} async-done(((bf16[16,2,272,128]{3,2,1,0:T(8,128)(2,1)}), bf16[16,2,272,128]{3,2,1,0:T(8,128)(2,1)S(1)}, u32[]{:S(2)}, u32[]{:S(2)}) %all-to-all-start.3) | async-done | bytes 2228256 | tf_op jit(solution)/shard_map/all_to_all | solution.py:670
  304.7 10.4 %all-to-all-start.5 = ((bf16[16,2,272,128]{3,2,1,0:T(8,128)(2,1)}), bf16[16,2,272,128]{3,2,1,0:T(8,128)(2,1)}, u32[]{:S(2)}, u32[]{:S(2)}) async-start(bf16[16,2,272,128]{3,2,1,0:T(8,128)(2,1)} %conv_path.3), calls=%async_computation.5 | async-start | bytes 4456448 | tf_op jit(solution)/shard_map/all_to_all | solution.py:670
  315.0 44.9 %all-to-all-done.5.y_ref = bf16[16,2,272,128]{3,2,1,0:T(8,128)(2,1)} async-done(((bf16[16,2,272,128]{3,2,1,0:T(8,128)(2,1)}), bf16[16,2,272,128]{3,2,1,0:T(8,128)(2,1)}, u32[]{:S(2)}, u32[]{:S(2)}) %all-to-all-start.5) | async-done | bytes 2228256 | tf_op jit(solution)/shard_map/all_to_all | solution.py:670
  359.9 10.2 %all-to-all-start.6 = ((bf16[8,2,512,128]{3,2,1,0:T(8,128)(2,1)}), bf16[8,2,512,128]{3,2,1,0:T(8,128)(2,1)}, u32[]{:S(2)}, u32[]{:S(2)}) async-start(bf16[8,2,512,128]{3,2,1,0:T(8,128)(2,1)} %get-tuple-element.35), calls=%async_computation.6 | async-start | bytes 4194304 | tf_op jit(solution)/shard_map/all_to_all | solution.py:670
  372.5 27.9 %collective-permute-done.1.n_ref = bf16[4,8,4096]{2,1,0:T(8,128)(2,1)S(1)} collective-permute-done((bf16[4,8,4096]{2,1,0:T(8,128)(2,1)S(1)}, bf16[4,8,4096]{2,1,0:T(8,128)(2,1)S(1)}, u32[]{:S(2)}, u32[]{:S(2)}) %collective-permute-start.1) | collective-permute-done | bytes 262176 | tf_op jit(solution)/shard_map/ppermute | solution.py:666
  401.0 12.8 %finish.2 = (bf16[256,4096]{1,0:T(8,128)(2,1)}, bf16[3,256,4096]{2,1,0:T(8,128)(2,1)}, f32[16,2,24,128]{3,2,1,0:T(8,128)}) custom-call(bf16[3,256,4096]{2,1,0:T(8,128)(2,1)} %x_ref.11, bf16[3,8,4096]{2,1,0:T(8,128)(2,1)} %copy-done.2, bf16[4,8,4096]{2,1,0:T(8,128)(2,1)} %copy-done.4, bf16[256,4096]{1,0:T(8,128)(2,1)} %go_ref.7, f32[3,7,4096]{2,1,0:T(8,128)} %w_ref.7, ...), custom_call_target="tpu_custom_call" | custom-call | flops 150000000 | bytes 12000000 | tf_op jit(solution)/shard_map/finish/pallas_call | solution.py:631
  413.9 12.9 %finish.3 = (bf16[256,4096]{1,0:T(8,128)(2,1)}, bf16[3,256,4096]{2,1,0:T(8,128)(2,1)}, f32[16,2,24,128]{3,2,1,0:T(8,128)}) custom-call(bf16[3,256,4096]{2,1,0:T(8,128)(2,1)} %x_ref.11, bf16[3,8,4096]{2,1,0:T(8,128)(2,1)} %copy-done.2, bf16[4,8,4096]{2,1,0:T(8,128)(2,1)} %copy-done.4, ...), custom_call_target="tpu_custom_call", output_to_operand_aliasing={{0}: (6, {}), {1}: (7, {}), {2}: (8, {})} | custom-call | flops 150000000 | bytes 12000000 | tf_op jit(solution)/shard_map/finish/pallas_call | solution.py:631
  426.7 6.2 %all-to-all-start.7 = ((f32[16,2,24,128]{3,2,1,0:T(8,128)}), f32[16,2,24,128]{3,2,1,0:T(8,128)S(1)}, u32[]{:S(2)}, u32[]{:S(2)}) async-start(f32[16,2,24,128]{3,2,1,0:T(8,128)} %get-tuple-element.36), calls=%async_computation.7 | async-start | bytes 786432 | tf_op jit(solution)/shard_map/all_to_all | solution.py:670
  435.4 10.2 %all-to-all-done.7 = f32[16,2,24,128]{3,2,1,0:T(8,128)S(1)} async-done(((f32[16,2,24,128]{3,2,1,0:T(8,128)}), f32[16,2,24,128]{3,2,1,0:T(8,128)S(1)}, u32[]{:S(2)}, u32[]{:S(2)}) %all-to-all-start.7) | async-done | bytes 393248 | tf_op jit(solution)/shard_map/all_to_all | solution.py:670
  447.2 15.5 %all_to_all.46 = f32[16,2,24,128]{3,1,2,0:T(2,128)S(1)} all-to-all(f32[16,2,24,128]{3,1,2,0:T(2,128)S(1)} %broadcast_in_dim.20), channel_id=1, replica_groups=mesh['seq'=16,'chan'=2] {'seq'}, dimensions={0} | all-to-all | bytes 786432 | tf_op jit(solution)/shard_map/all_to_all | solution.py:670
  463.3 3.1 psum.7
  468.6 7.9 %scale_taps.1 = f32[512,4096]{1,0:T(8,128)} custom-call(f32[1,1]{1,0:T(1,128)S(6)} %select_n.69.refs_0_, bf16[8,2,512,128]{3,2,1,0:T(8,128)(2,1)} %all-to-all-done.6.refs_1_, bf16[16,512,128]{2,1,0:T(8,128)(2,1)} %copy-done.1, bf16[16,512,128]{2,1,0:T(8,128)(2,1)} %all_to_all.45.refs_3_), custom_call_target="tpu_custom_call" | custom-call | tf_op jit(solution)/shard_map/scale_taps/pallas_call | solution.py:513
  (36 shorter events, 13.4 us)
Async XLA Ops:
  1.7 9.0 %collective-permute-start = (bf16[3,8,4096]{2,1,0:T(8,128)(2,1)S(1)}, bf16[3,8,4096]{2,1,0:T(8,128)(2,1)S(1)}, u32[]{:S(2)}, u32[]{:S(2)}) collective-permute-start(bf16[3,8,4096]{2,1,0:T(8,128)(2,1)S(1)} %get-tuple-element.38), channel_id=1, source_target_pairs={{0,2},{2,4},{4,6},{6,8},{8,10},{10,12},{12,14},{14,16},{16,18},{18... | collective-permute-start | bytes 589832 | tf_op jit(solution)/shard_map/ppermute | solution.py:666
  10.7 0.7 copy-start.2
  17.4 50.3 %all-to-all-start.1 = ((bf16[16,2,256,128]{3,2,1,0:T(8,128)(2,1)}), bf16[16,2,256,128]{3,2,1,0:T(8,128)(2,1)S(1)}, u32[]{:S(2)}, u32[]{:S(2)}) async-start(bf16[16,2,256,128]{3,2,1,0:T(8,128)(2,1)} %gates.3), calls=%async_computation.1 | async-start | bytes 4194304 | tf_op jit(solution)/shard_map/all_to_all | solution.py:670
  67.7 14.2 %copy-start.3 = (bf16[16,2,256,128]{3,2,1,0:T(8,128)(2,1)}, bf16[16,2,256,128]{3,2,1,0:T(8,128)(2,1)S(1)}, u32[]{:S(2)}) copy-start(bf16[16,2,256,128]{3,2,1,0:T(8,128)(2,1)S(1)} %all-to-all-done.1.refs_0_.x_ref) | copy-start | bytes 6291460
  67.7 52.5 %all-to-all-start = ((bf16[16,2,256,128]{3,2,1,0:T(8,128)(2,1)}), bf16[16,2,256,128]{3,2,1,0:T(8,128)(2,1)}, u32[]{:S(2)}, u32[]{:S(2)}) async-start(bf16[16,2,256,128]{3,2,1,0:T(8,128)(2,1)} %gates.2), calls=%async_computation | async-start | bytes 4194304 | tf_op jit(solution)/shard_map/all_to_all | solution.py:670
  202.2 46.4 %all-to-all-start.4 = ((bf16[16,512,128]{2,1,0:T(8,128)(2,1)}), bf16[16,512,128]{2,1,0:T(8,128)(2,1)S(1)}, u32[]{:S(2)}, u32[]{:S(2)}) async-start(bf16[16,512,128]{2,1,0:T(8,128)(2,1)} %get-tuple-element.24), calls=%async_computation.4 | async-start | bytes 4194304 | tf_op jit(solution)/shard_map/all_to_all | solution.py:670
  248.6 1.4 copy-start.1
  250.0 54.6 %all-to-all-start.3 = ((bf16[16,2,272,128]{3,2,1,0:T(8,128)(2,1)}), bf16[16,2,272,128]{3,2,1,0:T(8,128)(2,1)S(1)}, u32[]{:S(2)}, u32[]{:S(2)}) async-start(bf16[16,2,272,128]{3,2,1,0:T(8,128)(2,1)} %conv_path.2), calls=%async_computation.3 | async-start | bytes 4456448 | tf_op jit(solution)/shard_map/all_to_all | solution.py:670
  304.7 66.3 %copy-start = (bf16[16,2,272,128]{3,2,1,0:T(8,128)(2,1)}, bf16[16,2,272,128]{3,2,1,0:T(8,128)(2,1)S(1)}, u32[]{:S(2)}) copy-start(bf16[16,2,272,128]{3,2,1,0:T(8,128)(2,1)S(1)} %all-to-all-done.3.y_ref) | copy-start | bytes 6684676
  304.7 55.2 %all-to-all-start.5 = ((bf16[16,2,272,128]{3,2,1,0:T(8,128)(2,1)}), bf16[16,2,272,128]{3,2,1,0:T(8,128)(2,1)}, u32[]{:S(2)}, u32[]{:S(2)}) async-start(bf16[16,2,272,128]{3,2,1,0:T(8,128)(2,1)} %conv_path.3), calls=%async_computation.5 | async-start | bytes 4456448 | tf_op jit(solution)/shard_map/all_to_all | solution.py:670
  359.9 66.8 %all-to-all-start.6 = ((bf16[8,2,512,128]{3,2,1,0:T(8,128)(2,1)}), bf16[8,2,512,128]{3,2,1,0:T(8,128)(2,1)}, u32[]{:S(2)}, u32[]{:S(2)}) async-start(bf16[8,2,512,128]{3,2,1,0:T(8,128)(2,1)} %get-tuple-element.35), calls=%async_computation.6 | async-start | bytes 4194304 | tf_op jit(solution)/shard_map/all_to_all | solution.py:670
  371.0 29.3 %collective-permute-start.1 = (bf16[4,8,4096]{2,1,0:T(8,128)(2,1)S(1)}, bf16[4,8,4096]{2,1,0:T(8,128)(2,1)S(1)}, u32[]{:S(2)}, u32[]{:S(2)}) collective-permute-start(bf16[4,8,4096]{2,1,0:T(8,128)(2,1)S(1)} %pad_maximum_fusion.1), channel_id=1, source_target_pairs={{2,0},{4,2},{6,4},{8,6},{10,8},{12,10},{14,12},{16,14},{18,16},{20... | collective-permute-start | bytes 786440 | tf_op jit(solution)/shard_map/ppermute | solution.py:666
  400.3 0.7 copy-start.4
  413.8 19.1 %copy-start.5 = (f32[8,128]{1,0:T(8,128)S(1)}, f32[8,128]{1,0:T(8,128)}, u32[]{:S(2)}) copy-start(f32[8,128]{1,0:T(8,128)} %get-tuple-element.31) | copy-start | bytes 12292
  413.8 19.7 %copy-start.6 = (f32[8,128]{1,0:T(8,128)S(1)}, f32[8,128]{1,0:T(8,128)}, u32[]{:S(2)}) copy-start(f32[8,128]{1,0:T(8,128)} %get-tuple-element.32) | copy-start | bytes 12292
  426.7 18.9 %all-to-all-start.7 = ((f32[16,2,24,128]{3,2,1,0:T(8,128)}), f32[16,2,24,128]{3,2,1,0:T(8,128)S(1)}, u32[]{:S(2)}, u32[]{:S(2)}) async-start(f32[16,2,24,128]{3,2,1,0:T(8,128)} %get-tuple-element.36), calls=%async_computation.7 | async-start | bytes 786432 | tf_op jit(solution)/shard_map/all_to_all | solution.py:670

commit v3 on v2

--- a/solution.py
+++ b/solution.py
@@ -7,11 +7,12 @@
 from jax.experimental.pallas import tpu as pltpu
 from jax.sharding import PartitionSpec as P
 
+
 D = 8192
 LF = 8192
 TAPS = 7
 HALO = 8
-EDGE = 16
+EDGE = 8
 LANES = 128
 SUMS = 24
 F32 = jnp.float32
@@ -225,11 +226,15 @@
     return pl.BlockSpec(memory_space=pltpu.SMEM)
 
 
+def resident():
+    return pl.BlockSpec(memory_space=pltpu.VMEM)
+
+
 def untouched():
     return pl.BlockSpec(memory_space=pl.ANY)
 
 
-def raw_path(both, fwd, inv, is_low, packed, low_before, part, parts, tap_rows, live, fold):
+def raw_path(both, fwd, inv, where, packed, low_before, part, parts, tap_rows, live, fold):
     shards, _, rows, chans = both.shape
     steps = shards + 1
     step = max(chans, LANES)
@@ -251,6 +256,7 @@
             send_ref = refs.pop(0)
         a_ref, y_ref = refs
         k = pl.program_id(0)
+        mine = flag_ref[0, 1] if fold else 0
 
         @pl.when(k == 0)
         def _():
@@ -285,7 +291,8 @@
                 out = real_idft(load_spec(lambda at: (y_ref[at, 0, rs, :], y_ref[at, 1, rs, :]), shards), shards)
                 square = None
                 for s in range(blocks):
-                    low_ref[s // per_shard, 0, pl.ds((s % per_shard) * rows + r, 16), :] = out[s].astype(BF16)
+                    at = (s // per_shard) ^ mine
+                    low_ref[at, 0, pl.ds((s % per_shard) * rows + r, 16), :] = out[s].astype(BF16)
                     square = add(square, out[s] * out[s])
                 sq_ref[...] += square[:8] + square[8:]
 
@@ -301,18 +308,18 @@
                 def _():
                     for s in range(shards):
                         if s < live:
-                            send_ref[s] = low_ref[s, 0]
+                            send_ref[s] = low_ref[s ^ mine, 0]
                         else:
                             send_ref[s] = jnp.zeros((tap_rows, chans), BF16)
 
     ins = [both, fwd, inv]
     in_specs = [
-        whole(both.shape),
+        resident(),
         per_step((1, 2 * rows, rows)),
         per_step((1, 2 * rows, rows)),
     ]
     if fold:
-        ins += [is_low, packed]
+        ins += [where, packed]
         in_specs += [in_smem(), whole(packed.shape)]
     aliases = {}
     if part:
@@ -395,7 +402,7 @@
                     @pl.when(r == 0)
                     def _():
                         for s in range(shards - 1):
-                            out_ref[s, i, pl.ds(rows, EDGE), :] = out[s + 1]
+                            out_ref[s, i, pl.ds(rows, EDGE), :] = out[s + 1][:EDGE]
                         out_ref[shards - 1, i, pl.ds(rows, EDGE), :] = jnp.zeros((EDGE, chans), BF16)
 
                 over_tiles(rows, work)
@@ -405,8 +412,8 @@
         kernel,
         grid=(steps,),
         in_specs=[
-            whole(both.shape),
-            whole((blocks, rows, chans)),
+            resident(),
+            resident(),
             per_step((1, 2, rows, 2 * step)),
             whole((1, chans)),
             per_step((1, 2 * rows, rows)),
@@ -473,8 +480,8 @@
     )(long_filter)
 
 
-def scale_taps(clip, low, shared, shards):
-    live, parts, rows, chans = low.shape
+def scale_taps(clip, where, lows, shared, shards, live):
+    parts, rows, chans = lows[0].shape[-3:]
     width = shards * chans
     block = plan_lanes(width, chans)
     while (live * chans) % block:
@@ -482,9 +489,11 @@
     count = width // block
     groups = block // chans
     split = live // groups
+    listed = len(lows) > 1
 
     def kernel(*refs):
-        c_ref, low_ref = refs[:2]
+        c_ref, at_ref = refs[:2]
+        low_refs = refs[2 : 2 + len(lows)]
         o_ref = refs[-1]
         q = pl.program_id(0)
         i = pl.program_id(1)
@@ -492,13 +501,22 @@
 
         @pl.when(i < split)
         def _():
-            for c in range(0, block, LANES):
-                o_ref[:, pl.ds(c, LANES)] = take(low_ref, (0,), pl.ds(0, rows), c, LANES) * gain
-
-        for part, x_ref in enumerate(refs[2:-1]):
+            if not listed:
+                for c in range(0, block, LANES):
+                    o_ref[:, pl.ds(c, LANES)] = take(low_refs[0], (0,), pl.ds(0, rows), c, LANES) * gain
+                return
+            for j in range(groups):
+                source = (i * groups + j) ^ at_ref[0, 1]
+                for d, x_ref in enumerate(low_refs):
+
+                    @pl.when(source == d)
+                    def _(j=j, x_ref=x_ref):
+                        o_ref[:, pl.ds(j * chans, chans)] = x_ref[q].astype(F32) * gain
+
+        for part, x_ref in enumerate(refs[2 + len(lows) : -1]):
 
             @pl.when(jnp.logical_and(i >= split, q == part))
-            def _():
+            def _(x_ref=x_ref):
                 for c in range(0, block, LANES):
                     o_ref[:, pl.ds(c, LANES)] = take(x_ref, (), pl.ds(0, rows), c, LANES) * gain
 
@@ -510,18 +528,20 @@
 
         return index
 
+    if listed:
+        low_specs = [whole((parts, rows, chans)) for _ in lows]
+    else:
+        low_specs = [pl.BlockSpec((groups, 1, rows, chans), lambda q, i: (jnp.minimum(i, split - 1), q, 0, 0))]
     return pl.pallas_call(
         kernel,
         grid=(parts, count),
-        in_specs=[
-            in_smem(),
-            pl.BlockSpec((groups, 1, rows, chans), lambda q, i: (jnp.minimum(i, split - 1), q, 0, 0)),
-        ]
+        in_specs=[in_smem(), in_smem()]
+        + low_specs
         + [pl.BlockSpec((groups, rows, chans), shared_map(p)) for p in range(len(shared))],
         out_specs=pl.BlockSpec((rows, block), lambda q, i: (0, q * count + i)),
         out_shape=jax.ShapeDtypeStruct((rows, parts * width), F32),
         name="scale_taps",
-    )(clip, low, *shared)
+    )(clip, where, *lows, *shared)
 
 
 def short_rows(ext_ref, w_ref, i, cs, r, rows):
@@ -685,7 +705,8 @@
     live = min(shards, shards * rows // tap_rows)
     fold = 2 * live <= shards
     mine = lax.axis_index("seq")
-    is_low = (mine < live).astype(jnp.int32).reshape(1, 1)
+    is_low = mine < live
+    where = jnp.stack([is_low.astype(jnp.int32), mine % live]).reshape(1, 2)
     fwd, inv = turn_tables(shards, rows)
     before = shift(streams[:, rows - HALO :], "seq", 1)
     after = shift(jnp.concatenate([streams[:, :HALO], grad_out[None, :HALO]], axis=0), "seq", -1)
@@ -703,7 +724,7 @@
     squares = 0.0
     low = None
     for p in range(parts):
-        out = raw_path(both[p], fwd, inv, is_low, packed[p], low, p, parts, tap_rows, live, fold)
+        out = raw_path(both[p], fwd, inv, where, packed[p], low, p, parts, tap_rows, live, fold)
         spec.append(out[0])
         low = out[1]
         squares = squares + jnp.sum(out[2])
@@ -713,24 +734,31 @@
         taps = shared[p].reshape(shards * tap_rows // rows, rows, chans)
         sent = conv_path(both[p], taps, spec[p], skips[p], fwd, inv)
         back.append(exchange(sent))
-    groups = None
-    if fold:
-        groups = [list(range(i, i + live)) for i in range(0, shards, live)]
-    raw = exchange(following(low, back[-1]), groups)
     done = []
+    lows = []
     for p in range(parts):
         done = finish(streams, before, after, grad_out, short_filter, back[p], done, shards, p, parts)
+        if p == 0 and fold:
+            ready = following(low, done[2])
+            lows.append(ready[0])
+            for d in range(1, live):
+                lows.append(lax.ppermute(ready[d], "seq", [(i, i ^ d) for i in range(live)]))
     output, grad_streams, sums = done
-    mine_sums = jnp.sum(exchange(following(sums, raw)), axis=0)
+    if not fold:
+        lows.append(exchange(following(low, back[-1])))
+        sums = following(sums, lows[0])
+    mine_sums = jnp.sum(exchange(sums), axis=0)
     local_sq = squares + jnp.sum(mine_sums * mine_sums)
+    upper_sq = lax.reduce_precision(local_sq, 8, 7)
     line = lax.broadcasted_iota(jnp.int32, mine_sums.shape, 1)
-    mine_sums = jnp.where(line == SUMS - 1, local_sq, mine_sums)
-    small = exchange(jnp.broadcast_to(mine_sums[None], (shards,) + mine_sums.shape))
-    sq_total = lax.psum(jnp.sum(small[:, 0, SUMS - 1, 0]), "chan")
+    mine_sums = jnp.where(line == SUMS - 2, upper_sq, mine_sums)
+    mine_sums = jnp.where(line == SUMS - 1, local_sq - upper_sq, mine_sums).astype(BF16)
+    small = exchange(jnp.broadcast_to(mine_sums[None], (shards,) + mine_sums.shape)).astype(F32)
+    sq_total = lax.psum(jnp.sum(small[:, 0, SUMS - 2 :, 0]), "chan")
     param_count = LF * D + (3 * TAPS + 1) * D
     clip = 1.0 / jnp.sqrt(sq_total / param_count + 1e-06)
-    kept = jnp.where(is_low == 1, clip, 0.0)
-    filter_grad = scale_taps(kept, raw, shared if fold else [], shards)
+    kept = jnp.where(is_low, clip, 0.0).reshape(1, 1)
+    filter_grad = scale_taps(kept, where, lows, shared if fold else [], shards, live)
     small = small.transpose(2, 1, 0, 3).reshape(SUMS, width) * clip
     return (
         output,

time: 479 us -> 446 us (0.931)
  blocking collectives: 76.7 us -> 3.08 us
  starting transfers between devices: 64.6 us -> 120 us
  waiting for transfers between devices: 165 us -> 137 us
  local copies, waits for them, and re-layouts: 7.53 us -> 17.2 us
    all_to_all x2 -> x0, blocking collectives: 73.6 us -> none  [exchange(): lax.all_to_all(blocks, 'seq', split_axis=0, concat_axis=0, axis_index_gro...]
    all_to_all x7 -> x8, starting transfers between devices: 58.2 us -> 90.7 us  [exchange(): lax.all_to_all(blocks, 'seq', split_axis=0, concat_axis=0, axis_index_gro...]
    ppermute x0 -> x7, starting transfers between devices: none -> 22.7 us  [operator(): lax.ppermute(ready[d], 'seq', [(i, i ^ d) for i in range(live)])]
    ppermute x2, waiting for transfers between devices: 32 us -> 14.8 us  [shift(): return lax.ppermute(block, axis, route)]
    all_to_all x7 -> x8, waiting for transfers between devices: 133 us -> 119 us  [exchange(): lax.all_to_all(blocks, 'seq', split_axis=0, concat_axis=0, axis_index_gro...]
    unnamed x14 -> x33, local copies, waits for them, and re-layouts: 2.79 us -> 9.28 us
  transfers between devices with their start and end apart: 9 -> 17, of which waited for: 8 -> 11; matrix products, arithmetic and copies ran while one was open for 3% -> 5% of each run, Pallas kernels for 23% -> 27%
where the time goes in v3:
time: 446 us; the launch traced here: 443 us
  Pallas kernels  148 us (33%)
  waiting for transfers between devices  137 us (31%)
  starting transfers between devices  120 us (27%)
  local copies, waits for them, and re-layouts  17.2 us (4%)
  other arithmetic  13.6 us (3%)
  between operations  4.78 us (1%)
    all_to_all x8, waiting for transfers between devices, exchange(): lax.all_to_all(blocks, 'seq', split_axis=0, concat_axis=0, axis_index_gro...  119 us
    all_to_all x8, starting transfers between devices, exchange(): lax.all_to_all(blocks, 'seq', split_axis=0, concat_axis=0, axis_index_gro...  90.7 us
    pallas_call x2, Pallas kernels, raw_path(): pl.pallas_call(kernel, grid=(steps,), in_specs=in_specs, out_specs=out_sp...  47.8 us
    pallas_call x2, Pallas kernels, conv_path(): pl.pallas_call(kernel, grid=(steps,), in_specs=[resident(), resident(), p...  45.3 us
    pallas_call x2, Pallas kernels, finish(): pl.pallas_call(kernel, grid=(count,), in_specs=[pl.BlockSpec((3, rows, bl...  25.7 us
    ppermute x7, starting transfers between devices, operator(): lax.ppermute(ready[d], 'seq', [(i, i ^ d) for i in range(live)])  22.7 us
    ppermute x2, waiting for transfers between devices, shift(): return lax.ppermute(block, axis, route)  14.8 us
    pallas_call x2, Pallas kernels, gates(): pl.pallas_call(kernel, grid=(count,), in_specs=[pl.BlockSpec((3, rows, bl...  12.1 us
  transfers between devices with their start and end apart: 17, of which 11 were waited for; matrix products, arithmetic and copies ran while one was open for 5% of the time, Pallas kernels for 27%

profile of v3, /device:TPU:0, one launch (start us, length us, event | category | flops | bytes accessed | tf_op | source)
XLA Modules:
  0.0 443.0 jit_solution(14531398952684267380)
XLA Ops:
  1.7 4.9 %collective-permute-start = (bf16[3,8,4096]{2,1,0:T(8,128)(2,1)S(1)}, bf16[3,8,4096]{2,1,0:T(8,128)(2,1)S(1)}, u32[]{:S(2)}, u32[]{:S(2)}) collective-permute-start(bf16[3,8,4096]{2,1,0:T(8,128)(2,1)S(1)} %get-tuple-element.36), channel_id=1, source_target_pairs={{0,2},{2,4},{4,6},{6,8},{8,10},{10,12},{12,14},{14,16},{16,18},{18... | collective-permute-start | bytes 589832 | tf_op jit(solution)/shard_map/ppermute | solution.py:686
  6.6 4.1 collective-permute-done.b_ref
  11.4 6.1 %gates.3 = bf16[16,2,256,128]{3,2,1,0:T(8,128)(2,1)} custom-call(bf16[3,256,4096]{2,1,0:T(8,128)(2,1)} %x_ref.11, bf16[3,8,4096]{2,1,0:T(8,128)(2,1)} %copy-done.3, bf16[256,4096]{1,0:T(8,128)(2,1)} %go_ref.7, f32[3,7,4096]{2,1,0:T(8,128)} %w_ref.7), custom_call_target="tpu_custom_call" | custom-call | flops 60000000 | bytes 7000000 | tf_op jit(solution)/shard_map/gates/pallas_call | solution.py:576
  17.4 7.9 %all-to-all-start.1 = ((bf16[16,2,256,128]{3,2,1,0:T(8,128)(2,1)}), bf16[16,2,256,128]{3,2,1,0:T(8,128)(2,1)S(1)}, u32[]{:S(2)}, u32[]{:S(2)}) async-start(bf16[16,2,256,128]{3,2,1,0:T(8,128)(2,1)} %gates.3), calls=%async_computation.1 | async-start | bytes 4194304 | tf_op jit(solution)/shard_map/all_to_all | solution.py:690
  25.3 6.1 %gates.2 = bf16[16,2,256,128]{3,2,1,0:T(8,128)(2,1)} custom-call(bf16[3,256,4096]{2,1,0:T(8,128)(2,1)} %x_ref.11, bf16[3,8,4096]{2,1,0:T(8,128)(2,1)} %copy-done.3, bf16[256,4096]{1,0:T(8,128)(2,1)} %go_ref.7, f32[3,7,4096]{2,1,0:T(8,128)} %w_ref.7), custom_call_target="tpu_custom_call" | custom-call | flops 60000000 | bytes 7000000 | tf_op jit(solution)/shard_map/gates/pallas_call | solution.py:576
  31.4 36.4 %all-to-all-done.1.refs_0_.x_ref = bf16[16,2,256,128]{3,2,1,0:T(8,128)(2,1)S(1)} async-done(((bf16[16,2,256,128]{3,2,1,0:T(8,128)(2,1)}), bf16[16,2,256,128]{3,2,1,0:T(8,128)(2,1)S(1)}, u32[]{:S(2)}, u32[]{:S(2)}) %all-to-all-start.1) | async-done | bytes 2097184 | tf_op jit(solution)/shard_map/all_to_all | solution.py:690
  69.1 9.8 %all-to-all-start = ((bf16[16,2,256,128]{3,2,1,0:T(8,128)(2,1)}), bf16[16,2,256,128]{3,2,1,0:T(8,128)(2,1)S(1)}, u32[]{:S(2)}, u32[]{:S(2)}) async-start(bf16[16,2,256,128]{3,2,1,0:T(8,128)(2,1)} %gates.2), calls=%async_computation | async-start | bytes 4194304 | tf_op jit(solution)/shard_map/all_to_all | solution.py:690
  79.0 4.3 pack_taps.3.refs_4_
  93.6 23.9 %raw_path.2 = (f32[17,2,256,256]{3,2,1,0:T(8,128)}, bf16[8,2,512,128]{3,2,1,0:T(8,128)(2,1)}, f32[8,128]{1,0:T(8,128)}, bf16[16,512,128]{2,1,0:T(8,128)(2,1)}) custom-call(bf16[16,2,256,128]{3,2,1,0:T(8,128)(2,1)} %copy-done.5, bf16[17,512,256]{2,1,0:T(8,128)(2,1)} %pad_maximum_fusion.refs_1_.fwd_ref, bf16[17,512,256]{2,1,0:T(8,128)(2,1)} %fusion.refs_2_.inv_ref, ...), custom_call_target="tpu_custom_call" | custom-call | flops 20000000000 | bytes 25000000 | tf_op jit(solution)/shard_map/raw_path/pallas_call | solution.py:342
  117.5 4.1 all-to-all-done.refs_0_.x_ref
  122.8 9.8 %all-to-all-start.4 = ((bf16[16,512,128]{2,1,0:T(8,128)(2,1)}), bf16[16,512,128]{2,1,0:T(8,128)(2,1)S(1)}, u32[]{:S(2)}, u32[]{:S(2)}) async-start(bf16[16,512,128]{2,1,0:T(8,128)(2,1)} %get-tuple-element.23), calls=%async_computation.4 | async-start | bytes 4194304 | tf_op jit(solution)/shard_map/all_to_all | solution.py:690
  132.7 4.3 pack_taps.2.refs_4_
  137.0 23.9 %raw_path.3 = (f32[17,2,256,256]{3,2,1,0:T(8,128)}, bf16[8,2,512,128]{3,2,1,0:T(8,128)(2,1)}, f32[8,128]{1,0:T(8,128)}, bf16[16,512,128]{2,1,0:T(8,128)(2,1)}) custom-call(bf16[16,2,256,128]{3,2,1,0:T(8,128)(2,1)} %copy-done.4, bf16[17,512,256]{2,1,0:T(8,128)(2,1)} %pad_maximum_fusion.refs_1_.fwd_ref, ...), custom_call_target="tpu_custom_call", output_to_operand_aliasing={{1}: (5, {})} | custom-call | flops 20000000000 | bytes 25000000 | tf_op jit(solution)/shard_map/raw_path/pallas_call | solution.py:342
  160.9 14.3 %all-to-all-done.4.refs_10_ = bf16[16,512,128]{2,1,0:T(8,128)(2,1)S(1)} async-done(((bf16[16,512,128]{2,1,0:T(8,128)(2,1)}), bf16[16,512,128]{2,1,0:T(8,128)(2,1)S(1)}, u32[]{:S(2)}, u32[]{:S(2)}) %all-to-all-start.4) | async-done | bytes 2097184 | tf_op jit(solution)/shard_map/all_to_all | solution.py:690
  175.2 9.9 %all-to-all-start.2 = ((bf16[16,512,128]{2,1,0:T(8,128)(2,1)}), bf16[16,512,128]{2,1,0:T(8,128)(2,1)}, u32[]{:S(2)}, u32[]{:S(2)}) async-start(bf16[16,512,128]{2,1,0:T(8,128)(2,1)} %get-tuple-element.21), calls=%async_computation.2 | async-start | bytes 4194304 | tf_op jit(solution)/shard_map/all_to_all | solution.py:690
  186.5 22.6 %conv_path.3 = bf16[16,2,264,128]{3,2,1,0:T(8,128)(2,1)} custom-call(bf16[16,2,256,128]{3,2,1,0:T(8,128)(2,1)} %copy-done.5, bf16[32,256,128]{2,1,0:T(8,128)(2,1)} %bitcast.34, f32[17,2,256,256]{3,2,1,0:T(8,128)} %get-tuple-element.24.spec_ref, f32[1,128]{1,0:T(1,128)} %get-tuple-element.49.skip_ref, bf16[17,512,256]{2,1,0:T(8,128)(2,1)} %pad_maximum_fusion.refs_1_.fwd_ref, ...), custom_call_target="tpu_custom_call" | custom-call | flops 20000000000 | bytes 25000000 | tf_op jit(solution)/shard_map/conv_path/pallas_call | solution.py:411
  209.1 18.6 %all-to-all-done.2.refs_11_ = bf16[16,512,128]{2,1,0:T(8,128)(2,1)} async-done(((bf16[16,512,128]{2,1,0:T(8,128)(2,1)}), bf16[16,512,128]{2,1,0:T(8,128)(2,1)}, u32[]{:S(2)}, u32[]{:S(2)}) %all-to-all-start.2) | async-done | bytes 2097184 | tf_op jit(solution)/shard_map/all_to_all | solution.py:690
  227.7 9.8 %all-to-all-start.5 = ((bf16[16,2,264,128]{3,2,1,0:T(8,128)(2,1)}), bf16[16,2,264,128]{3,2,1,0:T(8,128)(2,1)S(1)}, u32[]{:S(2)}, u32[]{:S(2)}) async-start(bf16[16,2,264,128]{3,2,1,0:T(8,128)(2,1)} %conv_path.3), calls=%async_computation.5 | async-start | bytes 4325376 | tf_op jit(solution)/shard_map/all_to_all | solution.py:690
  237.5 22.7 %conv_path.2 = bf16[16,2,264,128]{3,2,1,0:T(8,128)(2,1)} custom-call(bf16[16,2,256,128]{3,2,1,0:T(8,128)(2,1)} %copy-done.4, bf16[32,256,128]{2,1,0:T(8,128)(2,1)} %bitcast.4.h_ref, f32[17,2,256,256]{3,2,1,0:T(8,128)} %get-tuple-element.22.spec_ref, f32[1,128]{1,0:T(1,128)} %get-tuple-element.50.skip_ref, ...), custom_call_target="tpu_custom_call" | custom-call | flops 20000000000 | bytes 25000000 | tf_op jit(solution)/shard_map/conv_path/pallas_call | solution.py:411
  260.2 21.0 %all-to-all-done.5.y_ref = bf16[16,2,264,128]{3,2,1,0:T(8,128)(2,1)S(1)} async-done(((bf16[16,2,264,128]{3,2,1,0:T(8,128)(2,1)}), bf16[16,2,264,128]{3,2,1,0:T(8,128)(2,1)S(1)}, u32[]{:S(2)}, u32[]{:S(2)}) %all-to-all-start.5) | async-done | bytes 2162720 | tf_op jit(solution)/shard_map/all_to_all | solution.py:690
  282.5 10.1 %all-to-all-start.3 = ((bf16[16,2,264,128]{3,2,1,0:T(8,128)(2,1)}), bf16[16,2,264,128]{3,2,1,0:T(8,128)(2,1)S(1)}, u32[]{:S(2)}, u32[]{:S(2)}) async-start(bf16[16,2,264,128]{3,2,1,0:T(8,128)(2,1)} %conv_path.2), calls=%async_computation.3 | async-start | bytes 4325376 | tf_op jit(solution)/shard_map/all_to_all | solution.py:690
  294.9 10.6 %collective-permute-done.1.n_ref = bf16[4,8,4096]{2,1,0:T(8,128)(2,1)S(1)} collective-permute-done((bf16[4,8,4096]{2,1,0:T(8,128)(2,1)S(1)}, bf16[4,8,4096]{2,1,0:T(8,128)(2,1)S(1)}, u32[]{:S(2)}, u32[]{:S(2)}) %collective-permute-start.1) | collective-permute-done | bytes 262176 | tf_op jit(solution)/shard_map/ppermute | solution.py:686
  306.3 12.8 %finish.2 = (bf16[256,4096]{1,0:T(8,128)(2,1)}, bf16[3,256,4096]{2,1,0:T(8,128)(2,1)}, f32[16,2,24,128]{3,2,1,0:T(8,128)}) custom-call(bf16[3,256,4096]{2,1,0:T(8,128)(2,1)} %x_ref.11, bf16[3,8,4096]{2,1,0:T(8,128)(2,1)} %copy-done.3, bf16[4,8,4096]{2,1,0:T(8,128)(2,1)} %copy-done.6, bf16[256,4096]{1,0:T(8,128)(2,1)} %go_ref.7, f32[3,7,4096]{2,1,0:T(8,128)} %w_ref.7, ...), custom_call_target="tpu_custom_call" | custom-call | flops 150000000 | bytes 12000000 | tf_op jit(solution)/shard_map/finish/pallas_call | solution.py:651
  320.9 15.4 %all-to-all-done.3.y_ref = bf16[16,2,264,128]{3,2,1,0:T(8,128)(2,1)S(1)} async-done(((bf16[16,2,264,128]{3,2,1,0:T(8,128)(2,1)}), bf16[16,2,264,128]{3,2,1,0:T(8,128)(2,1)S(1)}, u32[]{:S(2)}, u32[]{:S(2)}) %all-to-all-start.3) | async-done | bytes 2162720 | tf_op jit(solution)/shard_map/all_to_all | solution.py:690
  337.6 12.9 %finish.3 = (bf16[256,4096]{1,0:T(8,128)(2,1)}, bf16[3,256,4096]{2,1,0:T(8,128)(2,1)}, f32[16,2,24,128]{3,2,1,0:T(8,128)}) custom-call(bf16[3,256,4096]{2,1,0:T(8,128)(2,1)} %x_ref.11, bf16[3,8,4096]{2,1,0:T(8,128)(2,1)} %copy-done.3, bf16[4,8,4096]{2,1,0:T(8,128)(2,1)} %copy-done.6, ...), custom_call_target="tpu_custom_call", output_to_operand_aliasing={{0}: (6, {}), {1}: (7, {}), {2}: (8, {})} | custom-call | flops 150000000 | bytes 12000000 | tf_op jit(solution)/shard_map/finish/pallas_call | solution.py:651
  350.5 29.9 %all-to-all-start.6 = ((f32[16,2,24,128]{3,2,1,0:T(8,128)}), f32[16,2,24,128]{3,2,1,0:T(8,128)S(1)}, u32[]{:S(2)}, u32[]{:S(2)}) async-start(f32[16,2,24,128]{3,2,1,0:T(8,128)} %get-tuple-element.32), calls=%async_computation.6 | async-start | bytes 786432 | tf_op jit(solution)/shard_map/all_to_all | solution.py:690
  382.9 9.3 %all-to-all-done.6 = f32[16,2,24,128]{3,2,1,0:T(8,128)S(1)} async-done(((f32[16,2,24,128]{3,2,1,0:T(8,128)}), f32[16,2,24,128]{3,2,1,0:T(8,128)S(1)}, u32[]{:S(2)}, u32[]{:S(2)}) %all-to-all-start.6) | async-done | bytes 393248 | tf_op jit(solution)/shard_map/all_to_all | solution.py:690
  396.2 3.6 all-to-all-start.7
  402.3 5.6 %collective-permute-start.8 = (bf16[2,512,128]{2,1,0:T(8,128)(2,1)S(1)}, bf16[2,512,128]{2,1,0:T(8,128)(2,1)S(1)}, u32[]{:S(2)}, u32[]{:S(2)}) collective-permute-start(bf16[2,512,128]{2,1,0:T(8,128)(2,1)S(1)} %get-tuple-element.37), channel_id=1, source_target_pairs={{0,14},{2,12},{4,10},{6,8},{8,6},{10,4},{12,2},{14,0},{1,15},{3,13... | collective-permute-start | bytes 786440 | tf_op jit(solution)/shard_map/ppermute | solution.py:745
  410.4 3.4 collective-permute-start.6
  415.8 4.7 %collective-permute-start.4 = (bf16[2,512,128]{2,1,0:T(8,128)(2,1)S(1)}, bf16[2,512,128]{2,1,0:T(8,128)(2,1)S(1)}, u32[]{:S(2)}, u32[]{:S(2)}) collective-permute-start(bf16[2,512,128]{2,1,0:T(8,128)(2,1)S(1)} %get-tuple-element.41), channel_id=1, source_target_pairs={{0,6},{2,4},{4,2},{6,0},{8,14},{10,12},{12,10},{14,8},{1,7},{3,5},... | collective-permute-start | bytes 786440 | tf_op jit(solution)/shard_map/ppermute | solution.py:745
  434.8 8.2 %scale_taps.1 = f32[512,4096]{1,0:T(8,128)} custom-call(f32[1,1]{1,0:T(1,128)} %bitcast.8.refs_0_, s32[1,2]{1,0:T(1,128)} %add_bitcast_fusion.refs_3_.refs_1_, bf16[2,512,128]{2,1,0:T(8,128)(2,1)} %get-tuple-element.44.refs_2_, bf16[2,512,128]{2,1,0:T(8,128)(2,1)} %copy-done.13, bf16[2,512,128]{2,1,0:T(8,128)(2,1)} %copy-done.12, ...), custom_call_target="tpu_custom_call" | custom-call | tf_op jit(solution)/shard_map/scale_taps/pallas_call | solution.py:535
  (72 shorter events, 47.4 us)
Async XLA Ops:
  1.7 9.0 %collective-permute-start = (bf16[3,8,4096]{2,1,0:T(8,128)(2,1)S(1)}, bf16[3,8,4096]{2,1,0:T(8,128)(2,1)S(1)}, u32[]{:S(2)}, u32[]{:S(2)}) collective-permute-start(bf16[3,8,4096]{2,1,0:T(8,128)(2,1)S(1)} %get-tuple-element.36), channel_id=1, source_target_pairs={{0,2},{2,4},{4,6},{6,8},{8,10},{10,12},{12,14},{14,16},{16,18},{18... | collective-permute-start | bytes 589832 | tf_op jit(solution)/shard_map/ppermute | solution.py:686
  17.4 50.3 %all-to-all-start.1 = ((bf16[16,2,256,128]{3,2,1,0:T(8,128)(2,1)}), bf16[16,2,256,128]{3,2,1,0:T(8,128)(2,1)S(1)}, u32[]{:S(2)}, u32[]{:S(2)}) async-start(bf16[16,2,256,128]{3,2,1,0:T(8,128)(2,1)} %gates.3), calls=%async_computation.1 | async-start | bytes 4194304 | tf_op jit(solution)/shard_map/all_to_all | solution.py:690
  67.7 1.4 copy-start.5
  69.1 52.4 %all-to-all-start = ((bf16[16,2,256,128]{3,2,1,0:T(8,128)(2,1)}), bf16[16,2,256,128]{3,2,1,0:T(8,128)(2,1)S(1)}, u32[]{:S(2)}, u32[]{:S(2)}) async-start(bf16[16,2,256,128]{3,2,1,0:T(8,128)(2,1)} %gates.2), calls=%async_computation | async-start | bytes 4194304 | tf_op jit(solution)/shard_map/all_to_all | solution.py:690
  121.5 1.3 copy-start.4
  122.8 52.4 %all-to-all-start.4 = ((bf16[16,512,128]{2,1,0:T(8,128)(2,1)}), bf16[16,512,128]{2,1,0:T(8,128)(2,1)S(1)}, u32[]{:S(2)}, u32[]{:S(2)}) async-start(bf16[16,512,128]{2,1,0:T(8,128)(2,1)} %get-tuple-element.23), calls=%async_computation.4 | async-start | bytes 4194304 | tf_op jit(solution)/shard_map/all_to_all | solution.py:690
  175.2 11.2 %copy-start.2 = (bf16[16,512,128]{2,1,0:T(8,128)(2,1)}, bf16[16,512,128]{2,1,0:T(8,128)(2,1)S(1)}, u32[]{:S(2)}) copy-start(bf16[16,512,128]{2,1,0:T(8,128)(2,1)S(1)} %all-to-all-done.4.refs_10_) | copy-start | bytes 6291460
  175.2 52.5 %all-to-all-start.2 = ((bf16[16,512,128]{2,1,0:T(8,128)(2,1)}), bf16[16,512,128]{2,1,0:T(8,128)(2,1)}, u32[]{:S(2)}, u32[]{:S(2)}) async-start(bf16[16,512,128]{2,1,0:T(8,128)(2,1)} %get-tuple-element.21), calls=%async_computation.2 | async-start | bytes 4194304 | tf_op jit(solution)/shard_map/all_to_all | solution.py:690
  227.7 53.5 %all-to-all-start.5 = ((bf16[16,2,264,128]{3,2,1,0:T(8,128)(2,1)}), bf16[16,2,264,128]{3,2,1,0:T(8,128)(2,1)S(1)}, u32[]{:S(2)}, u32[]{:S(2)}) async-start(bf16[16,2,264,128]{3,2,1,0:T(8,128)(2,1)} %conv_path.3), calls=%async_computation.5 | async-start | bytes 4325376 | tf_op jit(solution)/shard_map/all_to_all | solution.py:690
  281.2 1.3 copy-start.1
  282.5 53.7 %all-to-all-start.3 = ((bf16[16,2,264,128]{3,2,1,0:T(8,128)(2,1)}), bf16[16,2,264,128]{3,2,1,0:T(8,128)(2,1)S(1)}, u32[]{:S(2)}, u32[]{:S(2)}) async-start(bf16[16,2,264,128]{3,2,1,0:T(8,128)(2,1)} %conv_path.2), calls=%async_computation.3 | async-start | bytes 4325376 | tf_op jit(solution)/shard_map/all_to_all | solution.py:690
  293.5 12.1 %collective-permute-start.1 = (bf16[4,8,4096]{2,1,0:T(8,128)(2,1)S(1)}, bf16[4,8,4096]{2,1,0:T(8,128)(2,1)S(1)}, u32[]{:S(2)}, u32[]{:S(2)}) collective-permute-start(bf16[4,8,4096]{2,1,0:T(8,128)(2,1)S(1)} %pad_maximum_fusion.1), channel_id=1, source_target_pairs={{2,0},{4,2},{6,4},{8,6},{10,8},{12,10},{14,12},{16,14},{18,16},{20... | collective-permute-start | bytes 786440 | tf_op jit(solution)/shard_map/ppermute | solution.py:686
  305.6 0.7 copy-start.6
  336.3 1.3 copy-start
  337.6 42.8 %copy-start.14 = (f32[8,128]{1,0:T(8,128)S(1)}, f32[8,128]{1,0:T(8,128)}, u32[]{:S(2)}) copy-start(f32[8,128]{1,0:T(8,128)} %get-tuple-element.30) | copy-start | bytes 12292
  337.6 43.4 %copy-start.15 = (f32[8,128]{1,0:T(8,128)S(1)}, f32[8,128]{1,0:T(8,128)}, u32[]{:S(2)}) copy-start(f32[8,128]{1,0:T(8,128)} %get-tuple-element.31) | copy-start | bytes 12292
  350.5 41.8 %all-to-all-start.6 = ((f32[16,2,24,128]{3,2,1,0:T(8,128)}), f32[16,2,24,128]{3,2,1,0:T(8,128)S(1)}, u32[]{:S(2)}, u32[]{:S(2)}) async-start(f32[16,2,24,128]{3,2,1,0:T(8,128)} %get-tuple-element.32), calls=%async_computation.6 | async-start | bytes 786432 | tf_op jit(solution)/shard_map/all_to_all | solution.py:690
  396.2 24.3 %all-to-all-start.7 = ((bf16[16,2,24,128]{3,1,2,0:T(2,128)(2,1)}), bf16[16,2,24,128]{3,1,2,0:T(2,128)(2,1)S(1)}, u32[]{:S(2)}, u32[]{:S(2)}) async-start(bf16[16,2,24,128]{3,1,2,0:T(2,128)(2,1)} %broadcast_in_dim.37), calls=%async_computation.7 | async-start | bytes 393216 | tf_op jit(solution)/shard_map/all_to_all | solution.py:690
  402.3 18.3 %collective-permute-start.8 = (bf16[2,512,128]{2,1,0:T(8,128)(2,1)S(1)}, bf16[2,512,128]{2,1,0:T(8,128)(2,1)S(1)}, u32[]{:S(2)}, u32[]{:S(2)}) collective-permute-start(bf16[2,512,128]{2,1,0:T(8,128)(2,1)S(1)} %get-tuple-element.37), channel_id=1, source_target_pairs={{0,14},{2,12},{4,10},{6,8},{8,6},{10,4},{12,2},{14,0},{1,15},{3,13... | collective-permute-start | bytes 786440 | tf_op jit(solution)/shard_map/ppermute | solution.py:745
  407.9 15.2 %collective-permute-start.7 = (bf16[2,512,128]{2,1,0:T(8,128)(2,1)S(1)}, bf16[2,512,128]{2,1,0:T(8,128)(2,1)S(1)}, u32[]{:S(2)}, u32[]{:S(2)}) collective-permute-start(bf16[2,512,128]{2,1,0:T(8,128)(2,1)S(1)} %get-tuple-element.38), channel_id=1, source_target_pairs={{0,12},{2,14},{4,8},{6,10},{8,4},{10,6},{12,0},{14,2},{1,13},{3,15... | collective-permute-start | bytes 786440 | tf_op jit(solution)/shard_map/ppermute | solution.py:745
  410.4 20.6 %collective-permute-start.6 = (bf16[2,512,128]{2,1,0:T(8,128)(2,1)S(1)}, bf16[2,512,128]{2,1,0:T(8,128)(2,1)S(1)}, u32[]{:S(2)}, u32[]{:S(2)}) collective-permute-start(bf16[2,512,128]{2,1,0:T(8,128)(2,1)S(1)} %get-tuple-element.39), channel_id=1, source_target_pairs={{0,10},{2,8},{4,14},{6,12},{8,2},{10,0},{12,6},{14,4},{1,11},{3,9}... | collective-permute-start | bytes 786440 | tf_op jit(solution)/shard_map/ppermute | solution.py:745
  413.7 17.2 %collective-permute-start.5 = (bf16[2,512,128]{2,1,0:T(8,128)(2,1)S(1)}, bf16[2,512,128]{2,1,0:T(8,128)(2,1)S(1)}, u32[]{:S(2)}, u32[]{:S(2)}) collective-permute-start(bf16[2,512,128]{2,1,0:T(8,128)(2,1)S(1)} %get-tuple-element.40), channel_id=1, source_target_pairs={{0,8},{2,10},{4,12},{6,14},{8,0},{10,2},{12,4},{14,6},{1,9},{3,11}... | collective-permute-start | bytes 786440 | tf_op jit(solution)/shard_map/ppermute | solution.py:745
  415.8 15.2 %collective-permute-start.4 = (bf16[2,512,128]{2,1,0:T(8,128)(2,1)S(1)}, bf16[2,512,128]{2,1,0:T(8,128)(2,1)S(1)}, u32[]{:S(2)}, u32[]{:S(2)}) collective-permute-start(bf16[2,512,128]{2,1,0:T(8,128)(2,1)S(1)} %get-tuple-element.41), channel_id=1, source_target_pairs={{0,6},{2,4},{4,2},{6,0},{8,14},{10,12},{12,10},{14,8},{1,7},{3,5},... | collective-permute-start | bytes 786440 | tf_op jit(solution)/shard_map/ppermute | solution.py:745
  420.6 13.6 %copy-start.7 = (bf16[2,512,128]{2,1,0:T(8,128)(2,1)}, bf16[2,512,128]{2,1,0:T(8,128)(2,1)S(1)}, u32[]{:S(2)}) copy-start(bf16[2,512,128]{2,1,0:T(8,128)(2,1)S(1)} %collective-permute-done.8.refs_9_) | copy-start | bytes 786436
  420.6 11.0 %collective-permute-start.3 = (bf16[2,512,128]{2,1,0:T(8,128)(2,1)S(1)}, bf16[2,512,128]{2,1,0:T(8,128)(2,1)S(1)}, u32[]{:S(2)}, u32[]{:S(2)}) collective-permute-start(bf16[2,512,128]{2,1,0:T(8,128)(2,1)S(1)} %get-tuple-element.42), channel_id=1, source_target_pairs={{0,4},{2,6},{4,0},{6,2},{8,12},{10,14},{12,8},{14,10},{1,5},{3,7},... | collective-permute-start | bytes 786440 | tf_op jit(solution)/shard_map/ppermute | solution.py:745
  423.1 11.1 %copy-start.8 = (bf16[2,512,128]{2,1,0:T(8,128)(2,1)}, bf16[2,512,128]{2,1,0:T(8,128)(2,1)S(1)}, u32[]{:S(2)}) copy-start(bf16[2,512,128]{2,1,0:T(8,128)(2,1)S(1)} %collective-permute-done.7.refs_8_) | copy-start | bytes 786436
  423.1 11.0 %collective-permute-start.2 = (bf16[2,512,128]{2,1,0:T(8,128)(2,1)S(1)}, bf16[2,512,128]{2,1,0:T(8,128)(2,1)S(1)}, u32[]{:S(2)}, u32[]{:S(2)}) collective-permute-start(bf16[2,512,128]{2,1,0:T(8,128)(2,1)S(1)} %get-tuple-element.43), channel_id=1, source_target_pairs={{0,2},{2,0},{4,6},{6,4},{8,10},{10,8},{12,14},{14,12},{1,3},{3,1},... | collective-permute-start | bytes 786440 | tf_op jit(solution)/shard_map/ppermute | solution.py:745
  431.0 3.2 copy-start.9
  431.0 3.2 copy-start.10
  431.0 3.1 copy-start.11
  431.6 2.6 copy-start.12
  434.1 0.7 copy-start.13
  (1 other events, 0.7 us)

commit v4 on v3

--- a/solution.py
+++ b/solution.py
@@ -15,6 +15,7 @@
 EDGE = 8
 LANES = 128
 SUMS = 24
+ON_CHIP_BYTES = 9 * 2**18
 F32 = jnp.float32
 BF16 = jnp.bfloat16
 
@@ -447,11 +448,11 @@
         ref[(c // chans + i,) + lead + (rs, slice(None))] = value[:, i * chans : (i + 1) * chans]
 
 
-def take(ref, lead, rs, c, width):
+def take(ref, lead, rs, c, width, base=0):
     chans = ref.shape[-1]
     if chans >= width:
-        return ref[(c // chans,) + lead + (rs, pl.ds(c % chans, width))].astype(F32)
-    first = c // chans
+        return ref[(base + c // chans,) + lead + (rs, pl.ds(c % chans, width))].astype(F32)
+    first = base + c // chans
     return jnp.concatenate(
         [ref[(first + i,) + lead + (rs, slice(None))].astype(F32) for i in range(width // chans)], axis=1
     )
@@ -529,7 +530,8 @@
         return index
 
     if listed:
-        low_specs = [whole((parts, rows, chans)) for _ in lows]
+        lows = [on_chip(x) for x in lows]
+        low_specs = [resident() for _ in lows]
     else:
         low_specs = [pl.BlockSpec((groups, 1, rows, chans), lambda q, i: (jnp.minimum(i, split - 1), q, 0, 0))]
     return pl.pallas_call(
@@ -590,6 +592,81 @@
     )(streams, before, grad_out, short_filter)
 
 
+def fill_ext(ext_ref, x_ref, b_ref, n_ref, cs, rows):
+    for i in range(3):
+        ext_ref[i, pl.ds(0, HALO), :] = b_ref[i, :, cs].astype(F32)
+        ext_ref[i, pl.ds(HALO, rows), :] = x_ref[i, :, cs].astype(F32)
+        if n_ref is not None:
+            ext_ref[i, pl.ds(HALO + rows, HALO), :] = n_ref[i, :, cs].astype(F32)
+
+
+def short_sums(streams, before, grad_out, short_filter, back, earlier, shards, part, parts):
+    _, rows, full = streams.shape
+    width = full // parts
+    chans = width // shards
+    block = plan_lanes(width, chans)
+    count = width // block
+    groups = block // chans
+    chunk = math.gcd(rows, 64)
+
+    def kernel(x_ref, b_ref, go_ref, w_ref, y_ref, *refs):
+        st_ref, ext_ref, pre_ref = refs[-3:]
+        base = pl.program_id(0) * groups
+        for c in range(0, block, LANES):
+            cs = pl.ds(c, LANES)
+            fill_ext(ext_ref, x_ref, b_ref, None, cs, rows)
+            bias = jnp.zeros((8, LANES), F32)
+            for r in range(0, rows, chunk):
+                rs = pl.ds(r, chunk)
+                gout = go_ref[rs, cs].astype(F32)
+                upper = take(y_ref, (1,), rs, c, LANES, base)
+                x1s = short_rows(ext_ref, w_ref, 0, cs, r, chunk)
+                vs = short_rows(ext_ref, w_ref, 2, cs, r, chunk)
+                pre_ref[0, rs, :] = upper * vs
+                pre_ref[2, rs, :] = upper * x1s
+                pre_ref[1, rs, :] = gout * take(y_ref, (0,), rs, c, LANES, base)
+                gated = (x1s * vs).astype(BF16).astype(F32)
+                x2s = short_rows(ext_ref, w_ref, 1, cs, r, chunk)
+                term = gated * (gout * x2s).astype(BF16).astype(F32)
+                bias = bias + jnp.sum(term.reshape(chunk // 8, 8, LANES), axis=0)
+            lines = []
+            for i in range(3):
+                sums = [jnp.zeros((8, LANES), F32) for _ in range(TAPS)]
+                for r in range(0, rows, chunk):
+                    own = pre_ref[i, pl.ds(r, chunk), :]
+                    for j in range(TAPS):
+                        term = own * ext_ref[i, pl.ds(HALO + r - j, chunk), :]
+                        sums[j] = sums[j] + jnp.sum(term.reshape(chunk // 8, 8, LANES), axis=0)
+                lines += [jnp.sum(v, axis=0, keepdims=True) for v in sums]
+            lines.append(jnp.sum(bias, axis=0, keepdims=True))
+            lines.append(jnp.zeros((SUMS - len(lines), LANES), F32))
+            put(st_ref, (0,), pl.ds(0, SUMS), c, jnp.concatenate(lines, axis=0))
+
+    at = lambda i: part * count + i
+    ins = [streams, before, grad_out, short_filter, back]
+    return pl.pallas_call(
+        kernel,
+        grid=(count,),
+        in_specs=[
+            pl.BlockSpec((3, rows, block), lambda i: (0, 0, at(i))),
+            pl.BlockSpec((3, HALO, block), lambda i: (0, 0, at(i))),
+            pl.BlockSpec((rows, block), lambda i: (0, at(i))),
+            pl.BlockSpec((3, TAPS, block), lambda i: (0, 0, at(i))),
+            resident(),
+        ]
+        + [untouched() for _ in earlier],
+        out_specs=pl.BlockSpec((groups, 1, SUMS, chans), lambda i: (i, part, 0, 0)),
+        out_shape=jax.ShapeDtypeStruct((shards, parts, SUMS, chans), F32),
+        scratch_shapes=[
+            pltpu.VMEM((3, rows + HALO, LANES), F32),
+            pltpu.VMEM((3, rows, LANES), F32),
+        ],
+        input_output_aliases={len(ins): 0} if earlier else {},
+        cost_estimate=pl.CostEstimate(flops=150 * 10**6, transcendentals=0, bytes_accessed=8 * 10**6),
+        name="short_sums",
+    )(*ins, *earlier)
+
+
 def finish(streams, before, after, grad_out, short_filter, back, earlier, shards, part, parts):
     _, rows, full = streams.shape
     width = full // parts
@@ -600,51 +677,30 @@
     chunk = math.gcd(rows, 64)
 
     def kernel(x_ref, b_ref, n_ref, go_ref, w_ref, y_ref, *refs):
-        o_ref, gs_ref, st_ref, ext_ref, pre_ref = refs[-5:]
+        o_ref, gs_ref, ext_ref, pre_ref = refs[-4:]
+        base = pl.program_id(0) * groups
         for c in range(0, block, LANES):
             cs = pl.ds(c, LANES)
-            for i in range(3):
-                ext_ref[i, pl.ds(0, HALO), :] = b_ref[i, :, cs].astype(F32)
-                ext_ref[i, pl.ds(HALO, rows), :] = x_ref[i, :, cs].astype(F32)
-                ext_ref[i, pl.ds(HALO + rows, HALO), :] = n_ref[i, :, cs].astype(F32)
-            bias = jnp.zeros((8, LANES), F32)
+            fill_ext(ext_ref, x_ref, b_ref, n_ref, cs, rows)
             for r in range(0, rows, chunk):
                 rs = pl.ds(r, chunk)
-                gout = go_ref[rs, cs].astype(F32)
-                mixed = take(y_ref, (0,), rs, c, LANES)
-                upper = take(y_ref, (1,), rs, c, LANES)
-                x1s = short_rows(ext_ref, w_ref, 0, cs, r, chunk)
-                vs = short_rows(ext_ref, w_ref, 2, cs, r, chunk)
-                pre_ref[0, rs, :] = upper * vs
-                pre_ref[2, rs, :] = upper * x1s
-                pre_ref[1, rs, :] = gout * mixed
-                gated = (x1s * vs).astype(BF16).astype(F32)
-                x2s = short_rows(ext_ref, w_ref, 1, cs, r, chunk)
-                o_ref[rs, cs] = (x2s * mixed).astype(BF16)
-                term = gated * (gout * x2s).astype(BF16).astype(F32)
-                bias = bias + jnp.sum(term.reshape(chunk // 8, 8, LANES), axis=0)
-            mixed = take(y_ref, (0,), pl.ds(rows, EDGE), c, LANES)[:HALO]
-            upper = take(y_ref, (1,), pl.ds(rows, EDGE), c, LANES)[:HALO]
+                mixed = take(y_ref, (0,), rs, c, LANES, base)
+                upper = take(y_ref, (1,), rs, c, LANES, base)
+                pre_ref[0, rs, :] = upper * short_rows(ext_ref, w_ref, 2, cs, r, chunk)
+                pre_ref[2, rs, :] = upper * short_rows(ext_ref, w_ref, 0, cs, r, chunk)
+                pre_ref[1, rs, :] = go_ref[rs, cs].astype(F32) * mixed
+                o_ref[rs, cs] = (short_rows(ext_ref, w_ref, 1, cs, r, chunk) * mixed).astype(BF16)
+            mixed = take(y_ref, (0,), pl.ds(rows, EDGE), c, LANES, base)[:HALO]
+            upper = take(y_ref, (1,), pl.ds(rows, EDGE), c, LANES, base)[:HALO]
             pre_ref[0, pl.ds(rows, HALO), :] = upper * short_rows(ext_ref, w_ref, 2, cs, rows, HALO)
             pre_ref[2, pl.ds(rows, HALO), :] = upper * short_rows(ext_ref, w_ref, 0, cs, rows, HALO)
             pre_ref[1, pl.ds(rows, HALO), :] = n_ref[3, :, cs].astype(F32) * mixed
-            lines = []
             for i in range(3):
-                sums = [jnp.zeros((8, LANES), F32) for _ in range(TAPS)]
                 for r in range(0, rows, chunk):
-                    rs = pl.ds(r, chunk)
-                    own = pre_ref[i, rs, :]
-                    total = w_ref[i, 0:1, cs] * own
-                    for j in range(TAPS):
-                        if j:
-                            total = total + w_ref[i, j : j + 1, cs] * pre_ref[i, pl.ds(r + j, chunk), :]
-                        term = own * ext_ref[i, pl.ds(HALO + r - j, chunk), :]
-                        sums[j] = sums[j] + jnp.sum(term.reshape(chunk // 8, 8, LANES), axis=0)
-                    gs_ref[i, rs, cs] = total.astype(BF16)
-                lines += [jnp.sum(v, axis=0, keepdims=True) for v in sums]
-            lines.append(jnp.sum(bias, axis=0, keepdims=True))
-            lines.append(jnp.zeros((SUMS - len(lines), LANES), F32))
-            put(st_ref, (0,), pl.ds(0, SUMS), c, jnp.concatenate(lines, axis=0))
+                    total = w_ref[i, 0:1, cs] * pre_ref[i, pl.ds(r, chunk), :]
+                    for j in range(1, TAPS):
+                        total = total + w_ref[i, j : j + 1, cs] * pre_ref[i, pl.ds(r + j, chunk), :]
+                    gs_ref[i, pl.ds(r, chunk), cs] = total.astype(BF16)
 
     at = lambda i: part * count + i
     ins = [streams, before, after, grad_out, short_filter, back]
@@ -657,18 +713,16 @@
             pl.BlockSpec((4, HALO, block), lambda i: (0, 0, at(i))),
             pl.BlockSpec((rows, block), lambda i: (0, at(i))),
             pl.BlockSpec((3, TAPS, block), lambda i: (0, 0, at(i))),
-            pl.BlockSpec((groups, 2, rows + EDGE, chans), lambda i: (i, 0, 0, 0)),
+            resident(),
         ]
         + [untouched() for _ in earlier],
         out_specs=[
             pl.BlockSpec((rows, block), lambda i: (0, at(i))),
             pl.BlockSpec((3, rows, block), lambda i: (0, 0, at(i))),
-            pl.BlockSpec((groups, 1, SUMS, chans), lambda i: (i, part, 0, 0)),
         ],
         out_shape=[
             jax.ShapeDtypeStruct((rows, full), BF16),
             jax.ShapeDtypeStruct((3, rows, full), BF16),
-            jax.ShapeDtypeStruct((shards, parts, SUMS, chans), F32),
         ],
         scratch_shapes=[
             pltpu.VMEM((3, rows + 2 * HALO, LANES), F32),
@@ -688,6 +742,13 @@
 
 def exchange(blocks, groups=None):
     return lax.all_to_all(blocks, "seq", split_axis=0, concat_axis=0, axis_index_groups=groups, tiled=True)
+
+
+def on_chip(value):
+    lanes = -(-value.shape[-1] // LANES) * LANES
+    if math.prod(value.shape[:-1]) * lanes * value.dtype.itemsize > ON_CHIP_BYTES:
+        return value
+    return pltpu.with_memory_space_constraint(value, pltpu.VMEM)
 
 
 def following(value, earlier):
@@ -716,7 +777,7 @@
     packed = []
     for p in range(parts):
         sent = gates(streams, before, grad_out, short_filter, shards, p, parts)
-        both.append(exchange(sent))
+        both.append(on_chip(exchange(sent)))
     for p in range(parts):
         packed.append(pack_taps(long_filter, shards, p, parts))
     spec = []
@@ -733,17 +794,28 @@
     for p in range(parts):
         taps = shared[p].reshape(shards * tap_rows // rows, rows, chans)
         sent = conv_path(both[p], taps, spec[p], skips[p], fwd, inv)
-        back.append(exchange(sent))
+        back.append(on_chip(exchange(sent)))
+        sent_last = sent
     done = []
+    sums = []
     lows = []
+
+    def send_low(first, last, cue):
+        ready = following(low, cue)
+        if first == 0:
+            lows.append(ready[0])
+        for d in range(max(first, 1), last):
+            lows.append(lax.ppermute(ready[d], "seq", [(i, i ^ d) for i in range(live)]))
+
+    if fold:
+        send_low(0, live // 2 + 1, sent_last)
     for p in range(parts):
+        sums = [short_sums(streams, before, grad_out, short_filter, back[p], sums, shards, p, parts)]
+        if p == 0 and fold:
+            send_low(live // 2 + 1, live, back[0])
         done = finish(streams, before, after, grad_out, short_filter, back[p], done, shards, p, parts)
-        if p == 0 and fold:
-            ready = following(low, done[2])
-            lows.append(ready[0])
-            for d in range(1, live):
-                lows.append(lax.ppermute(ready[d], "seq", [(i, i ^ d) for i in range(live)]))
-    output, grad_streams, sums = done
+    output, grad_streams = done
+    sums = sums[0]
     if not fold:
         lows.append(exchange(following(low, back[-1])))
         sums = following(sums, lows[0])

time: 446 us -> 437 us (0.980)
  starting transfers between devices: 120 us -> 99.8 us
  Pallas kernels: 148 us -> 160 us
  other arithmetic: 13.6 us -> 18.8 us
  local copies, waits for them, and re-layouts: 17.2 us -> 12 us
    pallas_call x0 -> x2, Pallas kernels: none -> 20 us  [short_sums(): pl.pallas_call(kernel, grid=(count,), in_specs=[pl.BlockSpec((3, rows, bl...]
    all_to_all x8, starting transfers between devices: 90.7 us -> 70.9 us  [exchange(): lax.all_to_all(blocks, 'seq', split_axis=0, concat_axis=0, axis_index_gro...]
    all_to_all x8, waiting for transfers between devices: 119 us -> 131 us  [exchange(): lax.all_to_all(blocks, 'seq', split_axis=0, concat_axis=0, axis_index_gro...]
    ppermute x2, waiting for transfers between devices: 14.8 us -> 4.13 us  [shift(): return lax.ppermute(block, axis, route)]
    unnamed x33 -> x10, local copies, waits for them, and re-layouts: 9.28 us -> 2.27 us
    pallas_call x2, Pallas kernels: 25.7 us -> 19.8 us  [finish(): pl.pallas_call(kernel, grid=(count,), in_specs=[pl.BlockSpec((3, rows, bl...]
  transfers between devices with their start and end apart: 17 -> 17, of which waited for: 11 -> 8; matrix products, arithmetic and copies ran while one was open for 5% -> 6% of each run, Pallas kernels for 27% -> 31%
where the time goes in v4:
time: 437 us; the launch traced here: 434 us
  Pallas kernels  160 us (37%)
  waiting for transfers between devices  135 us (31%)
  starting transfers between devices  99.8 us (23%)
  other arithmetic  18.8 us (4%)
  local copies, waits for them, and re-layouts  12 us (3%)
  between operations  4.71 us (1%)
    all_to_all x8, waiting for transfers between devices, exchange(): lax.all_to_all(blocks, 'seq', split_axis=0, concat_axis=0, axis_index_gro...  131 us
    all_to_all x8, starting transfers between devices, exchange(): lax.all_to_all(blocks, 'seq', split_axis=0, concat_axis=0, axis_index_gro...  70.9 us
    pallas_call x2, Pallas kernels, raw_path(): pl.pallas_call(kernel, grid=(steps,), in_specs=in_specs, out_specs=out_sp...  47.3 us
    pallas_call x2, Pallas kernels, conv_path(): pl.pallas_call(kernel, grid=(steps,), in_specs=[resident(), resident(), p...  44.6 us
    ppermute x7, starting transfers between devices, send_low(): lax.ppermute(ready[d], 'seq', [(i, i ^ d) for i in range(live)])  22.7 us
    pallas_call x2, Pallas kernels, short_sums(): pl.pallas_call(kernel, grid=(count,), in_specs=[pl.BlockSpec((3, rows, bl...  20 us
    pallas_call x2, Pallas kernels, finish(): pl.pallas_call(kernel, grid=(count,), in_specs=[pl.BlockSpec((3, rows, bl...  19.8 us
    pallas_call x2, Pallas kernels, gates(): pl.pallas_call(kernel, grid=(count,), in_specs=[pl.BlockSpec((3, rows, bl...  12.1 us
  transfers between devices with their start and end apart: 17, of which 8 were waited for; matrix products, arithmetic and copies ran while one was open for 6% of the time, Pallas kernels for 31%

profile of v4, /device:TPU:0, one launch (start us, length us, event | category | flops | bytes accessed | tf_op | source)
XLA Modules:
  0.0 434.1 jit_solution(7630442327469641748)
XLA Ops:
  1.7 4.9 %collective-permute-start = (bf16[3,8,4096]{2,1,0:T(8,128)(2,1)S(1)}, bf16[3,8,4096]{2,1,0:T(8,128)(2,1)S(1)}, u32[]{:S(2)}, u32[]{:S(2)}) collective-permute-start(bf16[3,8,4096]{2,1,0:T(8,128)(2,1)S(1)} %get-tuple-element.34), channel_id=1, source_target_pairs={{0,2},{2,4},{4,6},{6,8},{8,10},{10,12},{12,14},{14,16},{16,18},{18... | collective-permute-start | bytes 589832 | tf_op jit(solution)/shard_map/ppermute | solution.py:740
  6.6 4.1 collective-permute-done.b_ref
  11.4 6.1 %gates.3 = bf16[16,2,256,128]{3,2,1,0:T(8,128)(2,1)} custom-call(bf16[3,256,4096]{2,1,0:T(8,128)(2,1)} %x_ref.15, bf16[3,8,4096]{2,1,0:T(8,128)(2,1)} %copy-done.2, bf16[256,4096]{1,0:T(8,128)(2,1)} %go_ref.11, f32[3,7,4096]{2,1,0:T(8,128)} %w_ref.11), custom_call_target="tpu_custom_call" | custom-call | flops 60000000 | bytes 7000000 | tf_op jit(solution)/shard_map/gates/pallas_call | solution.py:578
  17.4 7.9 %all-to-all-start.1 = ((bf16[16,2,256,128]{3,2,1,0:T(8,128)(2,1)}), bf16[16,2,256,128]{3,2,1,0:T(8,128)(2,1)S(1)}, u32[]{:S(2)}, u32[]{:S(2)}) async-start(bf16[16,2,256,128]{3,2,1,0:T(8,128)(2,1)} %gates.3), calls=%async_computation.1 | async-start | bytes 4194304 | tf_op jit(solution)/shard_map/all_to_all | solution.py:744
  25.3 6.1 %gates.2 = bf16[16,2,256,128]{3,2,1,0:T(8,128)(2,1)} custom-call(bf16[3,256,4096]{2,1,0:T(8,128)(2,1)} %x_ref.15, bf16[3,8,4096]{2,1,0:T(8,128)(2,1)} %copy-done.2, bf16[256,4096]{1,0:T(8,128)(2,1)} %go_ref.11, f32[3,7,4096]{2,1,0:T(8,128)} %w_ref.11), custom_call_target="tpu_custom_call" | custom-call | flops 60000000 | bytes 7000000 | tf_op jit(solution)/shard_map/gates/pallas_call | solution.py:578
  31.4 36.4 %all-to-all-done.1.refs_0_.x_ref = bf16[16,2,256,128]{3,2,1,0:T(8,128)(2,1)S(1)} async-done(((bf16[16,2,256,128]{3,2,1,0:T(8,128)(2,1)}), bf16[16,2,256,128]{3,2,1,0:T(8,128)(2,1)S(1)}, u32[]{:S(2)}, u32[]{:S(2)}) %all-to-all-start.1) | async-done | bytes 2097184 | tf_op jit(solution)/shard_map/all_to_all | solution.py:744
  67.7 9.9 %all-to-all-start = ((bf16[16,2,256,128]{3,2,1,0:T(8,128)(2,1)}), bf16[16,2,256,128]{3,2,1,0:T(8,128)(2,1)}, u32[]{:S(2)}, u32[]{:S(2)}) async-start(bf16[16,2,256,128]{3,2,1,0:T(8,128)(2,1)} %gates.2), calls=%async_computation | async-start | bytes 4194304 | tf_op jit(solution)/shard_map/all_to_all | solution.py:744
  77.6 4.3 pack_taps.3.refs_4_
  90.2 5.5 %fusion.refs_2_.inv_ref = bf16[17,512,256]{2,1,0:T(8,128)(2,1)} fusion(f32[17,256,256]{2,1,0:T(8,128)} %get-tuple-element.45, f32[17,256,256]{2,1,0:T(8,128)S(1)} %get-tuple-element.43), kind=kLoop, calls=%fused_computation.1 | loop fusion | flops 6684672 | bytes 13369344 | tf_op jit(solution)/shard_map/convert_element_type | solution.py:164
  95.7 23.3 %raw_path.2 = (f32[17,2,256,256]{3,2,1,0:T(8,128)}, bf16[8,2,512,128]{3,2,1,0:T(8,128)(2,1)}, f32[8,128]{1,0:T(8,128)}, bf16[16,512,128]{2,1,0:T(8,128)(2,1)}) custom-call(bf16[16,2,256,128]{3,2,1,0:T(8,128)(2,1)S(1)} %all-to-all-done.1.refs_0_.x_ref, bf16[17,512,256]{2,1,0:T(8,128)(2,1)} %pad_maximum_fusion.refs_1_.fwd_ref, ...), custom_call_target="tpu_custom_call" | custom-call | flops 20000000000 | bytes 25000000 | tf_op jit(solution)/shard_map/raw_path/pallas_call | solution.py:343
  120.2 9.8 %all-to-all-start.4 = ((bf16[16,512,128]{2,1,0:T(8,128)(2,1)}), bf16[16,512,128]{2,1,0:T(8,128)(2,1)}, u32[]{:S(2)}, u32[]{:S(2)}) async-start(bf16[16,512,128]{2,1,0:T(8,128)(2,1)} %get-tuple-element.22), calls=%async_computation.4 | async-start | bytes 4194304 | tf_op jit(solution)/shard_map/all_to_all | solution.py:744
  130.1 4.3 pack_taps.2.refs_4_
  134.4 24.0 %raw_path.3 = (f32[17,2,256,256]{3,2,1,0:T(8,128)}, bf16[8,2,512,128]{3,2,1,0:T(8,128)(2,1)}, f32[8,128]{1,0:T(8,128)}, bf16[16,512,128]{2,1,0:T(8,128)(2,1)}) custom-call(bf16[16,2,256,128]{3,2,1,0:T(8,128)(2,1)} %all-to-all-done.refs_0_.x_ref, bf16[17,512,256]{2,1,0:T(8,128)(2,1)} %pad_maximum_fusion.refs_1_.fwd_ref, ...), custom_call_target="tpu_custom_call", output_to_operand_aliasing={{1}: (5, {})} | custom-call | flops 20000000000 | bytes 25000000 | tf_op jit(solution)/shard_map/raw_path/pallas_call | solution.py:343
  158.3 14.4 %all-to-all-done.4.refs_10_ = bf16[16,512,128]{2,1,0:T(8,128)(2,1)} async-done(((bf16[16,512,128]{2,1,0:T(8,128)(2,1)}), bf16[16,512,128]{2,1,0:T(8,128)(2,1)}, u32[]{:S(2)}, u32[]{:S(2)}) %all-to-all-start.4) | async-done | bytes 2097184 | tf_op jit(solution)/shard_map/all_to_all | solution.py:744
  172.7 9.7 %all-to-all-start.2 = ((bf16[16,512,128]{2,1,0:T(8,128)(2,1)}), bf16[16,512,128]{2,1,0:T(8,128)(2,1)}, u32[]{:S(2)}, u32[]{:S(2)}) async-start(bf16[16,512,128]{2,1,0:T(8,128)(2,1)} %get-tuple-element.20), calls=%async_computation.2 | async-start | bytes 4194304 | tf_op jit(solution)/shard_map/all_to_all | solution.py:744
  185.3 22.0 %conv_path.3 = bf16[16,2,264,128]{3,2,1,0:T(8,128)(2,1)} custom-call(bf16[16,2,256,128]{3,2,1,0:T(8,128)(2,1)S(1)} %copy-done.1, bf16[32,256,128]{2,1,0:T(8,128)(2,1)} %bitcast.6.h_ref, f32[17,2,256,256]{3,2,1,0:T(8,128)} %get-tuple-element.23.spec_ref, f32[1,128]{1,0:T(1,128)} %get-tuple-element.47.skip_ref, ...), custom_call_target="tpu_custom_call" | custom-call | flops 20000000000 | bytes 25000000 | tf_op jit(solution)/shard_map/conv_path/pallas_call | solution.py:412
  207.3 17.8 %all-to-all-done.2.refs_11_ = bf16[16,512,128]{2,1,0:T(8,128)(2,1)} async-done(((bf16[16,512,128]{2,1,0:T(8,128)(2,1)}), bf16[16,512,128]{2,1,0:T(8,128)(2,1)}, u32[]{:S(2)}, u32[]{:S(2)}) %all-to-all-start.2) | async-done | bytes 2097184 | tf_op jit(solution)/shard_map/all_to_all | solution.py:744
  225.1 9.5 %all-to-all-start.5 = ((bf16[16,2,264,128]{3,2,1,0:T(8,128)(2,1)}), bf16[16,2,264,128]{3,2,1,0:T(8,128)(2,1)}, u32[]{:S(2)}, u32[]{:S(2)}) async-start(bf16[16,2,264,128]{3,2,1,0:T(8,128)(2,1)} %conv_path.3), calls=%async_computation.5 | async-start | bytes 4325376 | tf_op jit(solution)/shard_map/all_to_all | solution.py:744
  234.6 22.7 %conv_path.2 = bf16[16,2,264,128]{3,2,1,0:T(8,128)(2,1)} custom-call(bf16[16,2,256,128]{3,2,1,0:T(8,128)(2,1)} %all-to-all-done.refs_0_.x_ref, bf16[32,256,128]{2,1,0:T(8,128)(2,1)} %bitcast.4.h_ref, f32[17,2,256,256]{3,2,1,0:T(8,128)} %get-tuple-element.21.spec_ref, f32[1,128]{1,0:T(1,128)} %get-tuple-element.48.skip_ref, ...), custom_call_target="tpu_custom_call" | custom-call | flops 20000000000 | bytes 25000000 | tf_op jit(solution)/shard_map/conv_path/pallas_call | solution.py:412
  257.3 20.9 %all-to-all-done.5.y_ref = bf16[16,2,264,128]{3,2,1,0:T(8,128)(2,1)} async-done(((bf16[16,2,264,128]{3,2,1,0:T(8,128)(2,1)}), bf16[16,2,264,128]{3,2,1,0:T(8,128)(2,1)}, u32[]{:S(2)}, u32[]{:S(2)}) %all-to-all-start.5) | async-done | bytes 2162720 | tf_op jit(solution)/shard_map/all_to_all | solution.py:744
  278.2 10.0 %all-to-all-start.3 = ((bf16[16,2,264,128]{3,2,1,0:T(8,128)(2,1)}), bf16[16,2,264,128]{3,2,1,0:T(8,128)(2,1)}, u32[]{:S(2)}, u32[]{:S(2)}) async-start(bf16[16,2,264,128]{3,2,1,0:T(8,128)(2,1)} %conv_path.2), calls=%async_computation.3 | async-start | bytes 4325376 | tf_op jit(solution)/shard_map/all_to_all | solution.py:744
  288.2 10.0 %short_sums.2.refs_0_ = f32[16,2,24,128]{3,2,1,0:T(8,128)} custom-call(bf16[3,256,4096]{2,1,0:T(8,128)(2,1)} %x_ref.15, bf16[3,8,4096]{2,1,0:T(8,128)(2,1)} %copy-done.2, bf16[256,4096]{1,0:T(8,128)(2,1)} %go_ref.11, f32[3,7,4096]{2,1,0:T(8,128)} %w_ref.11, bf16[16,2,264,128]{3,2,1,0:T(8,128)(2,1)} %all-to-all-done.5.y_ref), custom_call_target="tpu_custom_call" | custom-call | flops 150000000 | bytes 8000000 | tf_op jit(solution)/shard_map/short_sums/pallas_call | solution.py:647
  298.2 33.3 %all-to-all-done.3.y_ref = bf16[16,2,264,128]{3,2,1,0:T(8,128)(2,1)} async-done(((bf16[16,2,264,128]{3,2,1,0:T(8,128)(2,1)}), bf16[16,2,264,128]{3,2,1,0:T(8,128)(2,1)}, u32[]{:S(2)}, u32[]{:S(2)}) %all-to-all-start.3) | async-done | bytes 2162720 | tf_op jit(solution)/shard_map/all_to_all | solution.py:744
  331.5 10.0 %short_sums.3 = f32[16,2,24,128]{3,2,1,0:T(8,128)} custom-call(bf16[3,256,4096]{2,1,0:T(8,128)(2,1)} %x_ref.15, bf16[3,8,4096]{2,1,0:T(8,128)(2,1)} %copy-done.2, bf16[256,4096]{1,0:T(8,128)(2,1)} %go_ref.11, f32[3,7,4096]{2,1,0:T(8,128)} %w_ref.11, bf16[16,2,264,128]{3,2,1,0:T(8,128)(2,1)} %all-to-all-done.3.y_ref, ...), custom_call_target="tpu_custom_call", output_to_operand_aliasing={{}: (5, {})} | custom-call | flops 150000000 | bytes 8000000 | tf_op jit(solution)/shard_map/short_sums/pallas_call | solution.py:647
  341.5 10.0 %all-to-all-start.6 = ((f32[16,2,24,128]{3,2,1,0:T(8,128)}), f32[16,2,24,128]{3,2,1,0:T(8,128)S(1)}, u32[]{:S(2)}, u32[]{:S(2)}) async-start(f32[16,2,24,128]{3,2,1,0:T(8,128)} %short_sums.3), calls=%async_computation.6 | async-start | bytes 786432 | tf_op jit(solution)/shard_map/all_to_all | solution.py:744
  356.2 7.2 %all-to-all-done.6 = f32[16,2,24,128]{3,2,1,0:T(8,128)S(1)} async-done(((f32[16,2,24,128]{3,2,1,0:T(8,128)}), f32[16,2,24,128]{3,2,1,0:T(8,128)S(1)}, u32[]{:S(2)}, u32[]{:S(2)}) %all-to-all-start.6) | async-done | bytes 393248 | tf_op jit(solution)/shard_map/all_to_all | solution.py:744
  367.3 4.2 all-to-all-start.7
  377.4 4.3 collective-permute-start.4
  388.8 4.3 collective-permute-start.8
  393.0 9.9 %finish.2 = (bf16[256,4096]{1,0:T(8,128)(2,1)}, bf16[3,256,4096]{2,1,0:T(8,128)(2,1)}) custom-call(bf16[3,256,4096]{2,1,0:T(8,128)(2,1)} %x_ref.15, bf16[3,8,4096]{2,1,0:T(8,128)(2,1)} %copy-done.2, bf16[4,8,4096]{2,1,0:T(8,128)(2,1)} %collective-permute-done.1.n_ref, bf16[256,4096]{1,0:T(8,128)(2,1)} %go_ref.11, f32[3,7,4096]{2,1,0:T(8,128)} %w_ref.11, ...), custom_call_target="tpu_custom_call" | custom-call | flops 150000000 | bytes 12000000 | tf_op jit(solution)/shard_map/finish/pallas_call | solution.py:707
  410.1 9.9 %finish.3 = (bf16[256,4096]{1,0:T(8,128)(2,1)}, bf16[3,256,4096]{2,1,0:T(8,128)(2,1)}) custom-call(bf16[3,256,4096]{2,1,0:T(8,128)(2,1)} %x_ref.15, bf16[3,8,4096]{2,1,0:T(8,128)(2,1)} %copy-done.2, bf16[4,8,4096]{2,1,0:T(8,128)(2,1)} %collective-permute-done.1.n_ref, bf16[256,4096]{1,0:T(8,128)(2,1)} %go_ref.11, ...), custom_call_target="tpu_custom_call", output_to_operand_aliasing={{0}: (6, {}), {1}: (7, {})} | custom-call | flops 150000000 | bytes 12000000 | tf_op jit(solution)/shard_map/finish/pallas_call | solution.py:707
  426.2 7.8 %scale_taps.1 = f32[512,4096]{1,0:T(8,128)} custom-call(f32[1,1]{1,0:T(1,128)} %bitcast.8.refs_0_, s32[1,2]{1,0:T(1,128)} %add_bitcast_fusion.refs_3_.refs_1_, bf16[2,512,128]{2,1,0:T(8,128)(2,1)S(1)} %get-tuple-element.42.refs_2_, bf16[2,512,128]{2,1,0:T(8,128)(2,1)S(1)} %collective-permute-done.2.refs_3_, ...), custom_call_target="tpu_custom_call" | custom-call | tf_op jit(solution)/shard_map/scale_taps/pallas_call | solution.py:537
  (52 shorter events, 45.2 us)
Async XLA Ops:
  1.7 9.0 %collective-permute-start = (bf16[3,8,4096]{2,1,0:T(8,128)(2,1)S(1)}, bf16[3,8,4096]{2,1,0:T(8,128)(2,1)S(1)}, u32[]{:S(2)}, u32[]{:S(2)}) collective-permute-start(bf16[3,8,4096]{2,1,0:T(8,128)(2,1)S(1)} %get-tuple-element.34), channel_id=1, source_target_pairs={{0,2},{2,4},{4,6},{6,8},{8,10},{10,12},{12,14},{14,16},{16,18},{18... | collective-permute-start | bytes 589832 | tf_op jit(solution)/shard_map/ppermute | solution.py:740
  10.7 0.7 copy-start.2
  17.4 50.3 %all-to-all-start.1 = ((bf16[16,2,256,128]{3,2,1,0:T(8,128)(2,1)}), bf16[16,2,256,128]{3,2,1,0:T(8,128)(2,1)S(1)}, u32[]{:S(2)}, u32[]{:S(2)}) async-start(bf16[16,2,256,128]{3,2,1,0:T(8,128)(2,1)} %gates.3), calls=%async_computation.1 | async-start | bytes 4194304 | tf_op jit(solution)/shard_map/all_to_all | solution.py:744
  67.7 27.9 %copy-start = (bf16[16,2,256,128]{3,2,1,0:T(8,128)(2,1)}, bf16[16,2,256,128]{3,2,1,0:T(8,128)(2,1)S(1)}, u32[]{:S(2)}) copy-start(bf16[16,2,256,128]{3,2,1,0:T(8,128)(2,1)S(1)} %all-to-all-done.1.refs_0_.x_ref) | copy-start | bytes 6291460
  67.7 52.5 %all-to-all-start = ((bf16[16,2,256,128]{3,2,1,0:T(8,128)(2,1)}), bf16[16,2,256,128]{3,2,1,0:T(8,128)(2,1)}, u32[]{:S(2)}, u32[]{:S(2)}) async-start(bf16[16,2,256,128]{3,2,1,0:T(8,128)(2,1)} %gates.2), calls=%async_computation | async-start | bytes 4194304 | tf_op jit(solution)/shard_map/all_to_all | solution.py:744
  120.2 52.5 %all-to-all-start.4 = ((bf16[16,512,128]{2,1,0:T(8,128)(2,1)}), bf16[16,512,128]{2,1,0:T(8,128)(2,1)}, u32[]{:S(2)}, u32[]{:S(2)}) async-start(bf16[16,512,128]{2,1,0:T(8,128)(2,1)} %get-tuple-element.22), calls=%async_computation.4 | async-start | bytes 4194304 | tf_op jit(solution)/shard_map/all_to_all | solution.py:744
  172.7 52.4 %all-to-all-start.2 = ((bf16[16,512,128]{2,1,0:T(8,128)(2,1)}), bf16[16,512,128]{2,1,0:T(8,128)(2,1)}, u32[]{:S(2)}, u32[]{:S(2)}) async-start(bf16[16,512,128]{2,1,0:T(8,128)(2,1)} %get-tuple-element.20), calls=%async_computation.2 | async-start | bytes 4194304 | tf_op jit(solution)/shard_map/all_to_all | solution.py:744
  183.7 1.6 copy-start.1
  225.1 53.1 %all-to-all-start.5 = ((bf16[16,2,264,128]{3,2,1,0:T(8,128)(2,1)}), bf16[16,2,264,128]{3,2,1,0:T(8,128)(2,1)}, u32[]{:S(2)}, u32[]{:S(2)}) async-start(bf16[16,2,264,128]{3,2,1,0:T(8,128)(2,1)} %conv_path.3), calls=%async_computation.5 | async-start | bytes 4325376 | tf_op jit(solution)/shard_map/all_to_all | solution.py:744
  278.2 53.3 %all-to-all-start.3 = ((bf16[16,2,264,128]{3,2,1,0:T(8,128)(2,1)}), bf16[16,2,264,128]{3,2,1,0:T(8,128)(2,1)}, u32[]{:S(2)}, u32[]{:S(2)}) async-start(bf16[16,2,264,128]{3,2,1,0:T(8,128)(2,1)} %conv_path.2), calls=%async_computation.3 | async-start | bytes 4325376 | tf_op jit(solution)/shard_map/all_to_all | solution.py:744
  298.2 55.5 %copy-start.3 = (f32[8,128]{1,0:T(8,128)S(1)}, f32[8,128]{1,0:T(8,128)}, u32[]{:S(2)}) copy-start(f32[8,128]{1,0:T(8,128)} %get-tuple-element.28) | copy-start | bytes 12292
  298.2 56.1 %copy-start.4 = (f32[8,128]{1,0:T(8,128)S(1)}, f32[8,128]{1,0:T(8,128)}, u32[]{:S(2)}) copy-start(f32[8,128]{1,0:T(8,128)} %get-tuple-element.29) | copy-start | bytes 12292
  341.5 21.9 %all-to-all-start.6 = ((f32[16,2,24,128]{3,2,1,0:T(8,128)}), f32[16,2,24,128]{3,2,1,0:T(8,128)S(1)}, u32[]{:S(2)}, u32[]{:S(2)}) async-start(f32[16,2,24,128]{3,2,1,0:T(8,128)} %short_sums.3), calls=%async_computation.6 | async-start | bytes 786432 | tf_op jit(solution)/shard_map/all_to_all | solution.py:744
  352.3 36.4 %collective-permute-start.1 = (bf16[4,8,4096]{2,1,0:T(8,128)(2,1)S(1)}, bf16[4,8,4096]{2,1,0:T(8,128)(2,1)}, u32[]{:S(2)}, u32[]{:S(2)}) collective-permute-start(bf16[4,8,4096]{2,1,0:T(8,128)(2,1)S(1)} %pad_maximum_fusion.1), channel_id=1, source_target_pairs={{2,0},{4,2},{6,4},{8,6},{10,8},{12,10},{14,12},{16,14},{18,16},{20... | collective-permute-start | bytes 786440 | tf_op jit(solution)/shard_map/ppermute | solution.py:740
  367.3 35.6 %all-to-all-start.7 = ((bf16[16,2,24,128]{3,1,2,0:T(2,128)(2,1)}), bf16[16,2,24,128]{3,1,2,0:T(2,128)(2,1)}, u32[]{:S(2)}, u32[]{:S(2)}) async-start(bf16[16,2,24,128]{3,1,2,0:T(2,128)(2,1)} %broadcast_in_dim.37), calls=%async_computation.7 | async-start | bytes 393216 | tf_op jit(solution)/shard_map/all_to_all | solution.py:744
  373.8 30.2 %collective-permute-start.5 = (bf16[2,512,128]{2,1,0:T(8,128)(2,1)}, bf16[2,512,128]{2,1,0:T(8,128)(2,1)S(1)}, u32[]{:S(2)}, u32[]{:S(2)}) collective-permute-start(bf16[2,512,128]{2,1,0:T(8,128)(2,1)} %get-tuple-element.38), channel_id=1, source_target_pairs={{0,8},{2,10},{4,12},{6,14},{8,0},{10,2},{12,4},{14,6},{1,9},{3,11}... | collective-permute-start | bytes 786440 | tf_op jit(solution)/shard_map/ppermute | solution.py:808
  377.4 29.9 %collective-permute-start.4 = (bf16[2,512,128]{2,1,0:T(8,128)(2,1)}, bf16[2,512,128]{2,1,0:T(8,128)(2,1)S(1)}, u32[]{:S(2)}, u32[]{:S(2)}) collective-permute-start(bf16[2,512,128]{2,1,0:T(8,128)(2,1)} %get-tuple-element.39), channel_id=1, source_target_pairs={{0,6},{2,4},{4,2},{6,0},{8,14},{10,12},{12,10},{14,8},{1,7},{3,5},... | collective-permute-start | bytes 786440 | tf_op jit(solution)/shard_map/ppermute | solution.py:808
  381.7 44.5 %collective-permute-start.3 = (bf16[2,512,128]{2,1,0:T(8,128)(2,1)}, bf16[2,512,128]{2,1,0:T(8,128)(2,1)S(1)}, u32[]{:S(2)}, u32[]{:S(2)}) collective-permute-start(bf16[2,512,128]{2,1,0:T(8,128)(2,1)} %get-tuple-element.40), channel_id=1, source_target_pairs={{0,4},{2,6},{4,0},{6,2},{8,12},{10,14},{12,8},{14,10},{1,5},{3,7},... | collective-permute-start | bytes 786440 | tf_op jit(solution)/shard_map/ppermute | solution.py:808
  384.2 42.0 %collective-permute-start.2 = (bf16[2,512,128]{2,1,0:T(8,128)(2,1)}, bf16[2,512,128]{2,1,0:T(8,128)(2,1)S(1)}, u32[]{:S(2)}, u32[]{:S(2)}) collective-permute-start(bf16[2,512,128]{2,1,0:T(8,128)(2,1)} %get-tuple-element.41), channel_id=1, source_target_pairs={{0,2},{2,0},{4,6},{6,4},{8,10},{10,8},{12,14},{14,12},{1,3},{3,1},... | collective-permute-start | bytes 786440 | tf_op jit(solution)/shard_map/ppermute | solution.py:808
  388.8 37.5 %collective-permute-start.8 = (bf16[2,512,128]{2,1,0:T(8,128)(2,1)}, bf16[2,512,128]{2,1,0:T(8,128)(2,1)}, u32[]{:S(2)}, u32[]{:S(2)}) collective-permute-start(bf16[2,512,128]{2,1,0:T(8,128)(2,1)} %get-tuple-element.35), channel_id=1, source_target_pairs={{0,14},{2,12},{4,10},{6,8},{8,6},{10,4},{12,2},{14,0},{1,15},{3,13... | collective-permute-start | bytes 786440 | tf_op jit(solution)/shard_map/ppermute | solution.py:808
  403.9 22.3 %collective-permute-start.7 = (bf16[2,512,128]{2,1,0:T(8,128)(2,1)}, bf16[2,512,128]{2,1,0:T(8,128)(2,1)}, u32[]{:S(2)}, u32[]{:S(2)}) collective-permute-start(bf16[2,512,128]{2,1,0:T(8,128)(2,1)} %get-tuple-element.36), channel_id=1, source_target_pairs={{0,12},{2,14},{4,8},{6,10},{8,4},{10,6},{12,0},{14,2},{1,13},{3,15... | collective-permute-start | bytes 786440 | tf_op jit(solution)/shard_map/ppermute | solution.py:808
  407.3 18.9 %collective-permute-start.6 = (bf16[2,512,128]{2,1,0:T(8,128)(2,1)}, bf16[2,512,128]{2,1,0:T(8,128)(2,1)}, u32[]{:S(2)}, u32[]{:S(2)}) collective-permute-start(bf16[2,512,128]{2,1,0:T(8,128)(2,1)} %get-tuple-element.37), channel_id=1, source_target_pairs={{0,10},{2,8},{4,14},{6,12},{8,2},{10,0},{12,6},{14,4},{1,11},{3,9}... | collective-permute-start | bytes 786440 | tf_op jit(solution)/shard_map/ppermute | solution.py:808

commit v5 on v4

--- a/solution.py
+++ b/solution.py
@@ -481,7 +481,7 @@
     )(long_filter)
 
 
-def scale_taps(clip, where, lows, shared, shards, live):
+def scale_taps(small, where, lows, shared, shards, live, param_count):
     parts, rows, chans = lows[0].shape[-3:]
     width = shards * chans
     block = plan_lanes(width, chans)
@@ -493,12 +493,22 @@
     listed = len(lows) > 1
 
     def kernel(*refs):
-        c_ref, at_ref = refs[:2]
+        small_ref, at_ref = refs[:2]
         low_refs = refs[2 : 2 + len(lows)]
-        o_ref = refs[-1]
+        o_ref, short_ref, bias_ref = refs[-3:]
         q = pl.program_id(0)
         i = pl.program_id(1)
-        gain = c_ref[0, 0]
+        total = jnp.zeros((SUMS, min(chans, LANES)), F32)
+        for j in range(shards):
+            total = total + small_ref[j, 0, :, pl.ds(0, min(chans, LANES))].astype(F32)
+        total = total[SUMS - 2 : SUMS - 1, 0:1] + total[SUMS - 1 :, 0:1]
+        clip = 1.0 / jnp.sqrt(jnp.broadcast_to(total, (1, LANES)) / param_count + 1e-06)
+        gain = clip * at_ref[0, 0].astype(F32)
+        for c in range(0, block, LANES):
+            lines = take(small_ref, (q,), slice(None), c, LANES, i * groups) * clip
+            for j in range(3):
+                short_ref[j, :, pl.ds(c, LANES)] = lines[j * TAPS : (j + 1) * TAPS]
+            bias_ref[:, pl.ds(c, LANES)] = lines[3 * TAPS : 3 * TAPS + 1]
 
         @pl.when(i < split)
         def _():
@@ -512,9 +522,9 @@
 
                     @pl.when(source == d)
                     def _(j=j, x_ref=x_ref):
-                        o_ref[:, pl.ds(j * chans, chans)] = x_ref[q].astype(F32) * gain
-
-        for part, x_ref in enumerate(refs[2 + len(lows) : -1]):
+                        o_ref[:, pl.ds(j * chans, chans)] = x_ref[q].astype(F32) * jnp.concatenate([gain] * (chans // LANES), axis=1)
+
+        for part, x_ref in enumerate(refs[2 + len(lows) : -3]):
 
             @pl.when(jnp.logical_and(i >= split, q == part))
             def _(x_ref=x_ref):
@@ -537,13 +547,21 @@
     return pl.pallas_call(
         kernel,
         grid=(parts, count),
-        in_specs=[in_smem(), in_smem()]
+        in_specs=[whole(small.shape), in_smem()]
         + low_specs
         + [pl.BlockSpec((groups, rows, chans), shared_map(p)) for p in range(len(shared))],
-        out_specs=pl.BlockSpec((rows, block), lambda q, i: (0, q * count + i)),
-        out_shape=jax.ShapeDtypeStruct((rows, parts * width), F32),
+        out_specs=[
+            pl.BlockSpec((rows, block), lambda q, i: (0, q * count + i)),
+            pl.BlockSpec((3, TAPS, block), lambda q, i: (0, 0, q * count + i)),
+            pl.BlockSpec((1, block), lambda q, i: (0, q * count + i)),
+        ],
+        out_shape=[
+            jax.ShapeDtypeStruct((rows, parts * width), F32),
+            jax.ShapeDtypeStruct((3, TAPS, parts * width), F32),
+            jax.ShapeDtypeStruct((1, parts * width), F32),
+        ],
         name="scale_taps",
-    )(clip, where, *lows, *shared)
+    )(small, where, *lows, *shared)
 
 
 def short_rows(ext_ref, w_ref, i, cs, r, rows):
@@ -553,7 +571,7 @@
     return total
 
 
-def gates(streams, before, grad_out, short_filter, shards, part, parts):
+def gates(streams, before, grad_out, short_filter, shards, part, parts, keep):
     _, rows, width = streams.shape
     width = width // parts
     chans = width // shards
@@ -562,19 +580,39 @@
     groups = block // chans
     chunk = math.gcd(rows, 64)
 
-    def kernel(x_ref, b_ref, go_ref, w_ref, o_ref, ext_ref):
+    def kernel(x_ref, b_ref, go_ref, w_ref, o_ref, bias_ref, *refs):
+        ext_ref = refs[-1]
         for c in range(0, block, LANES):
             cs = pl.ds(c, LANES)
-            for i in range(3):
-                ext_ref[i, pl.ds(0, HALO), :] = b_ref[i, :, cs].astype(F32)
-                ext_ref[i, pl.ds(HALO, rows), :] = x_ref[i, :, cs].astype(F32)
+            fill_ext(ext_ref, x_ref, b_ref, None, cs, rows)
+            bias = jnp.zeros((8, LANES), F32)
             for r in range(0, rows, chunk):
                 rs = pl.ds(r, chunk)
-                gated = short_rows(ext_ref, w_ref, 0, cs, r, chunk) * short_rows(ext_ref, w_ref, 2, cs, r, chunk)
+                x1s = short_rows(ext_ref, w_ref, 0, cs, r, chunk)
+                vs = short_rows(ext_ref, w_ref, 2, cs, r, chunk)
+                gated = (x1s * vs).astype(BF16)
                 mix = go_ref[rs, cs].astype(F32) * short_rows(ext_ref, w_ref, 1, cs, r, chunk)
-                put(o_ref, (0,), rs, c, gated.astype(BF16))
-                put(o_ref, (1,), rs, c, mix.astype(BF16))
-
+                mix = mix.astype(BF16)
+                put(o_ref, (0,), rs, c, gated)
+                put(o_ref, (1,), rs, c, mix)
+                if keep:
+                    refs[0][0, rs, cs] = x1s
+                    refs[0][1, rs, cs] = vs
+                term = gated.astype(F32) * mix.astype(F32)
+                bias = bias + jnp.sum(term.reshape(chunk // 8, 8, LANES), axis=0)
+            bias_ref[:, cs] = jnp.sum(bias, axis=0, keepdims=True)
+
+    out_specs = [
+        pl.BlockSpec((groups, 2, rows, chans), lambda i: (i, 0, 0, 0)),
+        pl.BlockSpec((1, block), lambda i: (0, i)),
+    ]
+    out_shape = [
+        jax.ShapeDtypeStruct((shards, 2, rows, chans), BF16),
+        jax.ShapeDtypeStruct((1, width), F32),
+    ]
+    if keep:
+        out_specs.append(pl.BlockSpec((2, rows, block), lambda i: (0, 0, i)))
+        out_shape.append(jax.ShapeDtypeStruct((2, rows, width), F32))
     return pl.pallas_call(
         kernel,
         grid=(count,),
@@ -584,8 +622,8 @@
             pl.BlockSpec((rows, block), lambda i: (0, part * count + i)),
             pl.BlockSpec((3, TAPS, block), lambda i: (0, 0, part * count + i)),
         ],
-        out_specs=pl.BlockSpec((groups, 2, rows, chans), lambda i: (i, 0, 0, 0)),
-        out_shape=jax.ShapeDtypeStruct((shards, 2, rows, chans), BF16),
+        out_specs=out_specs,
+        out_shape=out_shape,
         scratch_shapes=[pltpu.VMEM((3, rows + HALO, LANES), F32)],
         cost_estimate=pl.CostEstimate(flops=60 * 10**6, transcendentals=0, bytes_accessed=7 * 10**6),
         name="gates",
@@ -600,7 +638,7 @@
             ext_ref[i, pl.ds(HALO + rows, HALO), :] = n_ref[i, :, cs].astype(F32)
 
 
-def short_sums(streams, before, grad_out, short_filter, back, earlier, shards, part, parts):
+def short_sums(streams, before, grad_out, short_filter, back, bias, kept, earlier, shards, part, parts):
     _, rows, full = streams.shape
     width = full // parts
     chans = width // shards
@@ -609,26 +647,24 @@
     groups = block // chans
     chunk = math.gcd(rows, 64)
 
-    def kernel(x_ref, b_ref, go_ref, w_ref, y_ref, *refs):
+    def kernel(x_ref, b_ref, go_ref, w_ref, y_ref, bias_ref, *refs):
         st_ref, ext_ref, pre_ref = refs[-3:]
         base = pl.program_id(0) * groups
         for c in range(0, block, LANES):
             cs = pl.ds(c, LANES)
             fill_ext(ext_ref, x_ref, b_ref, None, cs, rows)
-            bias = jnp.zeros((8, LANES), F32)
             for r in range(0, rows, chunk):
                 rs = pl.ds(r, chunk)
-                gout = go_ref[rs, cs].astype(F32)
                 upper = take(y_ref, (1,), rs, c, LANES, base)
-                x1s = short_rows(ext_ref, w_ref, 0, cs, r, chunk)
-                vs = short_rows(ext_ref, w_ref, 2, cs, r, chunk)
+                if kept is None:
+                    x1s = short_rows(ext_ref, w_ref, 0, cs, r, chunk)
+                    vs = short_rows(ext_ref, w_ref, 2, cs, r, chunk)
+                else:
+                    x1s = refs[0][0, rs, cs]
+                    vs = refs[0][1, rs, cs]
                 pre_ref[0, rs, :] = upper * vs
                 pre_ref[2, rs, :] = upper * x1s
-                pre_ref[1, rs, :] = gout * take(y_ref, (0,), rs, c, LANES, base)
-                gated = (x1s * vs).astype(BF16).astype(F32)
-                x2s = short_rows(ext_ref, w_ref, 1, cs, r, chunk)
-                term = gated * (gout * x2s).astype(BF16).astype(F32)
-                bias = bias + jnp.sum(term.reshape(chunk // 8, 8, LANES), axis=0)
+                pre_ref[1, rs, :] = go_ref[rs, cs].astype(F32) * take(y_ref, (0,), rs, c, LANES, base)
             lines = []
             for i in range(3):
                 sums = [jnp.zeros((8, LANES), F32) for _ in range(TAPS)]
@@ -638,25 +674,29 @@
                         term = own * ext_ref[i, pl.ds(HALO + r - j, chunk), :]
                         sums[j] = sums[j] + jnp.sum(term.reshape(chunk // 8, 8, LANES), axis=0)
                 lines += [jnp.sum(v, axis=0, keepdims=True) for v in sums]
-            lines.append(jnp.sum(bias, axis=0, keepdims=True))
+            lines.append(bias_ref[:, cs])
             lines.append(jnp.zeros((SUMS - len(lines), LANES), F32))
-            put(st_ref, (0,), pl.ds(0, SUMS), c, jnp.concatenate(lines, axis=0))
+            put(st_ref, (0,), pl.ds(0, SUMS), c, jnp.concatenate(lines, axis=0).astype(BF16))
 
     at = lambda i: part * count + i
-    ins = [streams, before, grad_out, short_filter, back]
+    ins = [streams, before, grad_out, short_filter, back, bias]
+    in_specs = [
+        pl.BlockSpec((3, rows, block), lambda i: (0, 0, at(i))),
+        pl.BlockSpec((3, HALO, block), lambda i: (0, 0, at(i))),
+        pl.BlockSpec((rows, block), lambda i: (0, at(i))),
+        pl.BlockSpec((3, TAPS, block), lambda i: (0, 0, at(i))),
+        resident(),
+        pl.BlockSpec((1, block), lambda i: (0, i)),
+    ]
+    if kept is not None:
+        ins.append(kept)
+        in_specs.append(pl.BlockSpec((2, rows, block), lambda i: (0, 0, i)))
     return pl.pallas_call(
         kernel,
         grid=(count,),
-        in_specs=[
-            pl.BlockSpec((3, rows, block), lambda i: (0, 0, at(i))),
-            pl.BlockSpec((3, HALO, block), lambda i: (0, 0, at(i))),
-            pl.BlockSpec((rows, block), lambda i: (0, at(i))),
-            pl.BlockSpec((3, TAPS, block), lambda i: (0, 0, at(i))),
-            resident(),
-        ]
-        + [untouched() for _ in earlier],
+        in_specs=in_specs + [untouched() for _ in earlier],
         out_specs=pl.BlockSpec((groups, 1, SUMS, chans), lambda i: (i, part, 0, 0)),
-        out_shape=jax.ShapeDtypeStruct((shards, parts, SUMS, chans), F32),
+        out_shape=jax.ShapeDtypeStruct((shards, parts, SUMS, chans), BF16),
         scratch_shapes=[
             pltpu.VMEM((3, rows + HALO, LANES), F32),
             pltpu.VMEM((3, rows, LANES), F32),
@@ -774,9 +814,14 @@
     skips = [lax.dynamic_slice_in_dim(skip_gain, p * span + mine * chans, chans)[None] for p in range(parts)]
 
     both = []
+    bias = []
+    filtered = []
     packed = []
     for p in range(parts):
-        sent = gates(streams, before, grad_out, short_filter, shards, p, parts)
+        keep = p == parts - 1 and parts > 1
+        sent, terms, *rest = gates(streams, before, grad_out, short_filter, shards, p, parts, keep)
+        bias.append(terms)
+        filtered.append(rest[0] if rest else None)
         both.append(on_chip(exchange(sent)))
     for p in range(parts):
         packed.append(pack_taps(long_filter, shards, p, parts))
@@ -810,7 +855,8 @@
     if fold:
         send_low(0, live // 2 + 1, sent_last)
     for p in range(parts):
-        sums = [short_sums(streams, before, grad_out, short_filter, back[p], sums, shards, p, parts)]
+        terms = (back[p], bias[p], filtered[p], sums)
+        sums = [short_sums(streams, before, grad_out, short_filter, *terms, shards, p, parts)]
         if p == 0 and fold:
             send_low(live // 2 + 1, live, back[0])
         done = finish(streams, before, after, grad_out, short_filter, back[p], done, shards, p, parts)
@@ -819,26 +865,18 @@
     if not fold:
         lows.append(exchange(following(low, back[-1])))
         sums = following(sums, lows[0])
-    mine_sums = jnp.sum(exchange(sums), axis=0)
-    local_sq = squares + jnp.sum(mine_sums * mine_sums)
+    mine_sums = jnp.sum(exchange(sums).astype(F32), axis=0)
+    local_sq = lax.psum(squares + jnp.sum(mine_sums * mine_sums), "chan")
     upper_sq = lax.reduce_precision(local_sq, 8, 7)
     line = lax.broadcasted_iota(jnp.int32, mine_sums.shape, 1)
     mine_sums = jnp.where(line == SUMS - 2, upper_sq, mine_sums)
     mine_sums = jnp.where(line == SUMS - 1, local_sq - upper_sq, mine_sums).astype(BF16)
-    small = exchange(jnp.broadcast_to(mine_sums[None], (shards,) + mine_sums.shape)).astype(F32)
-    sq_total = lax.psum(jnp.sum(small[:, 0, SUMS - 2 :, 0]), "chan")
+    small = exchange(jnp.broadcast_to(mine_sums[None], (shards,) + mine_sums.shape))
     param_count = LF * D + (3 * TAPS + 1) * D
-    clip = 1.0 / jnp.sqrt(sq_total / param_count + 1e-06)
-    kept = jnp.where(is_low, clip, 0.0).reshape(1, 1)
-    filter_grad = scale_taps(kept, where, lows, shared if fold else [], shards, live)
-    small = small.transpose(2, 1, 0, 3).reshape(SUMS, width) * clip
-    return (
-        output,
-        grad_streams,
-        filter_grad,
-        small[: 3 * TAPS].reshape(3, TAPS, width),
-        small[3 * TAPS],
+    filter_grad, short_grad, bias_grad = scale_taps(
+        small, where, lows, shared if fold else [], shards, live, param_count
     )
+    return output, grad_streams, filter_grad, short_grad, bias_grad[0]
 
 
 def solution(mesh):

time: 437 us -> 426 us (0.975)
  waiting for transfers between devices: 135 us -> 126 us
    all_to_all x8, waiting for transfers between devices: 131 us -> 122 us  [exchange(): lax.all_to_all(blocks, 'seq', split_axis=0, concat_axis=0, axis_index_gro...]
  transfers between devices with their start and end apart: 17 -> 17, of which waited for: 8 -> 7; matrix products, arithmetic and copies ran while one was open for 6% -> 6% of each run, Pallas kernels for 31% -> 34%
where the time goes in v5:
time: 426 us; the launch traced here: 423 us
  Pallas kernels  159 us (37%)
  waiting for transfers between devices  126 us (30%)
  starting transfers between devices  103 us (24%)
  other arithmetic  16.3 us (4%)
  local copies, waits for them, and re-layouts  10.4 us (2%)
  between operations  5.33 us (1%)
    all_to_all x8, waiting for transfers between devices, exchange(): lax.all_to_all(blocks, 'seq', split_axis=0, concat_axis=0, axis_index_gro...  122 us
    all_to_all x8, starting transfers between devices, exchange(): lax.all_to_all(blocks, 'seq', split_axis=0, concat_axis=0, axis_index_gro...  72.2 us
    pallas_call x2, Pallas kernels, raw_path(): pl.pallas_call(kernel, grid=(steps,), in_specs=in_specs, out_specs=out_sp...  47.2 us
    pallas_call x2, Pallas kernels, conv_path(): pl.pallas_call(kernel, grid=(steps,), in_specs=[resident(), resident(), p...  44.6 us
    ppermute x7, starting transfers between devices, send_low(): lax.ppermute(ready[d], 'seq', [(i, i ^ d) for i in range(live)])  24.3 us
    pallas_call x2, Pallas kernels, finish(): pl.pallas_call(kernel, grid=(count,), in_specs=[pl.BlockSpec((3, rows, bl...  19.8 us
    pallas_call x2, Pallas kernels, short_sums(): pl.pallas_call(kernel, grid=(count,), in_specs=in_specs + [untouched() fo...  16.5 us
    pallas_call x2, Pallas kernels, gates(): pl.pallas_call(kernel, grid=(count,), in_specs=[pl.BlockSpec((3, rows, bl...  13.8 us
  transfers between devices with their start and end apart: 17, of which 7 were waited for; matrix products, arithmetic and copies ran while one was open for 6% of the time, Pallas kernels for 34%

profile of v5, /device:TPU:0, one launch (start us, length us, event | category | flops | bytes accessed | tf_op | source)
XLA Modules:
  0.0 423.1 jit_solution(16968353813993030122)
XLA Ops:
  1.7 4.9 %collective-permute-start = (bf16[3,8,4096]{2,1,0:T(8,128)(2,1)S(1)}, bf16[3,8,4096]{2,1,0:T(8,128)(2,1)S(1)}, u32[]{:S(2)}, u32[]{:S(2)}) collective-permute-start(bf16[3,8,4096]{2,1,0:T(8,128)(2,1)S(1)} %get-tuple-element.50), channel_id=1, source_target_pairs={{0,2},{2,4},{4,6},{6,8},{8,10},{10,12},{12,14},{14,16},{16,18},{18... | collective-permute-start | bytes 589832 | tf_op jit(solution)/shard_map/ppermute | solution.py:780
  6.6 4.1 collective-permute-done.b_ref
  11.4 6.2 %gates.3 = (bf16[16,2,256,128]{3,2,1,0:T(8,128)(2,1)}, f32[1,2048]{1,0:T(1,128)}) custom-call(bf16[3,256,4096]{2,1,0:T(8,128)(2,1)} %x_ref.15, bf16[3,8,4096]{2,1,0:T(8,128)(2,1)} %copy-done.2, bf16[256,4096]{1,0:T(8,128)(2,1)} %go_ref.11, f32[3,7,4096]{2,1,0:T(8,128)} %w_ref.11), custom_call_target="tpu_custom_call" | custom-call | flops 60000000 | bytes 7000000 | tf_op jit(solution)/shard_map/gates/pallas_call | solution.py:616
  17.6 7.9 %all-to-all-start.1 = ((bf16[16,2,256,128]{3,2,1,0:T(8,128)(2,1)}), bf16[16,2,256,128]{3,2,1,0:T(8,128)(2,1)S(1)}, u32[]{:S(2)}, u32[]{:S(2)}) async-start(bf16[16,2,256,128]{3,2,1,0:T(8,128)(2,1)} %get-tuple-element.28), calls=%async_computation.1 | async-start | bytes 4194304 | tf_op jit(solution)/shard_map/all_to_all | solution.py:784
  25.5 7.5 %gates.2 = (bf16[16,2,256,128]{3,2,1,0:T(8,128)(2,1)}, f32[1,2048]{1,0:T(1,128)}, f32[2,256,2048]{2,1,0:T(8,128)}) custom-call(bf16[3,256,4096]{2,1,0:T(8,128)(2,1)} %x_ref.15, bf16[3,8,4096]{2,1,0:T(8,128)(2,1)} %copy-done.2, bf16[256,4096]{1,0:T(8,128)(2,1)} %go_ref.11, f32[3,7,4096]{2,1,0:T(8,128)} %w_ref.11), custom_call_target="tpu_custom_call" | custom-call | flops 60000000 | bytes 7000000 | tf_op jit(solution)/shard_map/gates/pallas_call | solution.py:616
  33.0 34.9 %all-to-all-done.1.refs_0_.x_ref = bf16[16,2,256,128]{3,2,1,0:T(8,128)(2,1)S(1)} async-done(((bf16[16,2,256,128]{3,2,1,0:T(8,128)(2,1)}), bf16[16,2,256,128]{3,2,1,0:T(8,128)(2,1)S(1)}, u32[]{:S(2)}, u32[]{:S(2)}) %all-to-all-start.1) | async-done | bytes 2097184 | tf_op jit(solution)/shard_map/all_to_all | solution.py:784
  67.9 9.9 %all-to-all-start = ((bf16[16,2,256,128]{3,2,1,0:T(8,128)(2,1)}), bf16[16,2,256,128]{3,2,1,0:T(8,128)(2,1)}, u32[]{:S(2)}, u32[]{:S(2)}) async-start(bf16[16,2,256,128]{3,2,1,0:T(8,128)(2,1)} %get-tuple-element.27), calls=%async_computation | async-start | bytes 4194304 | tf_op jit(solution)/shard_map/all_to_all | solution.py:784
  77.8 4.3 %pack_taps.3.refs_4_ = bf16[16,512,128]{2,1,0:T(8,128)(2,1)} custom-call(f32[512,4096]{1,0:T(8,128)} %x_ref.11), custom_call_target="tpu_custom_call" | custom-call | flops 1000000 | bytes 6000000 | tf_op jit(solution)/shard_map/pack_taps/pallas_call | solution.py:473
  83.8 4.1 multiply_subtract_fusion
  90.3 5.5 %fusion.refs_2_.inv_ref = bf16[17,512,256]{2,1,0:T(8,128)(2,1)} fusion(f32[17,256,256]{2,1,0:T(8,128)} %get-tuple-element.61, f32[17,256,256]{2,1,0:T(8,128)S(1)} %get-tuple-element.59), kind=kLoop, calls=%fused_computation.1 | loop fusion | flops 6684672 | bytes 13369344 | tf_op jit(solution)/shard_map/convert_element_type | solution.py:164
  95.8 23.3 %raw_path.2 = (f32[17,2,256,256]{3,2,1,0:T(8,128)}, bf16[8,2,512,128]{3,2,1,0:T(8,128)(2,1)}, f32[8,128]{1,0:T(8,128)}, bf16[16,512,128]{2,1,0:T(8,128)(2,1)}) custom-call(bf16[16,2,256,128]{3,2,1,0:T(8,128)(2,1)S(1)} %all-to-all-done.1.refs_0_.x_ref, bf16[17,512,256]{2,1,0:T(8,128)(2,1)} %pad_maximum_fusion.refs_1_.fwd_ref, ...), custom_call_target="tpu_custom_call" | custom-call | flops 20000000000 | bytes 25000000 | tf_op jit(solution)/shard_map/raw_path/pallas_call | solution.py:343
  120.4 9.9 %all-to-all-start.4 = ((bf16[16,512,128]{2,1,0:T(8,128)(2,1)}), bf16[16,512,128]{2,1,0:T(8,128)(2,1)}, u32[]{:S(2)}, u32[]{:S(2)}) async-start(bf16[16,512,128]{2,1,0:T(8,128)(2,1)} %get-tuple-element.32), calls=%async_computation.4 | async-start | bytes 4194304 | tf_op jit(solution)/shard_map/all_to_all | solution.py:784
  130.3 4.3 %pack_taps.2.refs_4_ = bf16[16,512,128]{2,1,0:T(8,128)(2,1)} custom-call(f32[512,4096]{1,0:T(8,128)} %x_ref.11), custom_call_target="tpu_custom_call" | custom-call | flops 1000000 | bytes 6000000 | tf_op jit(solution)/shard_map/pack_taps/pallas_call | solution.py:473
  134.5 23.9 %raw_path.3 = (f32[17,2,256,256]{3,2,1,0:T(8,128)}, bf16[8,2,512,128]{3,2,1,0:T(8,128)(2,1)}, f32[8,128]{1,0:T(8,128)}, bf16[16,512,128]{2,1,0:T(8,128)(2,1)}) custom-call(bf16[16,2,256,128]{3,2,1,0:T(8,128)(2,1)} %all-to-all-done.refs_0_.x_ref, bf16[17,512,256]{2,1,0:T(8,128)(2,1)} %pad_maximum_fusion.refs_1_.fwd_ref, ...), custom_call_target="tpu_custom_call", output_to_operand_aliasing={{1}: (5, {})} | custom-call | flops 20000000000 | bytes 25000000 | tf_op jit(solution)/shard_map/raw_path/pallas_call | solution.py:343
  158.5 14.4 %all-to-all-done.4.refs_10_ = bf16[16,512,128]{2,1,0:T(8,128)(2,1)} async-done(((bf16[16,512,128]{2,1,0:T(8,128)(2,1)}), bf16[16,512,128]{2,1,0:T(8,128)(2,1)}, u32[]{:S(2)}, u32[]{:S(2)}) %all-to-all-start.4) | async-done | bytes 2097184 | tf_op jit(solution)/shard_map/all_to_all | solution.py:784
  172.9 9.8 %all-to-all-start.2 = ((bf16[16,512,128]{2,1,0:T(8,128)(2,1)}), bf16[16,512,128]{2,1,0:T(8,128)(2,1)}, u32[]{:S(2)}, u32[]{:S(2)}) async-start(bf16[16,512,128]{2,1,0:T(8,128)(2,1)} %get-tuple-element.30), calls=%async_computation.2 | async-start | bytes 4194304 | tf_op jit(solution)/shard_map/all_to_all | solution.py:784
  185.6 21.9 %conv_path.3 = bf16[16,2,264,128]{3,2,1,0:T(8,128)(2,1)} custom-call(bf16[16,2,256,128]{3,2,1,0:T(8,128)(2,1)S(1)} %copy-done.1, bf16[32,256,128]{2,1,0:T(8,128)(2,1)} %bitcast.6.h_ref, f32[17,2,256,256]{3,2,1,0:T(8,128)} %get-tuple-element.33.spec_ref, f32[1,128]{1,0:T(1,128)} %get-tuple-element.63.skip_ref, ...), custom_call_target="tpu_custom_call" | custom-call | flops 20000000000 | bytes 25000000 | tf_op jit(solution)/shard_map/conv_path/pallas_call | solution.py:412
  207.6 17.8 %all-to-all-done.2.refs_11_ = bf16[16,512,128]{2,1,0:T(8,128)(2,1)} async-done(((bf16[16,512,128]{2,1,0:T(8,128)(2,1)}), bf16[16,512,128]{2,1,0:T(8,128)(2,1)}, u32[]{:S(2)}, u32[]{:S(2)}) %all-to-all-start.2) | async-done | bytes 2097184 | tf_op jit(solution)/shard_map/all_to_all | solution.py:784
  225.4 9.7 %all-to-all-start.5 = ((bf16[16,2,264,128]{3,2,1,0:T(8,128)(2,1)}), bf16[16,2,264,128]{3,2,1,0:T(8,128)(2,1)}, u32[]{:S(2)}, u32[]{:S(2)}) async-start(bf16[16,2,264,128]{3,2,1,0:T(8,128)(2,1)} %conv_path.3), calls=%async_computation.5 | async-start | bytes 4325376 | tf_op jit(solution)/shard_map/all_to_all | solution.py:784
  235.1 22.7 %conv_path.2 = bf16[16,2,264,128]{3,2,1,0:T(8,128)(2,1)} custom-call(bf16[16,2,256,128]{3,2,1,0:T(8,128)(2,1)} %all-to-all-done.refs_0_.x_ref, bf16[32,256,128]{2,1,0:T(8,128)(2,1)} %bitcast.4.h_ref, f32[17,2,256,256]{3,2,1,0:T(8,128)} %get-tuple-element.31.spec_ref, f32[1,128]{1,0:T(1,128)} %get-tuple-element.64.skip_ref, ...), custom_call_target="tpu_custom_call" | custom-call | flops 20000000000 | bytes 25000000 | tf_op jit(solution)/shard_map/conv_path/pallas_call | solution.py:412
  257.7 21.1 %all-to-all-done.5.y_ref = bf16[16,2,264,128]{3,2,1,0:T(8,128)(2,1)} async-done(((bf16[16,2,264,128]{3,2,1,0:T(8,128)(2,1)}), bf16[16,2,264,128]{3,2,1,0:T(8,128)(2,1)}, u32[]{:S(2)}, u32[]{:S(2)}) %all-to-all-start.5) | async-done | bytes 2162720 | tf_op jit(solution)/shard_map/all_to_all | solution.py:784
  278.9 9.8 %all-to-all-start.3 = ((bf16[16,2,264,128]{3,2,1,0:T(8,128)(2,1)}), bf16[16,2,264,128]{3,2,1,0:T(8,128)(2,1)}, u32[]{:S(2)}, u32[]{:S(2)}) async-start(bf16[16,2,264,128]{3,2,1,0:T(8,128)(2,1)} %conv_path.2), calls=%async_computation.3 | async-start | bytes 4325376 | tf_op jit(solution)/shard_map/all_to_all | solution.py:784
  291.0 8.6 %short_sums.2.refs_1_ = bf16[16,2,24,128]{3,2,1,0:T(8,128)(2,1)} custom-call(bf16[3,256,4096]{2,1,0:T(8,128)(2,1)} %x_ref.15, bf16[3,8,4096]{2,1,0:T(8,128)(2,1)} %copy-done.2, bf16[256,4096]{1,0:T(8,128)(2,1)} %go_ref.11, f32[3,7,4096]{2,1,0:T(8,128)} %w_ref.11, bf16[16,2,264,128]{3,2,1,0:T(8,128)(2,1)} %all-to-all-done.5.y_ref, ...), custom_call_target="tpu_custom_call" | custom-call | flops 150000000 | bytes 8000000 | tf_op jit(solution)/shard_map/short_sums/pallas_call | solution.py:694
  299.6 32.7 %all-to-all-done.3.y_ref = bf16[16,2,264,128]{3,2,1,0:T(8,128)(2,1)} async-done(((bf16[16,2,264,128]{3,2,1,0:T(8,128)(2,1)}), bf16[16,2,264,128]{3,2,1,0:T(8,128)(2,1)}, u32[]{:S(2)}, u32[]{:S(2)}) %all-to-all-start.3) | async-done | bytes 2162720 | tf_op jit(solution)/shard_map/all_to_all | solution.py:784
  332.3 7.9 %short_sums.3 = bf16[16,2,24,128]{3,2,1,0:T(8,128)(2,1)} custom-call(bf16[3,256,4096]{2,1,0:T(8,128)(2,1)} %x_ref.15, bf16[3,8,4096]{2,1,0:T(8,128)(2,1)} %copy-done.2, bf16[256,4096]{1,0:T(8,128)(2,1)} %go_ref.11, f32[3,7,4096]{2,1,0:T(8,128)} %w_ref.11, bf16[16,2,264,128]{3,2,1,0:T(8,128)(2,1)} %all-to-all-done.3.y_ref, ...), custom_call_target="tpu_custom_call", output_to_operand_aliasing={{}: (7, {})} | custom-call | flops 150000000 | bytes 8000000 | tf_op jit(solution)/shard_map/short_sums/pallas_call | solution.py:694
  340.2 11.1 %all-to-all-start.6 = ((bf16[16,2,24,128]{3,2,1,0:T(8,128)(2,1)}), bf16[16,2,24,128]{3,2,1,0:T(8,128)(2,1)S(1)}, u32[]{:S(2)}, u32[]{:S(2)}) async-start(bf16[16,2,24,128]{3,2,1,0:T(8,128)(2,1)} %short_sums.3), calls=%async_computation.6 | async-start | bytes 393216 | tf_op jit(solution)/shard_map/all_to_all | solution.py:784
  365.2 3.8 collective-permute-start.5
  377.2 4.2 all-to-all-start.7
  383.5 4.6 %collective-permute-start.6 = (bf16[2,512,128]{2,1,0:T(8,128)(2,1)}, bf16[2,512,128]{2,1,0:T(8,128)(2,1)}, u32[]{:S(2)}, u32[]{:S(2)}) collective-permute-start(bf16[2,512,128]{2,1,0:T(8,128)(2,1)} %get-tuple-element.53), channel_id=1, source_target_pairs={{0,10},{2,8},{4,14},{6,12},{8,2},{10,0},{12,6},{14,4},{1,11},{3,9}... | collective-permute-start | bytes 786440 | tf_op jit(solution)/shard_map/ppermute | solution.py:853
  394.8 9.9 %finish.2 = (bf16[256,4096]{1,0:T(8,128)(2,1)}, bf16[3,256,4096]{2,1,0:T(8,128)(2,1)}) custom-call(bf16[3,256,4096]{2,1,0:T(8,128)(2,1)} %x_ref.15, bf16[3,8,4096]{2,1,0:T(8,128)(2,1)} %copy-done.2, bf16[4,8,4096]{2,1,0:T(8,128)(2,1)} %copy-done.3, bf16[256,4096]{1,0:T(8,128)(2,1)} %go_ref.11, f32[3,7,4096]{2,1,0:T(8,128)} %w_ref.11, ...), custom_call_target="tpu_custom_call" | custom-call | flops 150000000 | bytes 12000000 | tf_op jit(solution)/shard_map/finish/pallas_call | solution.py:747
  404.7 9.9 %finish.3 = (bf16[256,4096]{1,0:T(8,128)(2,1)}, bf16[3,256,4096]{2,1,0:T(8,128)(2,1)}) custom-call(bf16[3,256,4096]{2,1,0:T(8,128)(2,1)} %x_ref.15, bf16[3,8,4096]{2,1,0:T(8,128)(2,1)} %copy-done.2, bf16[4,8,4096]{2,1,0:T(8,128)(2,1)} %copy-done.3, bf16[256,4096]{1,0:T(8,128)(2,1)} %go_ref.11, ...), custom_call_target="tpu_custom_call", output_to_operand_aliasing={{0}: (6, {}), {1}: (7, {})} | custom-call | flops 150000000 | bytes 12000000 | tf_op jit(solution)/shard_map/finish/pallas_call | solution.py:747
  414.7 8.4 %scale_taps.1 = (f32[512,4096]{1,0:T(8,128)}, f32[3,7,4096]{2,1,0:T(8,128)}, f32[1,4096]{1,0:T(1,128)}) custom-call(bf16[16,2,24,128]{3,2,1,0:T(8,128)(2,1)} %all-to-all-done.7.refs_0_, s32[1,2]{1,0:T(1,128)} %add_bitcast_fusion.refs_3_.refs_1_, bf16[2,512,128]{2,1,0:T(8,128)(2,1)S(1)} %get-tuple-element.58.refs_2_, ...), custom_call_target="tpu_custom_call" | custom-call | tf_op jit(solution)/shard_map/scale_taps/pallas_call | solution.py:547
  (47 shorter events, 38.7 us)
Async XLA Ops:
  1.7 9.0 %collective-permute-start = (bf16[3,8,4096]{2,1,0:T(8,128)(2,1)S(1)}, bf16[3,8,4096]{2,1,0:T(8,128)(2,1)S(1)}, u32[]{:S(2)}, u32[]{:S(2)}) collective-permute-start(bf16[3,8,4096]{2,1,0:T(8,128)(2,1)S(1)} %get-tuple-element.50), channel_id=1, source_target_pairs={{0,2},{2,4},{4,6},{6,8},{8,10},{10,12},{12,14},{14,16},{16,18},{18... | collective-permute-start | bytes 589832 | tf_op jit(solution)/shard_map/ppermute | solution.py:780
  10.7 0.7 copy-start.2
  17.6 50.3 %all-to-all-start.1 = ((bf16[16,2,256,128]{3,2,1,0:T(8,128)(2,1)}), bf16[16,2,256,128]{3,2,1,0:T(8,128)(2,1)S(1)}, u32[]{:S(2)}, u32[]{:S(2)}) async-start(bf16[16,2,256,128]{3,2,1,0:T(8,128)(2,1)} %get-tuple-element.28), calls=%async_computation.1 | async-start | bytes 4194304 | tf_op jit(solution)/shard_map/all_to_all | solution.py:784
  67.9 27.9 %copy-start = (bf16[16,2,256,128]{3,2,1,0:T(8,128)(2,1)}, bf16[16,2,256,128]{3,2,1,0:T(8,128)(2,1)S(1)}, u32[]{:S(2)}) copy-start(bf16[16,2,256,128]{3,2,1,0:T(8,128)(2,1)S(1)} %all-to-all-done.1.refs_0_.x_ref) | copy-start | bytes 6291460
  67.9 52.5 %all-to-all-start = ((bf16[16,2,256,128]{3,2,1,0:T(8,128)(2,1)}), bf16[16,2,256,128]{3,2,1,0:T(8,128)(2,1)}, u32[]{:S(2)}, u32[]{:S(2)}) async-start(bf16[16,2,256,128]{3,2,1,0:T(8,128)(2,1)} %get-tuple-element.27), calls=%async_computation | async-start | bytes 4194304 | tf_op jit(solution)/shard_map/all_to_all | solution.py:784
  120.4 52.5 %all-to-all-start.4 = ((bf16[16,512,128]{2,1,0:T(8,128)(2,1)}), bf16[16,512,128]{2,1,0:T(8,128)(2,1)}, u32[]{:S(2)}, u32[]{:S(2)}) async-start(bf16[16,512,128]{2,1,0:T(8,128)(2,1)} %get-tuple-element.32), calls=%async_computation.4 | async-start | bytes 4194304 | tf_op jit(solution)/shard_map/all_to_all | solution.py:784
  172.9 52.5 %all-to-all-start.2 = ((bf16[16,512,128]{2,1,0:T(8,128)(2,1)}), bf16[16,512,128]{2,1,0:T(8,128)(2,1)}, u32[]{:S(2)}, u32[]{:S(2)}) async-start(bf16[16,512,128]{2,1,0:T(8,128)(2,1)} %get-tuple-element.30), calls=%async_computation.2 | async-start | bytes 4194304 | tf_op jit(solution)/shard_map/all_to_all | solution.py:784
  184.0 1.6 copy-start.1
  225.4 53.5 %all-to-all-start.5 = ((bf16[16,2,264,128]{3,2,1,0:T(8,128)(2,1)}), bf16[16,2,264,128]{3,2,1,0:T(8,128)(2,1)}, u32[]{:S(2)}, u32[]{:S(2)}) async-start(bf16[16,2,264,128]{3,2,1,0:T(8,128)(2,1)} %conv_path.3), calls=%async_computation.5 | async-start | bytes 4325376 | tf_op jit(solution)/shard_map/all_to_all | solution.py:784
  278.9 53.4 %all-to-all-start.3 = ((bf16[16,2,264,128]{3,2,1,0:T(8,128)(2,1)}), bf16[16,2,264,128]{3,2,1,0:T(8,128)(2,1)}, u32[]{:S(2)}, u32[]{:S(2)}) async-start(bf16[16,2,264,128]{3,2,1,0:T(8,128)(2,1)} %conv_path.2), calls=%async_computation.3 | async-start | bytes 4325376 | tf_op jit(solution)/shard_map/all_to_all | solution.py:784
  289.5 93.9 %collective-permute-start.1 = (bf16[4,8,4096]{2,1,0:T(8,128)(2,1)S(1)}, bf16[4,8,4096]{2,1,0:T(8,128)(2,1)S(1)}, u32[]{:S(2)}, u32[]{:S(2)}) collective-permute-start(bf16[4,8,4096]{2,1,0:T(8,128)(2,1)S(1)} %pad_maximum_fusion.1), channel_id=1, source_target_pairs={{2,0},{4,2},{6,4},{8,6},{10,8},{12,10},{14,12},{16,14},{18,16},{20... | collective-permute-start | bytes 786440 | tf_op jit(solution)/shard_map/ppermute | solution.py:780
  332.3 19.0 %copy-start.5 = (f32[8,128]{1,0:T(8,128)S(1)}, f32[8,128]{1,0:T(8,128)}, u32[]{:S(2)}) copy-start(f32[8,128]{1,0:T(8,128)} %get-tuple-element.39) | copy-start | bytes 12292
  332.3 19.6 %copy-start.4 = (f32[8,128]{1,0:T(8,128)S(1)}, f32[8,128]{1,0:T(8,128)}, u32[]{:S(2)}) copy-start(f32[8,128]{1,0:T(8,128)} %get-tuple-element.38) | copy-start | bytes 12292
  340.2 28.9 %all-to-all-start.6 = ((bf16[16,2,24,128]{3,2,1,0:T(8,128)(2,1)}), bf16[16,2,24,128]{3,2,1,0:T(8,128)(2,1)S(1)}, u32[]{:S(2)}, u32[]{:S(2)}) async-start(bf16[16,2,24,128]{3,2,1,0:T(8,128)(2,1)} %short_sums.3), calls=%async_computation.6 | async-start | bytes 393216 | tf_op jit(solution)/shard_map/all_to_all | solution.py:784
  356.0 32.0 %collective-permute-start.2 = (bf16[2,512,128]{2,1,0:T(8,128)(2,1)S(1)}, bf16[2,512,128]{2,1,0:T(8,128)(2,1)S(1)}, u32[]{:S(2)}, u32[]{:S(2)}) collective-permute-start(bf16[2,512,128]{2,1,0:T(8,128)(2,1)S(1)} %get-tuple-element.57), channel_id=1, source_target_pairs={{0,2},{2,0},{4,6},{6,4},{8,10},{10,8},{12,14},{14,12},{1,3},{3,1},... | collective-permute-start | bytes 786440 | tf_op jit(solution)/shard_map/ppermute | solution.py:853
  359.8 31.6 %collective-permute-start.3 = (bf16[2,512,128]{2,1,0:T(8,128)(2,1)S(1)}, bf16[2,512,128]{2,1,0:T(8,128)(2,1)S(1)}, u32[]{:S(2)}, u32[]{:S(2)}) collective-permute-start(bf16[2,512,128]{2,1,0:T(8,128)(2,1)S(1)} %get-tuple-element.56), channel_id=1, source_target_pairs={{0,4},{2,6},{4,0},{6,2},{8,12},{10,14},{12,8},{14,10},{1,5},{3,7},... | collective-permute-start | bytes 786440 | tf_op jit(solution)/shard_map/ppermute | solution.py:853
  363.2 51.4 %collective-permute-start.4 = (bf16[2,512,128]{2,1,0:T(8,128)(2,1)}, bf16[2,512,128]{2,1,0:T(8,128)(2,1)S(1)}, u32[]{:S(2)}, u32[]{:S(2)}) collective-permute-start(bf16[2,512,128]{2,1,0:T(8,128)(2,1)} %get-tuple-element.55), channel_id=1, source_target_pairs={{0,6},{2,4},{4,2},{6,0},{8,14},{10,12},{12,10},{14,8},{1,7},{3,5},... | collective-permute-start | bytes 786440 | tf_op jit(solution)/shard_map/ppermute | solution.py:853
  365.2 49.4 %collective-permute-start.5 = (bf16[2,512,128]{2,1,0:T(8,128)(2,1)}, bf16[2,512,128]{2,1,0:T(8,128)(2,1)S(1)}, u32[]{:S(2)}, u32[]{:S(2)}) collective-permute-start(bf16[2,512,128]{2,1,0:T(8,128)(2,1)} %get-tuple-element.54), channel_id=1, source_target_pairs={{0,8},{2,10},{4,12},{6,14},{8,0},{10,2},{12,4},{14,6},{1,9},{3,11}... | collective-permute-start | bytes 786440 | tf_op jit(solution)/shard_map/ppermute | solution.py:853
  377.2 37.5 %all-to-all-start.7 = ((bf16[16,2,24,128]{3,2,1,0:T(8,128)(2,1)}), bf16[16,2,24,128]{3,2,1,0:T(8,128)(2,1)}, u32[]{:S(2)}, u32[]{:S(2)}) async-start(bf16[16,2,24,128]{3,2,1,0:T(8,128)(2,1)} %broadcast_in_dim.37), calls=%async_computation.7 | async-start | bytes 393216 | tf_op jit(solution)/shard_map/all_to_all | solution.py:784
  383.5 8.0 %copy-start.3 = (bf16[4,8,4096]{2,1,0:T(8,128)(2,1)}, bf16[4,8,4096]{2,1,0:T(8,128)(2,1)S(1)}, u32[]{:S(2)}) copy-start(bf16[4,8,4096]{2,1,0:T(8,128)(2,1)S(1)} %collective-permute-done.1.n_ref) | copy-start | bytes 786436
  383.5 31.2 %collective-permute-start.6 = (bf16[2,512,128]{2,1,0:T(8,128)(2,1)}, bf16[2,512,128]{2,1,0:T(8,128)(2,1)}, u32[]{:S(2)}, u32[]{:S(2)}) collective-permute-start(bf16[2,512,128]{2,1,0:T(8,128)(2,1)} %get-tuple-element.53), channel_id=1, source_target_pairs={{0,10},{2,8},{4,14},{6,12},{8,2},{10,0},{12,6},{14,4},{1,11},{3,9}... | collective-permute-start | bytes 786440 | tf_op jit(solution)/shard_map/ppermute | solution.py:853
  388.0 26.6 %collective-permute-start.7 = (bf16[2,512,128]{2,1,0:T(8,128)(2,1)}, bf16[2,512,128]{2,1,0:T(8,128)(2,1)}, u32[]{:S(2)}, u32[]{:S(2)}) collective-permute-start(bf16[2,512,128]{2,1,0:T(8,128)(2,1)} %get-tuple-element.52), channel_id=1, source_target_pairs={{0,12},{2,14},{4,8},{6,10},{8,4},{10,6},{12,0},{14,2},{1,13},{3,15... | collective-permute-start | bytes 786440 | tf_op jit(solution)/shard_map/ppermute | solution.py:853
  391.4 23.3 %collective-permute-start.8 = (bf16[2,512,128]{2,1,0:T(8,128)(2,1)}, bf16[2,512,128]{2,1,0:T(8,128)(2,1)}, u32[]{:S(2)}, u32[]{:S(2)}) collective-permute-start(bf16[2,512,128]{2,1,0:T(8,128)(2,1)} %get-tuple-element.51), channel_id=1, source_target_pairs={{0,14},{2,12},{4,10},{6,8},{8,6},{10,4},{12,2},{14,0},{1,15},{3,13... | collective-permute-start | bytes 786440 | tf_op jit(solution)/shard_map/ppermute | solution.py:853

commit v6 on v5

--- a/solution.py
+++ b/solution.py
@@ -431,9 +431,9 @@
     )(both, taps, spec, skip, fwd, inv)
 
 
-def plan_lanes(width, chans):
+def plan_lanes(width, chans, most=512):
     block = max(chans, LANES)
-    while block < 512 and width % (2 * block) == 0:
+    while block < most and width % (2 * block) == 0:
         block *= 2
     return block
 
@@ -484,13 +484,14 @@
 def scale_taps(small, where, lows, shared, shards, live, param_count):
     parts, rows, chans = lows[0].shape[-3:]
     width = shards * chans
-    block = plan_lanes(width, chans)
+    block = plan_lanes(width, chans, 1024)
     while (live * chans) % block:
         block //= 2
     count = width // block
     groups = block // chans
     split = live // groups
     listed = len(lows) > 1
+    sides = small.shape[0] // shards
 
     def kernel(*refs):
         small_ref, at_ref = refs[:2]
@@ -498,14 +499,17 @@
         o_ref, short_ref, bias_ref = refs[-3:]
         q = pl.program_id(0)
         i = pl.program_id(1)
-        total = jnp.zeros((SUMS, min(chans, LANES)), F32)
-        for j in range(shards):
-            total = total + small_ref[j, 0, :, pl.ds(0, min(chans, LANES))].astype(F32)
-        total = total[SUMS - 2 : SUMS - 1, 0:1] + total[SUMS - 1 :, 0:1]
+        lanes = min(chans, LANES)
+        total = jnp.sum(small_ref[:, 0, SUMS - 8 :, pl.ds(0, lanes)].astype(F32), axis=0)
+        total = total[6:7, 0:1] + total[7:8, 0:1]
         clip = 1.0 / jnp.sqrt(jnp.broadcast_to(total, (1, LANES)) / param_count + 1e-06)
         gain = clip * at_ref[0, 0].astype(F32)
         for c in range(0, block, LANES):
-            lines = take(small_ref, (q,), slice(None), c, LANES, i * groups) * clip
+            lines = [
+                small_ref[(i * groups + (c + b) // chans) * sides + at_ref[0, 2], q, :, pl.ds((c + b) % chans, lanes)]
+                for b in range(0, LANES, lanes)
+            ]
+            lines = jnp.concatenate([v.astype(F32) for v in lines], axis=1) * clip
             for j in range(3):
                 short_ref[j, :, pl.ds(c, LANES)] = lines[j * TAPS : (j + 1) * TAPS]
             bias_ref[:, pl.ds(c, LANES)] = lines[3 * TAPS : 3 * TAPS + 1]
@@ -707,18 +711,19 @@
     )(*ins, *earlier)
 
 
-def finish(streams, before, after, grad_out, short_filter, back, earlier, shards, part, parts):
+def finish(streams, before, after, grad_out, short_filter, back, earlier, shards, part, parts, piece, pieces):
     _, rows, full = streams.shape
     width = full // parts
     chans = width // shards
     block = plan_lanes(width, chans)
     count = width // block
+    steps = count // pieces
     groups = block // chans
     chunk = math.gcd(rows, 64)
 
     def kernel(x_ref, b_ref, n_ref, go_ref, w_ref, y_ref, *refs):
         o_ref, gs_ref, ext_ref, pre_ref = refs[-4:]
-        base = pl.program_id(0) * groups
+        base = (piece * steps + pl.program_id(0)) * groups
         for c in range(0, block, LANES):
             cs = pl.ds(c, LANES)
             fill_ext(ext_ref, x_ref, b_ref, n_ref, cs, rows)
@@ -742,11 +747,11 @@
                         total = total + w_ref[i, j : j + 1, cs] * pre_ref[i, pl.ds(r + j, chunk), :]
                     gs_ref[i, pl.ds(r, chunk), cs] = total.astype(BF16)
 
-    at = lambda i: part * count + i
+    at = lambda i: part * count + piece * steps + i
     ins = [streams, before, after, grad_out, short_filter, back]
     return pl.pallas_call(
         kernel,
-        grid=(count,),
+        grid=(steps,),
         in_specs=[
             pl.BlockSpec((3, rows, block), lambda i: (0, 0, at(i))),
             pl.BlockSpec((3, HALO, block), lambda i: (0, 0, at(i))),
@@ -807,7 +812,7 @@
     fold = 2 * live <= shards
     mine = lax.axis_index("seq")
     is_low = mine < live
-    where = jnp.stack([is_low.astype(jnp.int32), mine % live]).reshape(1, 2)
+    where = jnp.stack([is_low.astype(jnp.int32), mine % live, lax.axis_index("chan")]).reshape(1, 3)
     fwd, inv = turn_tables(shards, rows)
     before = shift(streams[:, rows - HALO :], "seq", 1)
     after = shift(jnp.concatenate([streams[:, :HALO], grad_out[None, :HALO]], axis=0), "seq", -1)
@@ -836,6 +841,8 @@
         squares = squares + jnp.sum(out[2])
         shared.append(exchange(out[3] if fold else packed[p]))
     back = []
+    if parts > 1:
+        skips[-1], squares = lax.optimization_barrier((skips[-1], squares))
     for p in range(parts):
         taps = shared[p].reshape(shards * tap_rows // rows, rows, chans)
         sent = conv_path(both[p], taps, spec[p], skips[p], fwd, inv)
@@ -859,19 +866,23 @@
         sums = [short_sums(streams, before, grad_out, short_filter, *terms, shards, p, parts)]
         if p == 0 and fold:
             send_low(live // 2 + 1, live, back[0])
-        done = finish(streams, before, after, grad_out, short_filter, back[p], done, shards, p, parts)
+        pieces = 2 if p and span // plan_lanes(span, chans) % 2 == 0 else 1
+        for piece in range(pieces):
+            given = (streams, before, after, grad_out, short_filter, back[p], done)
+            done = finish(*given, shards, p, parts, piece, pieces)
     output, grad_streams = done
     sums = sums[0]
     if not fold:
         lows.append(exchange(following(low, back[-1])))
         sums = following(sums, lows[0])
     mine_sums = jnp.sum(exchange(sums).astype(F32), axis=0)
-    local_sq = lax.psum(squares + jnp.sum(mine_sums * mine_sums), "chan")
+    local_sq = squares + jnp.sum(mine_sums * mine_sums)
     upper_sq = lax.reduce_precision(local_sq, 8, 7)
     line = lax.broadcasted_iota(jnp.int32, mine_sums.shape, 1)
     mine_sums = jnp.where(line == SUMS - 2, upper_sq, mine_sums)
     mine_sums = jnp.where(line == SUMS - 1, local_sq - upper_sq, mine_sums).astype(BF16)
-    small = exchange(jnp.broadcast_to(mine_sums[None], (shards,) + mine_sums.shape))
+    copies = jnp.broadcast_to(mine_sums[None], (shards * lax.axis_size("chan"),) + mine_sums.shape)
+    small = lax.all_to_all(copies, ("seq", "chan"), split_axis=0, concat_axis=0, tiled=True)
     param_count = LF * D + (3 * TAPS + 1) * D
     filter_grad, short_grad, bias_grad = scale_taps(
         small, where, lows, shared if fold else [], shards, live, param_count

time: 426 us -> 425 us (level)
  waiting for transfers between devices: 126 us -> 132 us
    all_to_all x8 -> x7, starting transfers between devices: 72.2 us -> 66.8 us  [exchange(): lax.all_to_all(blocks, 'seq', split_axis=0, concat_axis=0, axis_index_gro...]
    all_to_all x8 -> x7, waiting for transfers between devices: 122 us -> 128 us  [exchange(): lax.all_to_all(blocks, 'seq', split_axis=0, concat_axis=0, axis_index_gro...]
    pallas_call x2 -> x3, Pallas kernels: 19.8 us -> 22.8 us  [finish(): pl.pallas_call(kernel, grid=(steps,), in_specs=[pl.BlockSpec((3, rows, bl...]
  transfers between devices with their start and end apart: 17 -> 17, of which waited for: 7 -> 8; matrix products, arithmetic and copies ran while one was open for 6% -> 6% of each run, Pallas kernels for 34% -> 33%
where the time goes in v6:
time: 425 us; the launch traced here: 422 us
  Pallas kernels  160 us (38%)
  waiting for transfers between devices  132 us (31%)
  starting transfers between devices  98.9 us (23%)
  other arithmetic  16.3 us (4%)
  local copies, waits for them, and re-layouts  10.5 us (2%)
    all_to_all x7, waiting for transfers between devices, exchange(): lax.all_to_all(blocks, 'seq', split_axis=0, concat_axis=0, axis_index_gro...  128 us
    all_to_all x7, starting transfers between devices, exchange(): lax.all_to_all(blocks, 'seq', split_axis=0, concat_axis=0, axis_index_gro...  66.8 us
    pallas_call x2, Pallas kernels, raw_path(): pl.pallas_call(kernel, grid=(steps,), in_specs=in_specs, out_specs=out_sp...  47.3 us
    pallas_call x2, Pallas kernels, conv_path(): pl.pallas_call(kernel, grid=(steps,), in_specs=[resident(), resident(), p...  44.6 us
    pallas_call x3, Pallas kernels, finish(): pl.pallas_call(kernel, grid=(steps,), in_specs=[pl.BlockSpec((3, rows, bl...  22.8 us
    ppermute x7, starting transfers between devices, send_low(): lax.ppermute(ready[d], 'seq', [(i, i ^ d) for i in range(live)])  22.7 us
    pallas_call x2, Pallas kernels, short_sums(): pl.pallas_call(kernel, grid=(count,), in_specs=in_specs + [untouched() fo...  16.5 us
    pallas_call x2, Pallas kernels, gates(): pl.pallas_call(kernel, grid=(count,), in_specs=[pl.BlockSpec((3, rows, bl...  13.8 us
  transfers between devices with their start and end apart: 17, of which 8 were waited for; matrix products, arithmetic and copies ran while one was open for 6% of the time, Pallas kernels for 33%

profile of v6, /device:TPU:0, one launch (start us, length us, event | category | flops | bytes accessed | tf_op | source)
XLA Modules:
  0.0 421.7 jit_solution(9518481234816931141)
XLA Ops:
  1.7 4.9 %collective-permute-start = (bf16[3,8,4096]{2,1,0:T(8,128)(2,1)S(1)}, bf16[3,8,4096]{2,1,0:T(8,128)(2,1)S(1)}, u32[]{:S(2)}, u32[]{:S(2)}) collective-permute-start(bf16[3,8,4096]{2,1,0:T(8,128)(2,1)S(1)} %get-tuple-element.58), channel_id=1, source_target_pairs={{0,2},{2,4},{4,6},{6,8},{8,10},{10,12},{12,14},{14,16},{16,18},{18... | collective-permute-start | bytes 589832 | tf_op jit(solution)/shard_map/ppermute | solution.py:785
  6.6 4.1 collective-permute-done.b_ref
  11.4 6.2 %gates.3 = (bf16[16,2,256,128]{3,2,1,0:T(8,128)(2,1)}, f32[1,2048]{1,0:T(1,128)}) custom-call(bf16[3,256,4096]{2,1,0:T(8,128)(2,1)} %x_ref.17, bf16[3,8,4096]{2,1,0:T(8,128)(2,1)} %copy-done.2, bf16[256,4096]{1,0:T(8,128)(2,1)} %go_ref.13, f32[3,7,4096]{2,1,0:T(8,128)} %w_ref.13), custom_call_target="tpu_custom_call" | custom-call | flops 60000000 | bytes 7000000 | tf_op jit(solution)/shard_map/gates/pallas_call | solution.py:620
  17.6 7.9 %all-to-all-start.1 = ((bf16[16,2,256,128]{3,2,1,0:T(8,128)(2,1)}), bf16[16,2,256,128]{3,2,1,0:T(8,128)(2,1)S(1)}, u32[]{:S(2)}, u32[]{:S(2)}) async-start(bf16[16,2,256,128]{3,2,1,0:T(8,128)(2,1)} %get-tuple-element.32), calls=%async_computation.1 | async-start | bytes 4194304 | tf_op jit(solution)/shard_map/all_to_all | solution.py:789
  25.5 7.6 %gates.2 = (bf16[16,2,256,128]{3,2,1,0:T(8,128)(2,1)}, f32[1,2048]{1,0:T(1,128)}, f32[2,256,2048]{2,1,0:T(8,128)}) custom-call(bf16[3,256,4096]{2,1,0:T(8,128)(2,1)} %x_ref.17, bf16[3,8,4096]{2,1,0:T(8,128)(2,1)} %copy-done.2, bf16[256,4096]{1,0:T(8,128)(2,1)} %go_ref.13, f32[3,7,4096]{2,1,0:T(8,128)} %w_ref.13), custom_call_target="tpu_custom_call" | custom-call | flops 60000000 | bytes 7000000 | tf_op jit(solution)/shard_map/gates/pallas_call | solution.py:620
  33.0 34.9 %all-to-all-done.1.refs_0_.x_ref = bf16[16,2,256,128]{3,2,1,0:T(8,128)(2,1)S(1)} async-done(((bf16[16,2,256,128]{3,2,1,0:T(8,128)(2,1)}), bf16[16,2,256,128]{3,2,1,0:T(8,128)(2,1)S(1)}, u32[]{:S(2)}, u32[]{:S(2)}) %all-to-all-start.1) | async-done | bytes 2097184 | tf_op jit(solution)/shard_map/all_to_all | solution.py:789
  67.9 9.9 %all-to-all-start = ((bf16[16,2,256,128]{3,2,1,0:T(8,128)(2,1)}), bf16[16,2,256,128]{3,2,1,0:T(8,128)(2,1)}, u32[]{:S(2)}, u32[]{:S(2)}) async-start(bf16[16,2,256,128]{3,2,1,0:T(8,128)(2,1)} %get-tuple-element.31), calls=%async_computation | async-start | bytes 4194304 | tf_op jit(solution)/shard_map/all_to_all | solution.py:789
  77.8 4.3 %pack_taps.3.refs_4_ = bf16[16,512,128]{2,1,0:T(8,128)(2,1)} custom-call(f32[512,4096]{1,0:T(8,128)} %x_ref.12), custom_call_target="tpu_custom_call" | custom-call | flops 1000000 | bytes 6000000 | tf_op jit(solution)/shard_map/pack_taps/pallas_call | solution.py:473
  83.8 4.1 multiply_subtract_fusion
  90.3 5.5 %fusion.refs_2_.inv_ref = bf16[17,512,256]{2,1,0:T(8,128)(2,1)} fusion(f32[17,256,256]{2,1,0:T(8,128)} %get-tuple-element.69, f32[17,256,256]{2,1,0:T(8,128)S(1)} %get-tuple-element.67), kind=kLoop, calls=%fused_computation.1 | loop fusion | flops 6684672 | bytes 13369344 | tf_op jit(solution)/shard_map/convert_element_type | solution.py:164
  95.8 23.3 %raw_path.2 = (f32[17,2,256,256]{3,2,1,0:T(8,128)}, bf16[8,2,512,128]{3,2,1,0:T(8,128)(2,1)}, f32[8,128]{1,0:T(8,128)}, bf16[16,512,128]{2,1,0:T(8,128)(2,1)}) custom-call(bf16[16,2,256,128]{3,2,1,0:T(8,128)(2,1)S(1)} %all-to-all-done.1.refs_0_.x_ref, bf16[17,512,256]{2,1,0:T(8,128)(2,1)} %pad_maximum_fusion.refs_1_.fwd_ref, ...), custom_call_target="tpu_custom_call" | custom-call | flops 20000000000 | bytes 25000000 | tf_op jit(solution)/shard_map/raw_path/pallas_call | solution.py:343
  120.4 9.8 %all-to-all-start.4 = ((bf16[16,512,128]{2,1,0:T(8,128)(2,1)}), bf16[16,512,128]{2,1,0:T(8,128)(2,1)}, u32[]{:S(2)}, u32[]{:S(2)}) async-start(bf16[16,512,128]{2,1,0:T(8,128)(2,1)} %get-tuple-element.39), calls=%async_computation.4 | async-start | bytes 4194304 | tf_op jit(solution)/shard_map/all_to_all | solution.py:789
  130.3 4.3 %pack_taps.2.refs_4_ = bf16[16,512,128]{2,1,0:T(8,128)(2,1)} custom-call(f32[512,4096]{1,0:T(8,128)} %x_ref.12), custom_call_target="tpu_custom_call" | custom-call | flops 1000000 | bytes 6000000 | tf_op jit(solution)/shard_map/pack_taps/pallas_call | solution.py:473
  134.5 24.0 %raw_path.3 = (f32[17,2,256,256]{3,2,1,0:T(8,128)}, bf16[8,2,512,128]{3,2,1,0:T(8,128)(2,1)}, f32[8,128]{1,0:T(8,128)}, bf16[16,512,128]{2,1,0:T(8,128)(2,1)}) custom-call(bf16[16,2,256,128]{3,2,1,0:T(8,128)(2,1)} %all-to-all-done.refs_0_.x_ref, bf16[17,512,256]{2,1,0:T(8,128)(2,1)} %pad_maximum_fusion.refs_1_.fwd_ref, ...), custom_call_target="tpu_custom_call", output_to_operand_aliasing={{1}: (5, {})} | custom-call | flops 20000000000 | bytes 25000000 | tf_op jit(solution)/shard_map/raw_path/pallas_call | solution.py:343
  158.5 14.4 %all-to-all-done.4.refs_10_ = bf16[16,512,128]{2,1,0:T(8,128)(2,1)} async-done(((bf16[16,512,128]{2,1,0:T(8,128)(2,1)}), bf16[16,512,128]{2,1,0:T(8,128)(2,1)}, u32[]{:S(2)}, u32[]{:S(2)}) %all-to-all-start.4) | async-done | bytes 2097184 | tf_op jit(solution)/shard_map/all_to_all | solution.py:789
  172.9 9.8 %all-to-all-start.2 = ((bf16[16,512,128]{2,1,0:T(8,128)(2,1)}), bf16[16,512,128]{2,1,0:T(8,128)(2,1)}, u32[]{:S(2)}, u32[]{:S(2)}) async-start(bf16[16,512,128]{2,1,0:T(8,128)(2,1)} %get-tuple-element.34), calls=%async_computation.2 | async-start | bytes 4194304 | tf_op jit(solution)/shard_map/all_to_all | solution.py:789
  185.6 22.0 %conv_path.3 = bf16[16,2,264,128]{3,2,1,0:T(8,128)(2,1)} custom-call(bf16[16,2,256,128]{3,2,1,0:T(8,128)(2,1)S(1)} %copy-done.1, bf16[32,256,128]{2,1,0:T(8,128)(2,1)} %bitcast.7.h_ref, f32[17,2,256,256]{3,2,1,0:T(8,128)} %get-tuple-element.40.spec_ref, f32[1,128]{1,0:T(1,128)} %get-tuple-element.71.skip_ref, ...), custom_call_target="tpu_custom_call" | custom-call | flops 20000000000 | bytes 25000000 | tf_op jit(solution)/shard_map/conv_path/pallas_call | solution.py:412
  207.6 17.8 %all-to-all-done.2.refs_11_ = bf16[16,512,128]{2,1,0:T(8,128)(2,1)} async-done(((bf16[16,512,128]{2,1,0:T(8,128)(2,1)}), bf16[16,512,128]{2,1,0:T(8,128)(2,1)}, u32[]{:S(2)}, u32[]{:S(2)}) %all-to-all-start.2) | async-done | bytes 2097184 | tf_op jit(solution)/shard_map/all_to_all | solution.py:789
  225.4 9.6 %all-to-all-start.5 = ((bf16[16,2,264,128]{3,2,1,0:T(8,128)(2,1)}), bf16[16,2,264,128]{3,2,1,0:T(8,128)(2,1)}, u32[]{:S(2)}, u32[]{:S(2)}) async-start(bf16[16,2,264,128]{3,2,1,0:T(8,128)(2,1)} %conv_path.3), calls=%async_computation.5 | async-start | bytes 4325376 | tf_op jit(solution)/shard_map/all_to_all | solution.py:789
  237.5 22.7 %conv_path.2 = bf16[16,2,264,128]{3,2,1,0:T(8,128)(2,1)} custom-call(bf16[16,2,256,128]{3,2,1,0:T(8,128)(2,1)} %all-to-all-done.refs_0_.x_ref, bf16[32,256,128]{2,1,0:T(8,128)(2,1)} %bitcast.5.h_ref, f32[17,2,256,256]{3,2,1,0:T(8,128)} %get-tuple-element.35.spec_ref, f32[1,128]{1,0:T(1,128)} %get-tuple-element.38.skip_ref, ...), custom_call_target="tpu_custom_call" | custom-call | flops 20000000000 | bytes 25000000 | tf_op jit(solution)/shard_map/conv_path/pallas_call | solution.py:412
  260.1 18.5 %all-to-all-done.5.y_ref = bf16[16,2,264,128]{3,2,1,0:T(8,128)(2,1)} async-done(((bf16[16,2,264,128]{3,2,1,0:T(8,128)(2,1)}), bf16[16,2,264,128]{3,2,1,0:T(8,128)(2,1)}, u32[]{:S(2)}, u32[]{:S(2)}) %all-to-all-start.5) | async-done | bytes 2162720 | tf_op jit(solution)/shard_map/all_to_all | solution.py:789
  278.6 9.9 %all-to-all-start.3 = ((bf16[16,2,264,128]{3,2,1,0:T(8,128)(2,1)}), bf16[16,2,264,128]{3,2,1,0:T(8,128)(2,1)}, u32[]{:S(2)}, u32[]{:S(2)}) async-start(bf16[16,2,264,128]{3,2,1,0:T(8,128)(2,1)} %conv_path.2), calls=%async_computation.3 | async-start | bytes 4325376 | tf_op jit(solution)/shard_map/all_to_all | solution.py:789
  289.4 8.6 %short_sums.2.refs_1_ = bf16[16,2,24,128]{3,2,1,0:T(8,128)(2,1)} custom-call(bf16[3,256,4096]{2,1,0:T(8,128)(2,1)} %x_ref.17, bf16[3,8,4096]{2,1,0:T(8,128)(2,1)} %copy-done.2, bf16[256,4096]{1,0:T(8,128)(2,1)} %go_ref.13, f32[3,7,4096]{2,1,0:T(8,128)} %w_ref.13, bf16[16,2,264,128]{3,2,1,0:T(8,128)(2,1)} %all-to-all-done.5.y_ref, ...), custom_call_target="tpu_custom_call" | custom-call | flops 150000000 | bytes 8000000 | tf_op jit(solution)/shard_map/short_sums/pallas_call | solution.py:698
  298.0 33.9 %all-to-all-done.3.y_ref = bf16[16,2,264,128]{3,2,1,0:T(8,128)(2,1)} async-done(((bf16[16,2,264,128]{3,2,1,0:T(8,128)(2,1)}), bf16[16,2,264,128]{3,2,1,0:T(8,128)(2,1)}, u32[]{:S(2)}, u32[]{:S(2)}) %all-to-all-start.3) | async-done | bytes 2162720 | tf_op jit(solution)/shard_map/all_to_all | solution.py:789
  331.9 7.9 %short_sums.3 = bf16[16,2,24,128]{3,2,1,0:T(8,128)(2,1)} custom-call(bf16[3,256,4096]{2,1,0:T(8,128)(2,1)} %x_ref.17, bf16[3,8,4096]{2,1,0:T(8,128)(2,1)} %copy-done.2, bf16[256,4096]{1,0:T(8,128)(2,1)} %go_ref.13, f32[3,7,4096]{2,1,0:T(8,128)} %w_ref.13, bf16[16,2,264,128]{3,2,1,0:T(8,128)(2,1)} %all-to-all-done.3.y_ref, ...), custom_call_target="tpu_custom_call", output_to_operand_aliasing={{}: (7, {})} | custom-call | flops 150000000 | bytes 8000000 | tf_op jit(solution)/shard_map/short_sums/pallas_call | solution.py:698
  339.8 10.0 %all-to-all-start.6 = ((bf16[16,2,24,128]{3,2,1,0:T(8,128)(2,1)}), bf16[16,2,24,128]{3,2,1,0:T(8,128)(2,1)S(1)}, u32[]{:S(2)}, u32[]{:S(2)}) async-start(bf16[16,2,24,128]{3,2,1,0:T(8,128)(2,1)} %short_sums.3), calls=%async_computation.6 | async-start | bytes 393216 | tf_op jit(solution)/shard_map/all_to_all | solution.py:789
  351.2 6.8 %all-to-all-done.6 = bf16[16,2,24,128]{3,2,1,0:T(8,128)(2,1)S(1)} async-done(((bf16[16,2,24,128]{3,2,1,0:T(8,128)(2,1)}), bf16[16,2,24,128]{3,2,1,0:T(8,128)(2,1)S(1)}, u32[]{:S(2)}, u32[]{:S(2)}) %all-to-all-start.6) | async-done | bytes 196640 | tf_op jit(solution)/shard_map/all_to_all | solution.py:789
  385.6 4.4 %collective-permute-start.7 = (bf16[2,512,128]{2,1,0:T(8,128)(2,1)}, bf16[2,512,128]{2,1,0:T(8,128)(2,1)}, u32[]{:S(2)}, u32[]{:S(2)}) collective-permute-start(bf16[2,512,128]{2,1,0:T(8,128)(2,1)} %get-tuple-element.60), channel_id=1, source_target_pairs={{0,12},{2,14},{4,8},{6,10},{8,4},{10,6},{12,0},{14,2},{1,13},{3,15... | collective-permute-start | bytes 786440 | tf_op jit(solution)/shard_map/ppermute | solution.py:860
  392.2 9.9 %finish.3 = (bf16[256,4096]{1,0:T(8,128)(2,1)}, bf16[3,256,4096]{2,1,0:T(8,128)(2,1)}) custom-call(bf16[3,256,4096]{2,1,0:T(8,128)(2,1)} %x_ref.17, bf16[3,8,4096]{2,1,0:T(8,128)(2,1)} %copy-done.2, bf16[4,8,4096]{2,1,0:T(8,128)(2,1)} %copy-done.3, bf16[256,4096]{1,0:T(8,128)(2,1)} %go_ref.13, f32[3,7,4096]{2,1,0:T(8,128)} %w_ref.13, ...), custom_call_target="tpu_custom_call" | custom-call | flops 150000000 | bytes 12000000 | tf_op jit(solution)/shard_map/finish/pallas_call | solution.py:752
  402.2 6.4 %finish.4 = (bf16[256,4096]{1,0:T(8,128)(2,1)}, bf16[3,256,4096]{2,1,0:T(8,128)(2,1)}) custom-call(bf16[3,256,4096]{2,1,0:T(8,128)(2,1)} %x_ref.17, bf16[3,8,4096]{2,1,0:T(8,128)(2,1)} %copy-done.2, bf16[4,8,4096]{2,1,0:T(8,128)(2,1)} %copy-done.3, bf16[256,4096]{1,0:T(8,128)(2,1)} %go_ref.13, ...), custom_call_target="tpu_custom_call", output_to_operand_aliasing={{0}: (6, {}), {1}: (7, {})} | custom-call | flops 150000000 | bytes 12000000 | tf_op jit(solution)/shard_map/finish/pallas_call | solution.py:752
  408.6 6.4 %finish.5 = (bf16[256,4096]{1,0:T(8,128)(2,1)}, bf16[3,256,4096]{2,1,0:T(8,128)(2,1)}) custom-call(bf16[3,256,4096]{2,1,0:T(8,128)(2,1)} %x_ref.17, bf16[3,8,4096]{2,1,0:T(8,128)(2,1)} %copy-done.2, bf16[4,8,4096]{2,1,0:T(8,128)(2,1)} %copy-done.3, bf16[256,4096]{1,0:T(8,128)(2,1)} %go_ref.13, ...), custom_call_target="tpu_custom_call", output_to_operand_aliasing={{0}: (6, {}), {1}: (7, {})} | custom-call | flops 150000000 | bytes 12000000 | tf_op jit(solution)/shard_map/finish/pallas_call | solution.py:752
  415.1 6.7 %scale_taps.1 = (f32[512,4096]{1,0:T(8,128)}, f32[3,7,4096]{2,1,0:T(8,128)}, f32[1,4096]{1,0:T(1,128)}) custom-call(bf16[32,2,24,128]{3,2,1,0:T(8,128)(2,1)} %all-to-all-done.7.refs_0_, s32[1,3]{1,0:T(1,128)} %add_bitcast_fusion.refs_3_.refs_1_, bf16[2,512,128]{2,1,0:T(8,128)(2,1)S(1)} %get-tuple-element.66.refs_2_, ...), custom_call_target="tpu_custom_call" | custom-call | tf_op jit(solution)/shard_map/scale_taps/pallas_call | solution.py:551
  (47 shorter events, 41.4 us)
Async XLA Ops:
  1.7 9.0 %collective-permute-start = (bf16[3,8,4096]{2,1,0:T(8,128)(2,1)S(1)}, bf16[3,8,4096]{2,1,0:T(8,128)(2,1)S(1)}, u32[]{:S(2)}, u32[]{:S(2)}) collective-permute-start(bf16[3,8,4096]{2,1,0:T(8,128)(2,1)S(1)} %get-tuple-element.58), channel_id=1, source_target_pairs={{0,2},{2,4},{4,6},{6,8},{8,10},{10,12},{12,14},{14,16},{16,18},{18... | collective-permute-start | bytes 589832 | tf_op jit(solution)/shard_map/ppermute | solution.py:785
  10.7 0.7 copy-start.2
  17.6 50.3 %all-to-all-start.1 = ((bf16[16,2,256,128]{3,2,1,0:T(8,128)(2,1)}), bf16[16,2,256,128]{3,2,1,0:T(8,128)(2,1)S(1)}, u32[]{:S(2)}, u32[]{:S(2)}) async-start(bf16[16,2,256,128]{3,2,1,0:T(8,128)(2,1)} %get-tuple-element.32), calls=%async_computation.1 | async-start | bytes 4194304 | tf_op jit(solution)/shard_map/all_to_all | solution.py:789
  67.9 27.9 %copy-start = (bf16[16,2,256,128]{3,2,1,0:T(8,128)(2,1)}, bf16[16,2,256,128]{3,2,1,0:T(8,128)(2,1)S(1)}, u32[]{:S(2)}) copy-start(bf16[16,2,256,128]{3,2,1,0:T(8,128)(2,1)S(1)} %all-to-all-done.1.refs_0_.x_ref) | copy-start | bytes 6291460
  67.9 52.5 %all-to-all-start = ((bf16[16,2,256,128]{3,2,1,0:T(8,128)(2,1)}), bf16[16,2,256,128]{3,2,1,0:T(8,128)(2,1)}, u32[]{:S(2)}, u32[]{:S(2)}) async-start(bf16[16,2,256,128]{3,2,1,0:T(8,128)(2,1)} %get-tuple-element.31), calls=%async_computation | async-start | bytes 4194304 | tf_op jit(solution)/shard_map/all_to_all | solution.py:789
  120.4 52.5 %all-to-all-start.4 = ((bf16[16,512,128]{2,1,0:T(8,128)(2,1)}), bf16[16,512,128]{2,1,0:T(8,128)(2,1)}, u32[]{:S(2)}, u32[]{:S(2)}) async-start(bf16[16,512,128]{2,1,0:T(8,128)(2,1)} %get-tuple-element.39), calls=%async_computation.4 | async-start | bytes 4194304 | tf_op jit(solution)/shard_map/all_to_all | solution.py:789
  172.9 52.5 %all-to-all-start.2 = ((bf16[16,512,128]{2,1,0:T(8,128)(2,1)}), bf16[16,512,128]{2,1,0:T(8,128)(2,1)}, u32[]{:S(2)}, u32[]{:S(2)}) async-start(bf16[16,512,128]{2,1,0:T(8,128)(2,1)} %get-tuple-element.34), calls=%async_computation.2 | async-start | bytes 4194304 | tf_op jit(solution)/shard_map/all_to_all | solution.py:789
  184.0 1.6 copy-start.1
  185.6 49.4 %copy-start.5 = (f32[8,128]{1,0:T(8,128)S(1)}, f32[8,128]{1,0:T(8,128)}, u32[]{:S(2)}) copy-start(f32[8,128]{1,0:T(8,128)} %get-tuple-element.37) | copy-start | bytes 12292
  185.6 50.0 %copy-start.4 = (f32[8,128]{1,0:T(8,128)S(1)}, f32[8,128]{1,0:T(8,128)}, u32[]{:S(2)}) copy-start(f32[8,128]{1,0:T(8,128)} %get-tuple-element.36) | copy-start | bytes 12292
  225.4 53.2 %all-to-all-start.5 = ((bf16[16,2,264,128]{3,2,1,0:T(8,128)(2,1)}), bf16[16,2,264,128]{3,2,1,0:T(8,128)(2,1)}, u32[]{:S(2)}, u32[]{:S(2)}) async-start(bf16[16,2,264,128]{3,2,1,0:T(8,128)(2,1)} %conv_path.3), calls=%async_computation.5 | async-start | bytes 4325376 | tf_op jit(solution)/shard_map/all_to_all | solution.py:789
  278.6 53.3 %all-to-all-start.3 = ((bf16[16,2,264,128]{3,2,1,0:T(8,128)(2,1)}), bf16[16,2,264,128]{3,2,1,0:T(8,128)(2,1)}, u32[]{:S(2)}, u32[]{:S(2)}) async-start(bf16[16,2,264,128]{3,2,1,0:T(8,128)(2,1)} %conv_path.2), calls=%async_computation.3 | async-start | bytes 4325376 | tf_op jit(solution)/shard_map/all_to_all | solution.py:789
  339.8 18.1 %all-to-all-start.6 = ((bf16[16,2,24,128]{3,2,1,0:T(8,128)(2,1)}), bf16[16,2,24,128]{3,2,1,0:T(8,128)(2,1)S(1)}, u32[]{:S(2)}, u32[]{:S(2)}) async-start(bf16[16,2,24,128]{3,2,1,0:T(8,128)(2,1)} %short_sums.3), calls=%async_computation.6 | async-start | bytes 393216 | tf_op jit(solution)/shard_map/all_to_all | solution.py:789
  349.8 32.4 %collective-permute-start.1 = (bf16[4,8,4096]{2,1,0:T(8,128)(2,1)S(1)}, bf16[4,8,4096]{2,1,0:T(8,128)(2,1)S(1)}, u32[]{:S(2)}, u32[]{:S(2)}) collective-permute-start(bf16[4,8,4096]{2,1,0:T(8,128)(2,1)S(1)} %pad_maximum_fusion.1), channel_id=1, source_target_pairs={{2,0},{4,2},{6,4},{8,6},{10,8},{12,10},{14,12},{16,14},{18,16},{20... | collective-permute-start | bytes 786440 | tf_op jit(solution)/shard_map/ppermute | solution.py:785
  361.9 53.1 %all-to-all-start.7 = ((bf16[32,2,24,128]{3,2,1,0:T(8,128)(2,1)}), bf16[32,2,24,128]{3,2,1,0:T(8,128)(2,1)}, u32[]{:S(2)}, u32[]{:S(2)}) async-start(bf16[32,2,24,128]{3,2,1,0:T(8,128)(2,1)} %broadcast_in_dim.37), calls=%async_computation.7 | async-start | bytes 786432 | tf_op jit(solution)/shard_map/all_to_all | solution.py:885
  367.4 18.1 %collective-permute-start.2 = (bf16[2,512,128]{2,1,0:T(8,128)(2,1)S(1)}, bf16[2,512,128]{2,1,0:T(8,128)(2,1)S(1)}, u32[]{:S(2)}, u32[]{:S(2)}) collective-permute-start(bf16[2,512,128]{2,1,0:T(8,128)(2,1)S(1)} %get-tuple-element.65), channel_id=1, source_target_pairs={{0,2},{2,0},{4,6},{6,4},{8,10},{10,8},{12,14},{14,12},{1,3},{3,1},... | collective-permute-start | bytes 786440 | tf_op jit(solution)/shard_map/ppermute | solution.py:860
  370.9 19.0 %collective-permute-start.3 = (bf16[2,512,128]{2,1,0:T(8,128)(2,1)S(1)}, bf16[2,512,128]{2,1,0:T(8,128)(2,1)S(1)}, u32[]{:S(2)}, u32[]{:S(2)}) collective-permute-start(bf16[2,512,128]{2,1,0:T(8,128)(2,1)S(1)} %get-tuple-element.64), channel_id=1, source_target_pairs={{0,4},{2,6},{4,0},{6,2},{8,12},{10,14},{12,8},{14,10},{1,5},{3,7},... | collective-permute-start | bytes 786440 | tf_op jit(solution)/shard_map/ppermute | solution.py:860
  374.3 40.7 %collective-permute-start.4 = (bf16[2,512,128]{2,1,0:T(8,128)(2,1)}, bf16[2,512,128]{2,1,0:T(8,128)(2,1)S(1)}, u32[]{:S(2)}, u32[]{:S(2)}) collective-permute-start(bf16[2,512,128]{2,1,0:T(8,128)(2,1)} %get-tuple-element.63), channel_id=1, source_target_pairs={{0,6},{2,4},{4,2},{6,0},{8,14},{10,12},{12,10},{14,8},{1,7},{3,5},... | collective-permute-start | bytes 786440 | tf_op jit(solution)/shard_map/ppermute | solution.py:860
  376.7 38.4 %collective-permute-start.5 = (bf16[2,512,128]{2,1,0:T(8,128)(2,1)}, bf16[2,512,128]{2,1,0:T(8,128)(2,1)S(1)}, u32[]{:S(2)}, u32[]{:S(2)}) collective-permute-start(bf16[2,512,128]{2,1,0:T(8,128)(2,1)} %get-tuple-element.62), channel_id=1, source_target_pairs={{0,8},{2,10},{4,12},{6,14},{8,0},{10,2},{12,4},{14,6},{1,9},{3,11}... | collective-permute-start | bytes 786440 | tf_op jit(solution)/shard_map/ppermute | solution.py:860
  382.2 7.7 %copy-start.3 = (bf16[4,8,4096]{2,1,0:T(8,128)(2,1)}, bf16[4,8,4096]{2,1,0:T(8,128)(2,1)S(1)}, u32[]{:S(2)}) copy-start(bf16[4,8,4096]{2,1,0:T(8,128)(2,1)S(1)} %collective-permute-done.1.n_ref) | copy-start | bytes 786436
  382.2 32.8 %collective-permute-start.6 = (bf16[2,512,128]{2,1,0:T(8,128)(2,1)}, bf16[2,512,128]{2,1,0:T(8,128)(2,1)}, u32[]{:S(2)}, u32[]{:S(2)}) collective-permute-start(bf16[2,512,128]{2,1,0:T(8,128)(2,1)} %get-tuple-element.61), channel_id=1, source_target_pairs={{0,10},{2,8},{4,14},{6,12},{8,2},{10,0},{12,6},{14,4},{1,11},{3,9}... | collective-permute-start | bytes 786440 | tf_op jit(solution)/shard_map/ppermute | solution.py:860
  385.6 29.5 %collective-permute-start.7 = (bf16[2,512,128]{2,1,0:T(8,128)(2,1)}, bf16[2,512,128]{2,1,0:T(8,128)(2,1)}, u32[]{:S(2)}, u32[]{:S(2)}) collective-permute-start(bf16[2,512,128]{2,1,0:T(8,128)(2,1)} %get-tuple-element.60), channel_id=1, source_target_pairs={{0,12},{2,14},{4,8},{6,10},{8,4},{10,6},{12,0},{14,2},{1,13},{3,15... | collective-permute-start | bytes 786440 | tf_op jit(solution)/shard_map/ppermute | solution.py:860
  390.0 25.1 %collective-permute-start.8 = (bf16[2,512,128]{2,1,0:T(8,128)(2,1)}, bf16[2,512,128]{2,1,0:T(8,128)(2,1)}, u32[]{:S(2)}, u32[]{:S(2)}) collective-permute-start(bf16[2,512,128]{2,1,0:T(8,128)(2,1)} %get-tuple-element.59), channel_id=1, source_target_pairs={{0,14},{2,12},{4,10},{6,8},{8,6},{10,4},{12,2},{14,0},{1,15},{3,13... | collective-permute-start | bytes 786440 | tf_op jit(solution)/shard_map/ppermute | solution.py:860

commit v7 on v6

--- a/solution.py
+++ b/solution.py
@@ -568,6 +568,38 @@
     )(small, where, *lows, *shared)
 
 
+def add_sums(pieces, squares, copies):
+    shards, parts, lines, chans = pieces.shape
+
+    def kernel(x_ref, sq_ref, o_ref):
+        total = jnp.sum(sq_ref[...], axis=0, keepdims=True)
+        total = jnp.sum(total, axis=1, keepdims=True)
+        sums = []
+        for p in range(parts):
+            value = x_ref[0, p].astype(F32)
+            for s in range(1, shards):
+                value = value + x_ref[s, p].astype(F32)
+            sums.append(value)
+            square = jnp.sum(value * value, axis=0, keepdims=True)
+            total = total + jnp.sum(square, axis=1, keepdims=True)
+        upper = total.astype(BF16).astype(F32)
+        line = lax.broadcasted_iota(jnp.int32, (lines, chans), 0)
+        for p in range(parts):
+            value = jnp.where(line == lines - 2, upper, sums[p])
+            value = jnp.where(line == lines - 1, total - upper, value).astype(BF16)
+            for j in range(copies):
+                o_ref[j, p] = value
+
+    shape = (copies, parts, lines, chans)
+    return pl.pallas_call(
+        kernel,
+        in_specs=[resident(), resident()],
+        out_specs=resident(),
+        out_shape=jax.ShapeDtypeStruct(shape, BF16),
+        name="add_sums",
+    )(pieces, squares)
+
+
 def short_rows(ext_ref, w_ref, i, cs, r, rows):
     total = w_ref[i, 0:1, cs] * ext_ref[i, pl.ds(HALO + r, rows), :]
     for j in range(1, TAPS):
@@ -711,19 +743,18 @@
     )(*ins, *earlier)
 
 
-def finish(streams, before, after, grad_out, short_filter, back, earlier, shards, part, parts, piece, pieces):
+def finish(streams, before, after, grad_out, short_filter, back, earlier, shards, part, parts):
     _, rows, full = streams.shape
     width = full // parts
     chans = width // shards
     block = plan_lanes(width, chans)
     count = width // block
-    steps = count // pieces
     groups = block // chans
     chunk = math.gcd(rows, 64)
 
     def kernel(x_ref, b_ref, n_ref, go_ref, w_ref, y_ref, *refs):
         o_ref, gs_ref, ext_ref, pre_ref = refs[-4:]
-        base = (piece * steps + pl.program_id(0)) * groups
+        base = pl.program_id(0) * groups
         for c in range(0, block, LANES):
             cs = pl.ds(c, LANES)
             fill_ext(ext_ref, x_ref, b_ref, n_ref, cs, rows)
@@ -747,11 +778,11 @@
                         total = total + w_ref[i, j : j + 1, cs] * pre_ref[i, pl.ds(r + j, chunk), :]
                     gs_ref[i, pl.ds(r, chunk), cs] = total.astype(BF16)
 
-    at = lambda i: part * count + piece * steps + i
+    at = lambda i: part * count + i
     ins = [streams, before, after, grad_out, short_filter, back]
     return pl.pallas_call(
         kernel,
-        grid=(steps,),
+        grid=(count,),
         in_specs=[
             pl.BlockSpec((3, rows, block), lambda i: (0, 0, at(i))),
             pl.BlockSpec((3, HALO, block), lambda i: (0, 0, at(i))),
@@ -832,56 +863,48 @@
         packed.append(pack_taps(long_filter, shards, p, parts))
     spec = []
     shared = []
-    squares = 0.0
+    squares = []
     low = None
     for p in range(parts):
         out = raw_path(both[p], fwd, inv, where, packed[p], low, p, parts, tap_rows, live, fold)
         spec.append(out[0])
         low = out[1]
-        squares = squares + jnp.sum(out[2])
+        squares.append(out[2])
         shared.append(exchange(out[3] if fold else packed[p]))
     back = []
-    if parts > 1:
-        skips[-1], squares = lax.optimization_barrier((skips[-1], squares))
+    sent_all = []
     for p in range(parts):
         taps = shared[p].reshape(shards * tap_rows // rows, rows, chans)
         sent = conv_path(both[p], taps, spec[p], skips[p], fwd, inv)
         back.append(on_chip(exchange(sent)))
-        sent_last = sent
+        sent_all.append(sent)
     done = []
     sums = []
     lows = []
 
-    def send_low(first, last, cue):
+    def send_low(steps, cue):
         ready = following(low, cue)
-        if first == 0:
-            lows.append(ready[0])
-        for d in range(max(first, 1), last):
-            lows.append(lax.ppermute(ready[d], "seq", [(i, i ^ d) for i in range(live)]))
+        for d in steps:
+            lows[d] = lax.ppermute(ready[d], "seq", [(i, i ^ d) for i in range(live)])
 
     if fold:
-        send_low(0, live // 2 + 1, sent_last)
+        half = live // 2
+        lows = [low[0]] + [None] * (live - 1)
+        send_low(range(half, half + half // 2), sent_all[0])
+        send_low(range(half + half // 2, live), sent_all[-1])
     for p in range(parts):
         terms = (back[p], bias[p], filtered[p], sums)
         sums = [short_sums(streams, before, grad_out, short_filter, *terms, shards, p, parts)]
         if p == 0 and fold:
-            send_low(live // 2 + 1, live, back[0])
-        pieces = 2 if p and span // plan_lanes(span, chans) % 2 == 0 else 1
-        for piece in range(pieces):
-            given = (streams, before, after, grad_out, short_filter, back[p], done)
-            done = finish(*given, shards, p, parts, piece, pieces)
+            send_low(range(1, half), back[0])
+        done = finish(streams, before, after, grad_out, short_filter, back[p], done, shards, p, parts)
     output, grad_streams = done
     sums = sums[0]
     if not fold:
         lows.append(exchange(following(low, back[-1])))
         sums = following(sums, lows[0])
-    mine_sums = jnp.sum(exchange(sums).astype(F32), axis=0)
-    local_sq = squares + jnp.sum(mine_sums * mine_sums)
-    upper_sq = lax.reduce_precision(local_sq, 8, 7)
-    line = lax.broadcasted_iota(jnp.int32, mine_sums.shape, 1)
-    mine_sums = jnp.where(line == SUMS - 2, upper_sq, mine_sums)
-    mine_sums = jnp.where(line == SUMS - 1, local_sq - upper_sq, mine_sums).astype(BF16)
-    copies = jnp.broadcast_to(mine_sums[None], (shards * lax.axis_size("chan"),) + mine_sums.shape)
+    pieces = on_chip(exchange(sums))
+    copies = add_sums(pieces, jnp.concatenate(squares, axis=0), shards * lax.axis_size("chan"))
     small = lax.all_to_all(copies, ("seq", "chan"), split_axis=0, concat_axis=0, tiled=True)
     param_count = LF * D + (3 * TAPS + 1) * D
     filter_grad, short_grad, bias_grad = scale_taps(

time: 425 us -> 419 us (0.986)
  transfers between devices with their start and end apart: 17 -> 17, of which waited for: 8 -> 8; matrix products, arithmetic and copies ran while one was open for 6% -> 5% of each run, Pallas kernels for 33% -> 33%
where the time goes in v7:
time: 419 us; the launch traced here: 416 us
  Pallas kernels  159 us (38%)
  waiting for transfers between devices  132 us (32%)
  starting transfers between devices  99 us (24%)
  other arithmetic  16 us (4%)
  local copies, waits for them, and re-layouts  10 us (2%)
    all_to_all x7, waiting for transfers between devices, exchange(): lax.all_to_all(blocks, 'seq', split_axis=0, concat_axis=0, axis_index_gro...  128 us
    all_to_all x7, starting transfers between devices, exchange(): lax.all_to_all(blocks, 'seq', split_axis=0, concat_axis=0, axis_index_gro...  66.9 us
    pallas_call x2, Pallas kernels, raw_path(): pl.pallas_call(kernel, grid=(steps,), in_specs=in_specs, out_specs=out_sp...  47.3 us
    pallas_call x2, Pallas kernels, conv_path(): pl.pallas_call(kernel, grid=(steps,), in_specs=[resident(), resident(), p...  44.6 us
    ppermute x7, starting transfers between devices, send_low(): lows[d] = lax.ppermute(ready[d], 'seq', [(i, i ^ d) for i in range(live)])  22.7 us
    pallas_call x2, Pallas kernels, finish(): pl.pallas_call(kernel, grid=(count,), in_specs=[pl.BlockSpec((3, rows, bl...  19.8 us
    pallas_call x2, Pallas kernels, short_sums(): pl.pallas_call(kernel, grid=(count,), in_specs=in_specs + [untouched() fo...  16.5 us
    pallas_call x2, Pallas kernels, gates(): pl.pallas_call(kernel, grid=(count,), in_specs=[pl.BlockSpec((3, rows, bl...  13.8 us
  transfers between devices with their start and end apart: 17, of which 8 were waited for; matrix products, arithmetic and copies ran while one was open for 5% of the time, Pallas kernels for 33%

profile of v7, /device:TPU:0, one launch (start us, length us, event | category | flops | bytes accessed | tf_op | source)
XLA Modules:
  0.0 416.5 jit_solution(17741142661988042763)
XLA Ops:
  2.4 4.9 %collective-permute-start = (bf16[3,8,4096]{2,1,0:T(8,128)(2,1)S(1)}, bf16[3,8,4096]{2,1,0:T(8,128)(2,1)S(1)}, u32[]{:S(2)}, u32[]{:S(2)}) collective-permute-start(bf16[3,8,4096]{2,1,0:T(8,128)(2,1)S(1)} %get-tuple-element.52), channel_id=1, source_target_pairs={{0,2},{2,4},{4,6},{6,8},{8,10},{10,12},{12,14},{14,16},{16,18},{18... | collective-permute-start | bytes 589832 | tf_op jit(solution)/shard_map/ppermute | solution.py:816
  7.2 4.1 collective-permute-done.b_ref
  12.0 6.2 %gates.3 = (bf16[16,2,256,128]{3,2,1,0:T(8,128)(2,1)}, f32[1,2048]{1,0:T(1,128)}) custom-call(bf16[3,256,4096]{2,1,0:T(8,128)(2,1)} %x_ref.15, bf16[3,8,4096]{2,1,0:T(8,128)(2,1)} %copy-done.2, bf16[256,4096]{1,0:T(8,128)(2,1)} %go_ref.11, f32[3,7,4096]{2,1,0:T(8,128)} %w_ref.11), custom_call_target="tpu_custom_call" | custom-call | flops 60000000 | bytes 7000000 | tf_op jit(solution)/shard_map/gates/pallas_call | solution.py:652
  18.3 7.9 %all-to-all-start.1 = ((bf16[16,2,256,128]{3,2,1,0:T(8,128)(2,1)}), bf16[16,2,256,128]{3,2,1,0:T(8,128)(2,1)S(1)}, u32[]{:S(2)}, u32[]{:S(2)}) async-start(bf16[16,2,256,128]{3,2,1,0:T(8,128)(2,1)} %get-tuple-element.29), calls=%async_computation.1 | async-start | bytes 4194304 | tf_op jit(solution)/shard_map/all_to_all | solution.py:820
  26.1 7.6 %gates.2 = (bf16[16,2,256,128]{3,2,1,0:T(8,128)(2,1)}, f32[1,2048]{1,0:T(1,128)}, f32[2,256,2048]{2,1,0:T(8,128)}) custom-call(bf16[3,256,4096]{2,1,0:T(8,128)(2,1)} %x_ref.15, bf16[3,8,4096]{2,1,0:T(8,128)(2,1)} %copy-done.2, bf16[256,4096]{1,0:T(8,128)(2,1)} %go_ref.11, f32[3,7,4096]{2,1,0:T(8,128)} %w_ref.11), custom_call_target="tpu_custom_call" | custom-call | flops 60000000 | bytes 7000000 | tf_op jit(solution)/shard_map/gates/pallas_call | solution.py:652
  33.7 34.9 %all-to-all-done.1.refs_0_.x_ref = bf16[16,2,256,128]{3,2,1,0:T(8,128)(2,1)S(1)} async-done(((bf16[16,2,256,128]{3,2,1,0:T(8,128)(2,1)}), bf16[16,2,256,128]{3,2,1,0:T(8,128)(2,1)S(1)}, u32[]{:S(2)}, u32[]{:S(2)}) %all-to-all-start.1) | async-done | bytes 2097184 | tf_op jit(solution)/shard_map/all_to_all | solution.py:820
  68.6 9.9 %all-to-all-start = ((bf16[16,2,256,128]{3,2,1,0:T(8,128)(2,1)}), bf16[16,2,256,128]{3,2,1,0:T(8,128)(2,1)}, u32[]{:S(2)}, u32[]{:S(2)}) async-start(bf16[16,2,256,128]{3,2,1,0:T(8,128)(2,1)} %get-tuple-element.28), calls=%async_computation | async-start | bytes 4194304 | tf_op jit(solution)/shard_map/all_to_all | solution.py:820
  78.5 4.3 %pack_taps.3.refs_4_ = bf16[16,512,128]{2,1,0:T(8,128)(2,1)} custom-call(f32[512,4096]{1,0:T(8,128)} %x_ref.11), custom_call_target="tpu_custom_call" | custom-call | flops 1000000 | bytes 6000000 | tf_op jit(solution)/shard_map/pack_taps/pallas_call | solution.py:473
  84.5 4.1 multiply_subtract_fusion
  91.1 5.5 %fusion.refs_2_.inv_ref = bf16[17,512,256]{2,1,0:T(8,128)(2,1)} fusion(f32[17,256,256]{2,1,0:T(8,128)} %get-tuple-element.62, f32[17,256,256]{2,1,0:T(8,128)S(1)} %get-tuple-element.60), kind=kLoop, calls=%fused_computation.1 | loop fusion | flops 6684672 | bytes 13369344 | tf_op jit(solution)/shard_map/convert_element_type | solution.py:164
  96.5 23.3 %raw_path.2 = (f32[17,2,256,256]{3,2,1,0:T(8,128)}, bf16[8,2,512,128]{3,2,1,0:T(8,128)(2,1)}, f32[8,128]{1,0:T(8,128)}, bf16[16,512,128]{2,1,0:T(8,128)(2,1)}) custom-call(bf16[16,2,256,128]{3,2,1,0:T(8,128)(2,1)S(1)} %all-to-all-done.1.refs_0_.x_ref, bf16[17,512,256]{2,1,0:T(8,128)(2,1)} %pad_maximum_fusion.refs_1_.fwd_ref, ...), custom_call_target="tpu_custom_call" | custom-call | flops 20000000000 | bytes 25000000 | tf_op jit(solution)/shard_map/raw_path/pallas_call | solution.py:343
  121.1 9.8 %all-to-all-start.4 = ((bf16[16,512,128]{2,1,0:T(8,128)(2,1)}), bf16[16,512,128]{2,1,0:T(8,128)(2,1)}, u32[]{:S(2)}, u32[]{:S(2)}) async-start(bf16[16,512,128]{2,1,0:T(8,128)(2,1)} %get-tuple-element.33), calls=%async_computation.4 | async-start | bytes 4194304 | tf_op jit(solution)/shard_map/all_to_all | solution.py:820
  130.9 4.3 %pack_taps.2.refs_4_ = bf16[16,512,128]{2,1,0:T(8,128)(2,1)} custom-call(f32[512,4096]{1,0:T(8,128)} %x_ref.11), custom_call_target="tpu_custom_call" | custom-call | flops 1000000 | bytes 6000000 | tf_op jit(solution)/shard_map/pack_taps/pallas_call | solution.py:473
  135.2 23.9 %raw_path.3 = (f32[17,2,256,256]{3,2,1,0:T(8,128)}, bf16[8,2,512,128]{3,2,1,0:T(8,128)(2,1)}, f32[8,128]{1,0:T(8,128)}, bf16[16,512,128]{2,1,0:T(8,128)(2,1)}) custom-call(bf16[16,2,256,128]{3,2,1,0:T(8,128)(2,1)} %all-to-all-done.refs_0_.x_ref, bf16[17,512,256]{2,1,0:T(8,128)(2,1)} %pad_maximum_fusion.refs_1_.fwd_ref, ...), custom_call_target="tpu_custom_call", output_to_operand_aliasing={{1}: (5, {})} | custom-call | flops 20000000000 | bytes 25000000 | tf_op jit(solution)/shard_map/raw_path/pallas_call | solution.py:343
  159.1 14.5 %all-to-all-done.4.refs_10_ = bf16[16,512,128]{2,1,0:T(8,128)(2,1)} async-done(((bf16[16,512,128]{2,1,0:T(8,128)(2,1)}), bf16[16,512,128]{2,1,0:T(8,128)(2,1)}, u32[]{:S(2)}, u32[]{:S(2)}) %all-to-all-start.4) | async-done | bytes 2097184 | tf_op jit(solution)/shard_map/all_to_all | solution.py:820
  173.6 9.7 %all-to-all-start.2 = ((bf16[16,512,128]{2,1,0:T(8,128)(2,1)}), bf16[16,512,128]{2,1,0:T(8,128)(2,1)}, u32[]{:S(2)}, u32[]{:S(2)}) async-start(bf16[16,512,128]{2,1,0:T(8,128)(2,1)} %get-tuple-element.31), calls=%async_computation.2 | async-start | bytes 4194304 | tf_op jit(solution)/shard_map/all_to_all | solution.py:820
  186.2 21.9 %conv_path.3 = bf16[16,2,264,128]{3,2,1,0:T(8,128)(2,1)} custom-call(bf16[16,2,256,128]{3,2,1,0:T(8,128)(2,1)S(1)} %copy-done.1, bf16[32,256,128]{2,1,0:T(8,128)(2,1)} %bitcast.7.h_ref, f32[17,2,256,256]{3,2,1,0:T(8,128)} %get-tuple-element.34.spec_ref, f32[1,128]{1,0:T(1,128)} %get-tuple-element.64.skip_ref, ...), custom_call_target="tpu_custom_call" | custom-call | flops 20000000000 | bytes 25000000 | tf_op jit(solution)/shard_map/conv_path/pallas_call | solution.py:412
  208.1 17.8 %all-to-all-done.2.refs_11_ = bf16[16,512,128]{2,1,0:T(8,128)(2,1)} async-done(((bf16[16,512,128]{2,1,0:T(8,128)(2,1)}), bf16[16,512,128]{2,1,0:T(8,128)(2,1)}, u32[]{:S(2)}, u32[]{:S(2)}) %all-to-all-start.2) | async-done | bytes 2097184 | tf_op jit(solution)/shard_map/all_to_all | solution.py:820
  226.0 9.5 %all-to-all-start.5 = ((bf16[16,2,264,128]{3,2,1,0:T(8,128)(2,1)}), bf16[16,2,264,128]{3,2,1,0:T(8,128)(2,1)}, u32[]{:S(2)}, u32[]{:S(2)}) async-start(bf16[16,2,264,128]{3,2,1,0:T(8,128)(2,1)} %conv_path.3), calls=%async_computation.5 | async-start | bytes 4325376 | tf_op jit(solution)/shard_map/all_to_all | solution.py:820
  235.5 22.7 %conv_path.2 = bf16[16,2,264,128]{3,2,1,0:T(8,128)(2,1)} custom-call(bf16[16,2,256,128]{3,2,1,0:T(8,128)(2,1)} %all-to-all-done.refs_0_.x_ref, bf16[32,256,128]{2,1,0:T(8,128)(2,1)} %bitcast.5.h_ref, f32[17,2,256,256]{3,2,1,0:T(8,128)} %get-tuple-element.32.spec_ref, f32[1,128]{1,0:T(1,128)} %get-tuple-element.65.skip_ref, ...), custom_call_target="tpu_custom_call" | custom-call | flops 20000000000 | bytes 25000000 | tf_op jit(solution)/shard_map/conv_path/pallas_call | solution.py:412
  258.1 20.9 %all-to-all-done.5.y_ref = bf16[16,2,264,128]{3,2,1,0:T(8,128)(2,1)} async-done(((bf16[16,2,264,128]{3,2,1,0:T(8,128)(2,1)}), bf16[16,2,264,128]{3,2,1,0:T(8,128)(2,1)}, u32[]{:S(2)}, u32[]{:S(2)}) %all-to-all-start.5) | async-done | bytes 2162720 | tf_op jit(solution)/shard_map/all_to_all | solution.py:820
  279.0 10.0 %all-to-all-start.3 = ((bf16[16,2,264,128]{3,2,1,0:T(8,128)(2,1)}), bf16[16,2,264,128]{3,2,1,0:T(8,128)(2,1)}, u32[]{:S(2)}, u32[]{:S(2)}) async-start(bf16[16,2,264,128]{3,2,1,0:T(8,128)(2,1)} %conv_path.2), calls=%async_computation.3 | async-start | bytes 4325376 | tf_op jit(solution)/shard_map/all_to_all | solution.py:820
  289.8 8.6 %short_sums.2.refs_1_ = bf16[16,2,24,128]{3,2,1,0:T(8,128)(2,1)} custom-call(bf16[3,256,4096]{2,1,0:T(8,128)(2,1)} %x_ref.15, bf16[3,8,4096]{2,1,0:T(8,128)(2,1)} %copy-done.2, bf16[256,4096]{1,0:T(8,128)(2,1)} %go_ref.11, f32[3,7,4096]{2,1,0:T(8,128)} %w_ref.11, bf16[16,2,264,128]{3,2,1,0:T(8,128)(2,1)} %all-to-all-done.5.y_ref, ...), custom_call_target="tpu_custom_call" | custom-call | flops 150000000 | bytes 8000000 | tf_op jit(solution)/shard_map/short_sums/pallas_call | solution.py:730
  298.4 33.8 %all-to-all-done.3.y_ref = bf16[16,2,264,128]{3,2,1,0:T(8,128)(2,1)} async-done(((bf16[16,2,264,128]{3,2,1,0:T(8,128)(2,1)}), bf16[16,2,264,128]{3,2,1,0:T(8,128)(2,1)}, u32[]{:S(2)}, u32[]{:S(2)}) %all-to-all-start.3) | async-done | bytes 2162720 | tf_op jit(solution)/shard_map/all_to_all | solution.py:820
  332.3 7.9 %short_sums.3 = bf16[16,2,24,128]{3,2,1,0:T(8,128)(2,1)} custom-call(bf16[3,256,4096]{2,1,0:T(8,128)(2,1)} %x_ref.15, bf16[3,8,4096]{2,1,0:T(8,128)(2,1)} %copy-done.2, bf16[256,4096]{1,0:T(8,128)(2,1)} %go_ref.11, f32[3,7,4096]{2,1,0:T(8,128)} %w_ref.11, bf16[16,2,264,128]{3,2,1,0:T(8,128)(2,1)} %all-to-all-done.3.y_ref, ...), custom_call_target="tpu_custom_call", output_to_operand_aliasing={{}: (7, {})} | custom-call | flops 150000000 | bytes 8000000 | tf_op jit(solution)/shard_map/short_sums/pallas_call | solution.py:730
  340.2 10.1 %all-to-all-start.6 = ((bf16[16,2,24,128]{3,2,1,0:T(8,128)(2,1)}), bf16[16,2,24,128]{3,2,1,0:T(8,128)(2,1)S(1)}, u32[]{:S(2)}, u32[]{:S(2)}) async-start(bf16[16,2,24,128]{3,2,1,0:T(8,128)(2,1)} %short_sums.3), calls=%async_computation.6 | async-start | bytes 393216 | tf_op jit(solution)/shard_map/all_to_all | solution.py:820
  353.9 4.5 %all-to-all-done.6.x_ref = bf16[16,2,24,128]{3,2,1,0:T(8,128)(2,1)S(1)} async-done(((bf16[16,2,24,128]{3,2,1,0:T(8,128)(2,1)}), bf16[16,2,24,128]{3,2,1,0:T(8,128)(2,1)S(1)}, u32[]{:S(2)}, u32[]{:S(2)}) %all-to-all-start.6) | async-done | bytes 196640 | tf_op jit(solution)/shard_map/all_to_all | solution.py:820
  364.3 4.5 %collective-permute-start.7 = (bf16[2,512,128]{2,1,0:T(8,128)(2,1)S(1)}, bf16[2,512,128]{2,1,0:T(8,128)(2,1)S(1)}, u32[]{:S(2)}, u32[]{:S(2)}) collective-permute-start(bf16[2,512,128]{2,1,0:T(8,128)(2,1)S(1)} %get-tuple-element.54), channel_id=1, source_target_pairs={{0,12},{2,14},{4,8},{6,10},{8,4},{10,6},{12,0},{14,2},{1,13},{3,15... | collective-permute-start | bytes 786440 | tf_op jit(solution)/shard_map/ppermute | solution.py:888
  380.6 3.5 collective-permute-start.2
  389.9 9.9 %finish.2 = (bf16[256,4096]{1,0:T(8,128)(2,1)}, bf16[3,256,4096]{2,1,0:T(8,128)(2,1)}) custom-call(bf16[3,256,4096]{2,1,0:T(8,128)(2,1)} %x_ref.15, bf16[3,8,4096]{2,1,0:T(8,128)(2,1)} %copy-done.2, bf16[4,8,4096]{2,1,0:T(8,128)(2,1)} %copy-done.4, bf16[256,4096]{1,0:T(8,128)(2,1)} %go_ref.11, f32[3,7,4096]{2,1,0:T(8,128)} %w_ref.11, ...), custom_call_target="tpu_custom_call" | custom-call | flops 150000000 | bytes 12000000 | tf_op jit(solution)/shard_map/finish/pallas_call | solution.py:783
  399.8 9.9 %finish.3 = (bf16[256,4096]{1,0:T(8,128)(2,1)}, bf16[3,256,4096]{2,1,0:T(8,128)(2,1)}) custom-call(bf16[3,256,4096]{2,1,0:T(8,128)(2,1)} %x_ref.15, bf16[3,8,4096]{2,1,0:T(8,128)(2,1)} %copy-done.2, bf16[4,8,4096]{2,1,0:T(8,128)(2,1)} %copy-done.4, bf16[256,4096]{1,0:T(8,128)(2,1)} %go_ref.11, ...), custom_call_target="tpu_custom_call", output_to_operand_aliasing={{0}: (6, {}), {1}: (7, {})} | custom-call | flops 150000000 | bytes 12000000 | tf_op jit(solution)/shard_map/finish/pallas_call | solution.py:783
  409.8 6.7 %scale_taps.1 = (f32[512,4096]{1,0:T(8,128)}, f32[3,7,4096]{2,1,0:T(8,128)}, f32[1,4096]{1,0:T(1,128)}) custom-call(bf16[32,2,24,128]{3,2,1,0:T(8,128)(2,1)} %all-to-all-done.7.refs_0_, s32[1,3]{1,0:T(1,128)} %add_bitcast_fusion.refs_3_.refs_1_, bf16[2,512,128]{2,1,0:T(8,128)(2,1)S(1)} %slice_bitcast_fusion.7.refs_2_, ...), custom_call_target="tpu_custom_call" | custom-call | tf_op jit(solution)/shard_map/scale_taps/pallas_call | solution.py:551
  (45 shorter events, 38.6 us)
Async XLA Ops:
  2.4 9.0 %collective-permute-start = (bf16[3,8,4096]{2,1,0:T(8,128)(2,1)S(1)}, bf16[3,8,4096]{2,1,0:T(8,128)(2,1)S(1)}, u32[]{:S(2)}, u32[]{:S(2)}) collective-permute-start(bf16[3,8,4096]{2,1,0:T(8,128)(2,1)S(1)} %get-tuple-element.52), channel_id=1, source_target_pairs={{0,2},{2,4},{4,6},{6,8},{8,10},{10,12},{12,14},{14,16},{16,18},{18... | collective-permute-start | bytes 589832 | tf_op jit(solution)/shard_map/ppermute | solution.py:816
  11.4 0.7 copy-start.2
  18.3 50.3 %all-to-all-start.1 = ((bf16[16,2,256,128]{3,2,1,0:T(8,128)(2,1)}), bf16[16,2,256,128]{3,2,1,0:T(8,128)(2,1)S(1)}, u32[]{:S(2)}, u32[]{:S(2)}) async-start(bf16[16,2,256,128]{3,2,1,0:T(8,128)(2,1)} %get-tuple-element.29), calls=%async_computation.1 | async-start | bytes 4194304 | tf_op jit(solution)/shard_map/all_to_all | solution.py:820
  68.6 28.0 %copy-start = (bf16[16,2,256,128]{3,2,1,0:T(8,128)(2,1)}, bf16[16,2,256,128]{3,2,1,0:T(8,128)(2,1)S(1)}, u32[]{:S(2)}) copy-start(bf16[16,2,256,128]{3,2,1,0:T(8,128)(2,1)S(1)} %all-to-all-done.1.refs_0_.x_ref) | copy-start | bytes 6291460
  68.6 52.5 %all-to-all-start = ((bf16[16,2,256,128]{3,2,1,0:T(8,128)(2,1)}), bf16[16,2,256,128]{3,2,1,0:T(8,128)(2,1)}, u32[]{:S(2)}, u32[]{:S(2)}) async-start(bf16[16,2,256,128]{3,2,1,0:T(8,128)(2,1)} %get-tuple-element.28), calls=%async_computation | async-start | bytes 4194304 | tf_op jit(solution)/shard_map/all_to_all | solution.py:820
  121.1 52.5 %all-to-all-start.4 = ((bf16[16,512,128]{2,1,0:T(8,128)(2,1)}), bf16[16,512,128]{2,1,0:T(8,128)(2,1)}, u32[]{:S(2)}, u32[]{:S(2)}) async-start(bf16[16,512,128]{2,1,0:T(8,128)(2,1)} %get-tuple-element.33), calls=%async_computation.4 | async-start | bytes 4194304 | tf_op jit(solution)/shard_map/all_to_all | solution.py:820
  173.6 52.4 %all-to-all-start.2 = ((bf16[16,512,128]{2,1,0:T(8,128)(2,1)}), bf16[16,512,128]{2,1,0:T(8,128)(2,1)}, u32[]{:S(2)}, u32[]{:S(2)}) async-start(bf16[16,512,128]{2,1,0:T(8,128)(2,1)} %get-tuple-element.31), calls=%async_computation.2 | async-start | bytes 4194304 | tf_op jit(solution)/shard_map/all_to_all | solution.py:820
  184.6 1.6 copy-start.1
  226.0 53.0 %all-to-all-start.5 = ((bf16[16,2,264,128]{3,2,1,0:T(8,128)(2,1)}), bf16[16,2,264,128]{3,2,1,0:T(8,128)(2,1)}, u32[]{:S(2)}, u32[]{:S(2)}) async-start(bf16[16,2,264,128]{3,2,1,0:T(8,128)(2,1)} %conv_path.3), calls=%async_computation.5 | async-start | bytes 4325376 | tf_op jit(solution)/shard_map/all_to_all | solution.py:820
  279.0 53.3 %all-to-all-start.3 = ((bf16[16,2,264,128]{3,2,1,0:T(8,128)(2,1)}), bf16[16,2,264,128]{3,2,1,0:T(8,128)(2,1)}, u32[]{:S(2)}, u32[]{:S(2)}) async-start(bf16[16,2,264,128]{3,2,1,0:T(8,128)(2,1)} %conv_path.2), calls=%async_computation.3 | async-start | bytes 4325376 | tf_op jit(solution)/shard_map/all_to_all | solution.py:820
  332.3 21.0 %copy-start.5 = (f32[8,128]{1,0:T(8,128)S(1)}, f32[8,128]{1,0:T(8,128)}, u32[]{:S(2)}) copy-start(f32[8,128]{1,0:T(8,128)} %get-tuple-element.42) | copy-start | bytes 12292
  332.3 21.0 %copy-start.6 = (f32[8,128]{1,0:T(8,128)S(1)}, f32[8,128]{1,0:T(8,128)}, u32[]{:S(2)}) copy-start(f32[8,128]{1,0:T(8,128)} %get-tuple-element.43) | copy-start | bytes 12292
  340.2 39.6 %copy-start.3 = (bf16[8,2,512,128]{3,2,1,0:T(8,128)(2,1)S(1)}, bf16[8,2,512,128]{3,2,1,0:T(8,128)(2,1)}, u32[]{:S(2)}) copy-start(bf16[8,2,512,128]{3,2,1,0:T(8,128)(2,1)} %get-tuple-element.47) | copy-start | bytes 6291460
  340.2 18.2 %all-to-all-start.6 = ((bf16[16,2,24,128]{3,2,1,0:T(8,128)(2,1)}), bf16[16,2,24,128]{3,2,1,0:T(8,128)(2,1)S(1)}, u32[]{:S(2)}, u32[]{:S(2)}) async-start(bf16[16,2,24,128]{3,2,1,0:T(8,128)(2,1)} %short_sums.3), calls=%async_computation.6 | async-start | bytes 393216 | tf_op jit(solution)/shard_map/all_to_all | solution.py:820
  352.0 28.7 %collective-permute-start.1 = (bf16[4,8,4096]{2,1,0:T(8,128)(2,1)}, bf16[4,8,4096]{2,1,0:T(8,128)(2,1)S(1)}, u32[]{:S(2)}, u32[]{:S(2)}) collective-permute-start(bf16[4,8,4096]{2,1,0:T(8,128)(2,1)} %pad_maximum_fusion.1), channel_id=1, source_target_pairs={{2,0},{4,2},{6,4},{8,6},{10,8},{12,10},{14,12},{16,14},{18,16},{20... | collective-permute-start | bytes 786440 | tf_op jit(solution)/shard_map/ppermute | solution.py:816
  360.0 49.8 %all-to-all-start.7 = ((bf16[32,2,24,128]{3,2,1,0:T(8,128)(2,1)}), bf16[32,2,24,128]{3,2,1,0:T(8,128)(2,1)}, u32[]{:S(2)}, u32[]{:S(2)}) async-start(bf16[32,2,24,128]{3,2,1,0:T(8,128)(2,1)} %add_sums.1), calls=%async_computation.7 | async-start | bytes 786432 | tf_op jit(solution)/shard_map/all_to_all | solution.py:908
  364.3 19.8 %collective-permute-start.7 = (bf16[2,512,128]{2,1,0:T(8,128)(2,1)S(1)}, bf16[2,512,128]{2,1,0:T(8,128)(2,1)S(1)}, u32[]{:S(2)}, u32[]{:S(2)}) collective-permute-start(bf16[2,512,128]{2,1,0:T(8,128)(2,1)S(1)} %get-tuple-element.54), channel_id=1, source_target_pairs={{0,12},{2,14},{4,8},{6,10},{8,4},{10,6},{12,0},{14,2},{1,13},{3,15... | collective-permute-start | bytes 786440 | tf_op jit(solution)/shard_map/ppermute | solution.py:888
  368.8 18.7 %collective-permute-start.8 = (bf16[2,512,128]{2,1,0:T(8,128)(2,1)S(1)}, bf16[2,512,128]{2,1,0:T(8,128)(2,1)S(1)}, u32[]{:S(2)}, u32[]{:S(2)}) collective-permute-start(bf16[2,512,128]{2,1,0:T(8,128)(2,1)S(1)} %get-tuple-element.53), channel_id=1, source_target_pairs={{0,14},{2,12},{4,10},{6,8},{8,6},{10,4},{12,2},{14,0},{1,15},{3,13... | collective-permute-start | bytes 786440 | tf_op jit(solution)/shard_map/ppermute | solution.py:888
  374.0 35.8 %collective-permute-start.5 = (bf16[2,512,128]{2,1,0:T(8,128)(2,1)}, bf16[2,512,128]{2,1,0:T(8,128)(2,1)S(1)}, u32[]{:S(2)}, u32[]{:S(2)}) collective-permute-start(bf16[2,512,128]{2,1,0:T(8,128)(2,1)} %get-tuple-element.56), channel_id=1, source_target_pairs={{0,8},{2,10},{4,12},{6,14},{8,0},{10,2},{12,4},{14,6},{1,9},{3,11}... | collective-permute-start | bytes 786440 | tf_op jit(solution)/shard_map/ppermute | solution.py:888
  377.4 32.4 %collective-permute-start.6 = (bf16[2,512,128]{2,1,0:T(8,128)(2,1)}, bf16[2,512,128]{2,1,0:T(8,128)(2,1)S(1)}, u32[]{:S(2)}, u32[]{:S(2)}) collective-permute-start(bf16[2,512,128]{2,1,0:T(8,128)(2,1)} %get-tuple-element.55), channel_id=1, source_target_pairs={{0,10},{2,8},{4,14},{6,12},{8,2},{10,0},{12,6},{14,4},{1,11},{3,9}... | collective-permute-start | bytes 786440 | tf_op jit(solution)/shard_map/ppermute | solution.py:888
  380.6 6.9 %copy-start.4 = (bf16[4,8,4096]{2,1,0:T(8,128)(2,1)}, bf16[4,8,4096]{2,1,0:T(8,128)(2,1)S(1)}, u32[]{:S(2)}) copy-start(bf16[4,8,4096]{2,1,0:T(8,128)(2,1)S(1)} %collective-permute-done.1.n_ref) | copy-start | bytes 786436
  380.6 29.1 %collective-permute-start.2 = (bf16[2,512,128]{2,1,0:T(8,128)(2,1)}, bf16[2,512,128]{2,1,0:T(8,128)(2,1)}, u32[]{:S(2)}, u32[]{:S(2)}) collective-permute-start(bf16[2,512,128]{2,1,0:T(8,128)(2,1)} %get-tuple-element.59), channel_id=1, source_target_pairs={{0,2},{2,0},{4,6},{6,4},{8,10},{10,8},{12,14},{14,12},{1,3},{3,1},... | collective-permute-start | bytes 786440 | tf_op jit(solution)/shard_map/ppermute | solution.py:888
  384.1 25.7 %collective-permute-start.3 = (bf16[2,512,128]{2,1,0:T(8,128)(2,1)}, bf16[2,512,128]{2,1,0:T(8,128)(2,1)}, u32[]{:S(2)}, u32[]{:S(2)}) collective-permute-start(bf16[2,512,128]{2,1,0:T(8,128)(2,1)} %get-tuple-element.58), channel_id=1, source_target_pairs={{0,4},{2,6},{4,0},{6,2},{8,12},{10,14},{12,8},{14,10},{1,5},{3,7},... | collective-permute-start | bytes 786440 | tf_op jit(solution)/shard_map/ppermute | solution.py:888
  387.6 22.2 %collective-permute-start.4 = (bf16[2,512,128]{2,1,0:T(8,128)(2,1)}, bf16[2,512,128]{2,1,0:T(8,128)(2,1)}, u32[]{:S(2)}, u32[]{:S(2)}) collective-permute-start(bf16[2,512,128]{2,1,0:T(8,128)(2,1)} %get-tuple-element.57), channel_id=1, source_target_pairs={{0,6},{2,4},{4,2},{6,0},{8,14},{10,12},{12,10},{14,8},{1,7},{3,5},... | collective-permute-start | bytes 786440 | tf_op jit(solution)/shard_map/ppermute | solution.py:888

commit v8 on v7

--- a/solution.py
+++ b/solution.py
@@ -890,13 +890,12 @@
     if fold:
         half = live // 2
         lows = [low[0]] + [None] * (live - 1)
-        send_low(range(half, half + half // 2), sent_all[0])
-        send_low(range(half + half // 2, live), sent_all[-1])
+        send_low(range(1, half), sent_all[-1])
     for p in range(parts):
         terms = (back[p], bias[p], filtered[p], sums)
         sums = [short_sums(streams, before, grad_out, short_filter, *terms, shards, p, parts)]
         if p == 0 and fold:
-            send_low(range(1, half), back[0])
+            send_low(range(half, live), back[0])
         done = finish(streams, before, after, grad_out, short_filter, back[p], done, shards, p, parts)
     output, grad_streams = done
     sums = sums[0]

time: 419 us -> 419 us (level)
  no operation moved by 1% of the time
where the time goes in v8:
time: 419 us; the launch traced here: 416 us
  Pallas kernels  159 us (38%)
  waiting for transfers between devices  132 us (32%)
  starting transfers between devices  99.2 us (24%)
  other arithmetic  16 us (4%)
  local copies, waits for them, and re-layouts  9.06 us (2%)
    all_to_all x7, waiting for transfers between devices, exchange(): lax.all_to_all(blocks, 'seq', split_axis=0, concat_axis=0, axis_index_gro...  128 us
    all_to_all x7, starting transfers between devices, exchange(): lax.all_to_all(blocks, 'seq', split_axis=0, concat_axis=0, axis_index_gro...  67 us
    pallas_call x2, Pallas kernels, raw_path(): pl.pallas_call(kernel, grid=(steps,), in_specs=in_specs, out_specs=out_sp...  47.2 us
    pallas_call x2, Pallas kernels, conv_path(): pl.pallas_call(kernel, grid=(steps,), in_specs=[resident(), resident(), p...  44.6 us
    ppermute x7, starting transfers between devices, send_low(): lows[d] = lax.ppermute(ready[d], 'seq', [(i, i ^ d) for i in range(live)])  22.8 us
    pallas_call x2, Pallas kernels, finish(): pl.pallas_call(kernel, grid=(count,), in_specs=[pl.BlockSpec((3, rows, bl...  19.8 us
    pallas_call x2, Pallas kernels, short_sums(): pl.pallas_call(kernel, grid=(count,), in_specs=in_specs + [untouched() fo...  16.5 us
    pallas_call x2, Pallas kernels, gates(): pl.pallas_call(kernel, grid=(count,), in_specs=[pl.BlockSpec((3, rows, bl...  13.7 us
  transfers between devices with their start and end apart: 17, of which 8 were waited for; matrix products, arithmetic and copies ran while one was open for 5% of the time, Pallas kernels for 33%

profile of v8, /device:TPU:0, one launch (start us, length us, event | category | flops | bytes accessed | tf_op | source)
XLA Modules:
  0.0 416.4 jit_solution(11625840376022376563)
XLA Ops:
  2.4 4.9 %collective-permute-start = (bf16[3,8,4096]{2,1,0:T(8,128)(2,1)S(1)}, bf16[3,8,4096]{2,1,0:T(8,128)(2,1)S(1)}, u32[]{:S(2)}, u32[]{:S(2)}) collective-permute-start(bf16[3,8,4096]{2,1,0:T(8,128)(2,1)S(1)} %get-tuple-element.50), channel_id=1, source_target_pairs={{0,2},{2,4},{4,6},{6,8},{8,10},{10,12},{12,14},{14,16},{16,18},{18... | collective-permute-start | bytes 589832 | tf_op jit(solution)/shard_map/ppermute | solution.py:816
  7.2 4.1 collective-permute-done.b_ref
  12.0 6.2 %gates.3 = (bf16[16,2,256,128]{3,2,1,0:T(8,128)(2,1)}, f32[1,2048]{1,0:T(1,128)}) custom-call(bf16[3,256,4096]{2,1,0:T(8,128)(2,1)} %x_ref.15, bf16[3,8,4096]{2,1,0:T(8,128)(2,1)} %copy-done.2, bf16[256,4096]{1,0:T(8,128)(2,1)} %go_ref.11, f32[3,7,4096]{2,1,0:T(8,128)} %w_ref.11), custom_call_target="tpu_custom_call" | custom-call | flops 60000000 | bytes 7000000 | tf_op jit(solution)/shard_map/gates/pallas_call | solution.py:652
  18.3 7.9 %all-to-all-start.1 = ((bf16[16,2,256,128]{3,2,1,0:T(8,128)(2,1)}), bf16[16,2,256,128]{3,2,1,0:T(8,128)(2,1)S(1)}, u32[]{:S(2)}, u32[]{:S(2)}) async-start(bf16[16,2,256,128]{3,2,1,0:T(8,128)(2,1)} %get-tuple-element.28), calls=%async_computation.1 | async-start | bytes 4194304 | tf_op jit(solution)/shard_map/all_to_all | solution.py:820
  26.1 7.5 %gates.2 = (bf16[16,2,256,128]{3,2,1,0:T(8,128)(2,1)}, f32[1,2048]{1,0:T(1,128)}, f32[2,256,2048]{2,1,0:T(8,128)}) custom-call(bf16[3,256,4096]{2,1,0:T(8,128)(2,1)} %x_ref.15, bf16[3,8,4096]{2,1,0:T(8,128)(2,1)} %copy-done.2, bf16[256,4096]{1,0:T(8,128)(2,1)} %go_ref.11, f32[3,7,4096]{2,1,0:T(8,128)} %w_ref.11), custom_call_target="tpu_custom_call" | custom-call | flops 60000000 | bytes 7000000 | tf_op jit(solution)/shard_map/gates/pallas_call | solution.py:652
  33.6 35.0 %all-to-all-done.1.refs_0_.x_ref = bf16[16,2,256,128]{3,2,1,0:T(8,128)(2,1)S(1)} async-done(((bf16[16,2,256,128]{3,2,1,0:T(8,128)(2,1)}), bf16[16,2,256,128]{3,2,1,0:T(8,128)(2,1)S(1)}, u32[]{:S(2)}, u32[]{:S(2)}) %all-to-all-start.1) | async-done | bytes 2097184 | tf_op jit(solution)/shard_map/all_to_all | solution.py:820
  68.6 9.9 %all-to-all-start = ((bf16[16,2,256,128]{3,2,1,0:T(8,128)(2,1)}), bf16[16,2,256,128]{3,2,1,0:T(8,128)(2,1)}, u32[]{:S(2)}, u32[]{:S(2)}) async-start(bf16[16,2,256,128]{3,2,1,0:T(8,128)(2,1)} %get-tuple-element.27), calls=%async_computation | async-start | bytes 4194304 | tf_op jit(solution)/shard_map/all_to_all | solution.py:820
  78.5 4.3 %pack_taps.3.refs_4_ = bf16[16,512,128]{2,1,0:T(8,128)(2,1)} custom-call(f32[512,4096]{1,0:T(8,128)} %x_ref.11), custom_call_target="tpu_custom_call" | custom-call | flops 1000000 | bytes 6000000 | tf_op jit(solution)/shard_map/pack_taps/pallas_call | solution.py:473
  84.6 4.1 multiply_subtract_fusion
  91.1 5.5 %fusion.refs_2_.inv_ref = bf16[17,512,256]{2,1,0:T(8,128)(2,1)} fusion(f32[17,256,256]{2,1,0:T(8,128)} %get-tuple-element.60, f32[17,256,256]{2,1,0:T(8,128)S(1)} %get-tuple-element.58), kind=kLoop, calls=%fused_computation.1 | loop fusion | flops 6684672 | bytes 13369344 | tf_op jit(solution)/shard_map/convert_element_type | solution.py:164
  96.6 23.3 %raw_path.2 = (f32[17,2,256,256]{3,2,1,0:T(8,128)}, bf16[8,2,512,128]{3,2,1,0:T(8,128)(2,1)}, f32[8,128]{1,0:T(8,128)}, bf16[16,512,128]{2,1,0:T(8,128)(2,1)}) custom-call(bf16[16,2,256,128]{3,2,1,0:T(8,128)(2,1)S(1)} %all-to-all-done.1.refs_0_.x_ref, bf16[17,512,256]{2,1,0:T(8,128)(2,1)} %pad_maximum_fusion.refs_1_.fwd_ref, ...), custom_call_target="tpu_custom_call" | custom-call | flops 20000000000 | bytes 25000000 | tf_op jit(solution)/shard_map/raw_path/pallas_call | solution.py:343
  121.1 9.9 %all-to-all-start.4 = ((bf16[16,512,128]{2,1,0:T(8,128)(2,1)}), bf16[16,512,128]{2,1,0:T(8,128)(2,1)}, u32[]{:S(2)}, u32[]{:S(2)}) async-start(bf16[16,512,128]{2,1,0:T(8,128)(2,1)} %get-tuple-element.32), calls=%async_computation.4 | async-start | bytes 4194304 | tf_op jit(solution)/shard_map/all_to_all | solution.py:820
  130.9 4.3 %pack_taps.2.refs_4_ = bf16[16,512,128]{2,1,0:T(8,128)(2,1)} custom-call(f32[512,4096]{1,0:T(8,128)} %x_ref.11), custom_call_target="tpu_custom_call" | custom-call | flops 1000000 | bytes 6000000 | tf_op jit(solution)/shard_map/pack_taps/pallas_call | solution.py:473
  135.2 23.9 %raw_path.3 = (f32[17,2,256,256]{3,2,1,0:T(8,128)}, bf16[8,2,512,128]{3,2,1,0:T(8,128)(2,1)}, f32[8,128]{1,0:T(8,128)}, bf16[16,512,128]{2,1,0:T(8,128)(2,1)}) custom-call(bf16[16,2,256,128]{3,2,1,0:T(8,128)(2,1)} %all-to-all-done.refs_0_.x_ref, bf16[17,512,256]{2,1,0:T(8,128)(2,1)} %pad_maximum_fusion.refs_1_.fwd_ref, ...), custom_call_target="tpu_custom_call", output_to_operand_aliasing={{1}: (5, {})} | custom-call | flops 20000000000 | bytes 25000000 | tf_op jit(solution)/shard_map/raw_path/pallas_call | solution.py:343
  159.1 14.4 %all-to-all-done.4.refs_10_ = bf16[16,512,128]{2,1,0:T(8,128)(2,1)} async-done(((bf16[16,512,128]{2,1,0:T(8,128)(2,1)}), bf16[16,512,128]{2,1,0:T(8,128)(2,1)}, u32[]{:S(2)}, u32[]{:S(2)}) %all-to-all-start.4) | async-done | bytes 2097184 | tf_op jit(solution)/shard_map/all_to_all | solution.py:820
  173.6 9.8 %all-to-all-start.2 = ((bf16[16,512,128]{2,1,0:T(8,128)(2,1)}), bf16[16,512,128]{2,1,0:T(8,128)(2,1)}, u32[]{:S(2)}, u32[]{:S(2)}) async-start(bf16[16,512,128]{2,1,0:T(8,128)(2,1)} %get-tuple-element.30), calls=%async_computation.2 | async-start | bytes 4194304 | tf_op jit(solution)/shard_map/all_to_all | solution.py:820
  186.3 21.9 %conv_path.3 = bf16[16,2,264,128]{3,2,1,0:T(8,128)(2,1)} custom-call(bf16[16,2,256,128]{3,2,1,0:T(8,128)(2,1)S(1)} %copy-done.1, bf16[32,256,128]{2,1,0:T(8,128)(2,1)} %bitcast.7.h_ref, f32[17,2,256,256]{3,2,1,0:T(8,128)} %get-tuple-element.33.spec_ref, f32[1,128]{1,0:T(1,128)} %get-tuple-element.62.skip_ref, ...), custom_call_target="tpu_custom_call" | custom-call | flops 20000000000 | bytes 25000000 | tf_op jit(solution)/shard_map/conv_path/pallas_call | solution.py:412
  208.2 17.8 %all-to-all-done.2.refs_11_ = bf16[16,512,128]{2,1,0:T(8,128)(2,1)} async-done(((bf16[16,512,128]{2,1,0:T(8,128)(2,1)}), bf16[16,512,128]{2,1,0:T(8,128)(2,1)}, u32[]{:S(2)}, u32[]{:S(2)}) %all-to-all-start.2) | async-done | bytes 2097184 | tf_op jit(solution)/shard_map/all_to_all | solution.py:820
  226.1 9.7 %all-to-all-start.5 = ((bf16[16,2,264,128]{3,2,1,0:T(8,128)(2,1)}), bf16[16,2,264,128]{3,2,1,0:T(8,128)(2,1)}, u32[]{:S(2)}, u32[]{:S(2)}) async-start(bf16[16,2,264,128]{3,2,1,0:T(8,128)(2,1)} %conv_path.3), calls=%async_computation.5 | async-start | bytes 4325376 | tf_op jit(solution)/shard_map/all_to_all | solution.py:820
  235.8 22.7 %conv_path.2 = bf16[16,2,264,128]{3,2,1,0:T(8,128)(2,1)} custom-call(bf16[16,2,256,128]{3,2,1,0:T(8,128)(2,1)} %all-to-all-done.refs_0_.x_ref, bf16[32,256,128]{2,1,0:T(8,128)(2,1)} %bitcast.5.h_ref, f32[17,2,256,256]{3,2,1,0:T(8,128)} %get-tuple-element.31.spec_ref, f32[1,128]{1,0:T(1,128)} %get-tuple-element.63.skip_ref, ...), custom_call_target="tpu_custom_call" | custom-call | flops 20000000000 | bytes 25000000 | tf_op jit(solution)/shard_map/conv_path/pallas_call | solution.py:412
  258.4 21.1 %all-to-all-done.5.y_ref = bf16[16,2,264,128]{3,2,1,0:T(8,128)(2,1)} async-done(((bf16[16,2,264,128]{3,2,1,0:T(8,128)(2,1)}), bf16[16,2,264,128]{3,2,1,0:T(8,128)(2,1)}, u32[]{:S(2)}, u32[]{:S(2)}) %all-to-all-start.5) | async-done | bytes 2162720 | tf_op jit(solution)/shard_map/all_to_all | solution.py:820
  279.6 9.8 %all-to-all-start.3 = ((bf16[16,2,264,128]{3,2,1,0:T(8,128)(2,1)}), bf16[16,2,264,128]{3,2,1,0:T(8,128)(2,1)}, u32[]{:S(2)}, u32[]{:S(2)}) async-start(bf16[16,2,264,128]{3,2,1,0:T(8,128)(2,1)} %conv_path.2), calls=%async_computation.3 | async-start | bytes 4325376 | tf_op jit(solution)/shard_map/all_to_all | solution.py:820
  290.3 8.6 %short_sums.2.refs_1_ = bf16[16,2,24,128]{3,2,1,0:T(8,128)(2,1)} custom-call(bf16[3,256,4096]{2,1,0:T(8,128)(2,1)} %x_ref.15, bf16[3,8,4096]{2,1,0:T(8,128)(2,1)} %copy-done.2, bf16[256,4096]{1,0:T(8,128)(2,1)} %go_ref.11, f32[3,7,4096]{2,1,0:T(8,128)} %w_ref.11, bf16[16,2,264,128]{3,2,1,0:T(8,128)(2,1)} %all-to-all-done.5.y_ref, ...), custom_call_target="tpu_custom_call" | custom-call | flops 150000000 | bytes 8000000 | tf_op jit(solution)/shard_map/short_sums/pallas_call | solution.py:730
  298.8 34.1 %all-to-all-done.3.y_ref = bf16[16,2,264,128]{3,2,1,0:T(8,128)(2,1)} async-done(((bf16[16,2,264,128]{3,2,1,0:T(8,128)(2,1)}), bf16[16,2,264,128]{3,2,1,0:T(8,128)(2,1)}, u32[]{:S(2)}, u32[]{:S(2)}) %all-to-all-start.3) | async-done | bytes 2162720 | tf_op jit(solution)/shard_map/all_to_all | solution.py:820
  333.0 7.9 %short_sums.3 = bf16[16,2,24,128]{3,2,1,0:T(8,128)(2,1)} custom-call(bf16[3,256,4096]{2,1,0:T(8,128)(2,1)} %x_ref.15, bf16[3,8,4096]{2,1,0:T(8,128)(2,1)} %copy-done.2, bf16[256,4096]{1,0:T(8,128)(2,1)} %go_ref.11, f32[3,7,4096]{2,1,0:T(8,128)} %w_ref.11, bf16[16,2,264,128]{3,2,1,0:T(8,128)(2,1)} %all-to-all-done.3.y_ref, ...), custom_call_target="tpu_custom_call", output_to_operand_aliasing={{}: (7, {})} | custom-call | flops 150000000 | bytes 8000000 | tf_op jit(solution)/shard_map/short_sums/pallas_call | solution.py:730
  340.9 10.1 %all-to-all-start.6 = ((bf16[16,2,24,128]{3,2,1,0:T(8,128)(2,1)}), bf16[16,2,24,128]{3,2,1,0:T(8,128)(2,1)S(1)}, u32[]{:S(2)}, u32[]{:S(2)}) async-start(bf16[16,2,24,128]{3,2,1,0:T(8,128)(2,1)} %short_sums.3), calls=%async_computation.6 | async-start | bytes 393216 | tf_op jit(solution)/shard_map/all_to_all | solution.py:820
  354.5 4.6 %all-to-all-done.6.x_ref = bf16[16,2,24,128]{3,2,1,0:T(8,128)(2,1)S(1)} async-done(((bf16[16,2,24,128]{3,2,1,0:T(8,128)(2,1)}), bf16[16,2,24,128]{3,2,1,0:T(8,128)(2,1)S(1)}, u32[]{:S(2)}, u32[]{:S(2)}) %all-to-all-start.6) | async-done | bytes 196640 | tf_op jit(solution)/shard_map/all_to_all | solution.py:820
  376.1 3.5 collective-permute-start.5
  383.0 4.4 %collective-permute-start.7 = (bf16[2,512,128]{2,1,0:T(8,128)(2,1)}, bf16[2,512,128]{2,1,0:T(8,128)(2,1)}, u32[]{:S(2)}, u32[]{:S(2)}) collective-permute-start(bf16[2,512,128]{2,1,0:T(8,128)(2,1)} %get-tuple-element.52), channel_id=1, source_target_pairs={{0,12},{2,14},{4,8},{6,10},{8,4},{10,6},{12,0},{14,2},{1,13},{3,15... | collective-permute-start | bytes 786440 | tf_op jit(solution)/shard_map/ppermute | solution.py:888
  389.8 9.9 %finish.2 = (bf16[256,4096]{1,0:T(8,128)(2,1)}, bf16[3,256,4096]{2,1,0:T(8,128)(2,1)}) custom-call(bf16[3,256,4096]{2,1,0:T(8,128)(2,1)} %x_ref.15, bf16[3,8,4096]{2,1,0:T(8,128)(2,1)} %copy-done.2, bf16[4,8,4096]{2,1,0:T(8,128)(2,1)} %copy-done.4, bf16[256,4096]{1,0:T(8,128)(2,1)} %go_ref.11, f32[3,7,4096]{2,1,0:T(8,128)} %w_ref.11, ...), custom_call_target="tpu_custom_call" | custom-call | flops 150000000 | bytes 12000000 | tf_op jit(solution)/shard_map/finish/pallas_call | solution.py:783
  399.7 9.9 %finish.3 = (bf16[256,4096]{1,0:T(8,128)(2,1)}, bf16[3,256,4096]{2,1,0:T(8,128)(2,1)}) custom-call(bf16[3,256,4096]{2,1,0:T(8,128)(2,1)} %x_ref.15, bf16[3,8,4096]{2,1,0:T(8,128)(2,1)} %copy-done.2, bf16[4,8,4096]{2,1,0:T(8,128)(2,1)} %copy-done.4, bf16[256,4096]{1,0:T(8,128)(2,1)} %go_ref.11, ...), custom_call_target="tpu_custom_call", output_to_operand_aliasing={{0}: (6, {}), {1}: (7, {})} | custom-call | flops 150000000 | bytes 12000000 | tf_op jit(solution)/shard_map/finish/pallas_call | solution.py:783
  409.7 6.7 %scale_taps.1 = (f32[512,4096]{1,0:T(8,128)}, f32[3,7,4096]{2,1,0:T(8,128)}, f32[1,4096]{1,0:T(1,128)}) custom-call(bf16[32,2,24,128]{3,2,1,0:T(8,128)(2,1)} %all-to-all-done.7.refs_0_, s32[1,3]{1,0:T(1,128)} %add_bitcast_fusion.refs_3_.refs_1_, bf16[2,512,128]{2,1,0:T(8,128)(2,1)S(1)} %slice_bitcast_fusion.7.refs_2_, ...), custom_call_target="tpu_custom_call" | custom-call | tf_op jit(solution)/shard_map/scale_taps/pallas_call | solution.py:551
  (44 shorter events, 37.8 us)
Async XLA Ops:
  2.4 9.0 %collective-permute-start = (bf16[3,8,4096]{2,1,0:T(8,128)(2,1)S(1)}, bf16[3,8,4096]{2,1,0:T(8,128)(2,1)S(1)}, u32[]{:S(2)}, u32[]{:S(2)}) collective-permute-start(bf16[3,8,4096]{2,1,0:T(8,128)(2,1)S(1)} %get-tuple-element.50), channel_id=1, source_target_pairs={{0,2},{2,4},{4,6},{6,8},{8,10},{10,12},{12,14},{14,16},{16,18},{18... | collective-permute-start | bytes 589832 | tf_op jit(solution)/shard_map/ppermute | solution.py:816
  11.4 0.7 copy-start.2
  18.3 50.3 %all-to-all-start.1 = ((bf16[16,2,256,128]{3,2,1,0:T(8,128)(2,1)}), bf16[16,2,256,128]{3,2,1,0:T(8,128)(2,1)S(1)}, u32[]{:S(2)}, u32[]{:S(2)}) async-start(bf16[16,2,256,128]{3,2,1,0:T(8,128)(2,1)} %get-tuple-element.28), calls=%async_computation.1 | async-start | bytes 4194304 | tf_op jit(solution)/shard_map/all_to_all | solution.py:820
  68.6 28.0 %copy-start = (bf16[16,2,256,128]{3,2,1,0:T(8,128)(2,1)}, bf16[16,2,256,128]{3,2,1,0:T(8,128)(2,1)S(1)}, u32[]{:S(2)}) copy-start(bf16[16,2,256,128]{3,2,1,0:T(8,128)(2,1)S(1)} %all-to-all-done.1.refs_0_.x_ref) | copy-start | bytes 6291460
  68.6 52.5 %all-to-all-start = ((bf16[16,2,256,128]{3,2,1,0:T(8,128)(2,1)}), bf16[16,2,256,128]{3,2,1,0:T(8,128)(2,1)}, u32[]{:S(2)}, u32[]{:S(2)}) async-start(bf16[16,2,256,128]{3,2,1,0:T(8,128)(2,1)} %get-tuple-element.27), calls=%async_computation | async-start | bytes 4194304 | tf_op jit(solution)/shard_map/all_to_all | solution.py:820
  121.1 52.5 %all-to-all-start.4 = ((bf16[16,512,128]{2,1,0:T(8,128)(2,1)}), bf16[16,512,128]{2,1,0:T(8,128)(2,1)}, u32[]{:S(2)}, u32[]{:S(2)}) async-start(bf16[16,512,128]{2,1,0:T(8,128)(2,1)} %get-tuple-element.32), calls=%async_computation.4 | async-start | bytes 4194304 | tf_op jit(solution)/shard_map/all_to_all | solution.py:820
  173.6 52.5 %all-to-all-start.2 = ((bf16[16,512,128]{2,1,0:T(8,128)(2,1)}), bf16[16,512,128]{2,1,0:T(8,128)(2,1)}, u32[]{:S(2)}, u32[]{:S(2)}) async-start(bf16[16,512,128]{2,1,0:T(8,128)(2,1)} %get-tuple-element.30), calls=%async_computation.2 | async-start | bytes 4194304 | tf_op jit(solution)/shard_map/all_to_all | solution.py:820
  184.7 1.6 copy-start.1
  226.1 53.5 %all-to-all-start.5 = ((bf16[16,2,264,128]{3,2,1,0:T(8,128)(2,1)}), bf16[16,2,264,128]{3,2,1,0:T(8,128)(2,1)}, u32[]{:S(2)}, u32[]{:S(2)}) async-start(bf16[16,2,264,128]{3,2,1,0:T(8,128)(2,1)} %conv_path.3), calls=%async_computation.5 | async-start | bytes 4325376 | tf_op jit(solution)/shard_map/all_to_all | solution.py:820
  279.6 53.4 %all-to-all-start.3 = ((bf16[16,2,264,128]{3,2,1,0:T(8,128)(2,1)}), bf16[16,2,264,128]{3,2,1,0:T(8,128)(2,1)}, u32[]{:S(2)}, u32[]{:S(2)}) async-start(bf16[16,2,264,128]{3,2,1,0:T(8,128)(2,1)} %conv_path.2), calls=%async_computation.3 | async-start | bytes 4325376 | tf_op jit(solution)/shard_map/all_to_all | solution.py:820
  333.0 20.9 %copy-start.5 = (f32[8,128]{1,0:T(8,128)S(1)}, f32[8,128]{1,0:T(8,128)}, u32[]{:S(2)}) copy-start(f32[8,128]{1,0:T(8,128)} %get-tuple-element.41) | copy-start | bytes 12292
  333.0 20.9 %copy-start.6 = (f32[8,128]{1,0:T(8,128)S(1)}, f32[8,128]{1,0:T(8,128)}, u32[]{:S(2)}) copy-start(f32[8,128]{1,0:T(8,128)} %get-tuple-element.42) | copy-start | bytes 12292
  340.9 34.2 %copy-start.3 = (bf16[8,2,512,128]{3,2,1,0:T(8,128)(2,1)S(1)}, bf16[8,2,512,128]{3,2,1,0:T(8,128)(2,1)}, u32[]{:S(2)}) copy-start(bf16[8,2,512,128]{3,2,1,0:T(8,128)(2,1)} %get-tuple-element.45) | copy-start | bytes 6291460
  340.9 18.2 %all-to-all-start.6 = ((bf16[16,2,24,128]{3,2,1,0:T(8,128)(2,1)}), bf16[16,2,24,128]{3,2,1,0:T(8,128)(2,1)S(1)}, u32[]{:S(2)}, u32[]{:S(2)}) async-start(bf16[16,2,24,128]{3,2,1,0:T(8,128)(2,1)} %short_sums.3), calls=%async_computation.6 | async-start | bytes 393216 | tf_op jit(solution)/shard_map/all_to_all | solution.py:820
  352.6 27.0 %collective-permute-start.1 = (bf16[4,8,4096]{2,1,0:T(8,128)(2,1)}, bf16[4,8,4096]{2,1,0:T(8,128)(2,1)S(1)}, u32[]{:S(2)}, u32[]{:S(2)}) collective-permute-start(bf16[4,8,4096]{2,1,0:T(8,128)(2,1)} %pad_maximum_fusion.1), channel_id=1, source_target_pairs={{2,0},{4,2},{6,4},{8,6},{10,8},{12,10},{14,12},{16,14},{18,16},{20... | collective-permute-start | bytes 786440 | tf_op jit(solution)/shard_map/ppermute | solution.py:816
  360.7 49.0 %all-to-all-start.7 = ((bf16[32,2,24,128]{3,2,1,0:T(8,128)(2,1)}), bf16[32,2,24,128]{3,2,1,0:T(8,128)(2,1)}, u32[]{:S(2)}, u32[]{:S(2)}) async-start(bf16[32,2,24,128]{3,2,1,0:T(8,128)(2,1)} %add_sums.1), calls=%async_computation.7 | async-start | bytes 786432 | tf_op jit(solution)/shard_map/all_to_all | solution.py:907
  365.9 17.1 %collective-permute-start.2 = (bf16[2,512,128]{2,1,0:T(8,128)(2,1)S(1)}, bf16[2,512,128]{2,1,0:T(8,128)(2,1)S(1)}, u32[]{:S(2)}, u32[]{:S(2)}) collective-permute-start(bf16[2,512,128]{2,1,0:T(8,128)(2,1)S(1)} %get-tuple-element.57), channel_id=1, source_target_pairs={{0,2},{2,0},{4,6},{6,4},{8,10},{10,8},{12,14},{14,12},{1,3},{3,1},... | collective-permute-start | bytes 786440 | tf_op jit(solution)/shard_map/ppermute | solution.py:888
  369.3 18.0 %collective-permute-start.3 = (bf16[2,512,128]{2,1,0:T(8,128)(2,1)S(1)}, bf16[2,512,128]{2,1,0:T(8,128)(2,1)S(1)}, u32[]{:S(2)}, u32[]{:S(2)}) collective-permute-start(bf16[2,512,128]{2,1,0:T(8,128)(2,1)S(1)} %get-tuple-element.56), channel_id=1, source_target_pairs={{0,4},{2,6},{4,0},{6,2},{8,12},{10,14},{12,8},{14,10},{1,5},{3,7},... | collective-permute-start | bytes 786440 | tf_op jit(solution)/shard_map/ppermute | solution.py:888
  372.8 36.9 %collective-permute-start.4 = (bf16[2,512,128]{2,1,0:T(8,128)(2,1)}, bf16[2,512,128]{2,1,0:T(8,128)(2,1)S(1)}, u32[]{:S(2)}, u32[]{:S(2)}) collective-permute-start(bf16[2,512,128]{2,1,0:T(8,128)(2,1)} %get-tuple-element.55), channel_id=1, source_target_pairs={{0,6},{2,4},{4,2},{6,0},{8,14},{10,12},{12,10},{14,8},{1,7},{3,5},... | collective-permute-start | bytes 786440 | tf_op jit(solution)/shard_map/ppermute | solution.py:888
  376.1 33.5 %collective-permute-start.5 = (bf16[2,512,128]{2,1,0:T(8,128)(2,1)}, bf16[2,512,128]{2,1,0:T(8,128)(2,1)S(1)}, u32[]{:S(2)}, u32[]{:S(2)}) collective-permute-start(bf16[2,512,128]{2,1,0:T(8,128)(2,1)} %get-tuple-element.54), channel_id=1, source_target_pairs={{0,8},{2,10},{4,12},{6,14},{8,0},{10,2},{12,4},{14,6},{1,9},{3,11}... | collective-permute-start | bytes 786440 | tf_op jit(solution)/shard_map/ppermute | solution.py:888
  379.7 7.7 %copy-start.4 = (bf16[4,8,4096]{2,1,0:T(8,128)(2,1)}, bf16[4,8,4096]{2,1,0:T(8,128)(2,1)S(1)}, u32[]{:S(2)}) copy-start(bf16[4,8,4096]{2,1,0:T(8,128)(2,1)S(1)} %collective-permute-done.1.n_ref) | copy-start | bytes 786436
  379.7 30.0 %collective-permute-start.6 = (bf16[2,512,128]{2,1,0:T(8,128)(2,1)}, bf16[2,512,128]{2,1,0:T(8,128)(2,1)}, u32[]{:S(2)}, u32[]{:S(2)}) collective-permute-start(bf16[2,512,128]{2,1,0:T(8,128)(2,1)} %get-tuple-element.53), channel_id=1, source_target_pairs={{0,10},{2,8},{4,14},{6,12},{8,2},{10,0},{12,6},{14,4},{1,11},{3,9}... | collective-permute-start | bytes 786440 | tf_op jit(solution)/shard_map/ppermute | solution.py:888
  383.0 26.7 %collective-permute-start.7 = (bf16[2,512,128]{2,1,0:T(8,128)(2,1)}, bf16[2,512,128]{2,1,0:T(8,128)(2,1)}, u32[]{:S(2)}, u32[]{:S(2)}) collective-permute-start(bf16[2,512,128]{2,1,0:T(8,128)(2,1)} %get-tuple-element.52), channel_id=1, source_target_pairs={{0,12},{2,14},{4,8},{6,10},{8,4},{10,6},{12,0},{14,2},{1,13},{3,15... | collective-permute-start | bytes 786440 | tf_op jit(solution)/shard_map/ppermute | solution.py:888
  387.4 22.3 %collective-permute-start.8 = (bf16[2,512,128]{2,1,0:T(8,128)(2,1)}, bf16[2,512,128]{2,1,0:T(8,128)(2,1)}, u32[]{:S(2)}, u32[]{:S(2)}) collective-permute-start(bf16[2,512,128]{2,1,0:T(8,128)(2,1)} %get-tuple-element.51), channel_id=1, source_target_pairs={{0,14},{2,12},{4,10},{6,8},{8,6},{10,4},{12,2},{14,0},{1,15},{3,13... | collective-permute-start | bytes 786440 | tf_op jit(solution)/shard_map/ppermute | solution.py:888
